TPU v7x, 256 devices: a whole 4x4x8 slice. The times are simulated.
256 devices in a mesh: seq: 32 (over z, y), head: 8 (over x, core).
Axes of the slice: x: 4, y: 4, z: 8, core: 2. Of those that a mesh axis runs over, the one named last changes fastest.
Arguments:
- queries: bfloat16 [16384, 4096], P('seq', 'head'), may hold values from -16 to 16
- latents: bfloat16 [384, 64, 1280], P('seq'), may hold values from -6 to 6
- key_weight: bfloat16 [1280, 4096], P(None, 'head'), may hold values from -0.15625 to 0.15625
- value_weight: bfloat16 [1280, 4096], P(None, 'head'), may hold values from -0.15625 to 0.15625
- visible: int32 [32, 16], P('seq'), may hold values from -1 to 63, as said below
- outbound: int32 [32, 32, 2], P('seq'), may hold values from -1 to 11, as said below
- token_slot: int32 [16384], P('seq'), may hold values from -1 to 15, as said below
- grad_out: bfloat16 [16384, 4096], P('seq', 'head'), may hold values from -6 to 6
Outputs:
- attended: bfloat16 [16384, 4096], P('seq', 'head')
- grad_queries: bfloat16 [16384, 4096], P('seq', 'head')
- grad_latents: float32 [384, 64, 1280], P('seq', 'head')
- grad_key_weight: float32 [1280, 4096], P('seq', 'head')
- grad_value_weight: float32 [1280, 4096], P('seq', 'head')
Inputs may be any that keep to these rules, and one draw needn't show every extreme that they name: `visible`: row c lists each image that the tokens of text block c attend to once, in order of first appearance, then -1. An entry p names place p % 2 among the images that index p // 2 of seq holds and sends to block c. Some row lists 16 images. outbound[o, c, s] is the index, among the 12 images held by index o of seq (image o * 12 + index), of the image at place s of its sends to text block c, and -1 exactly where no entry of row c of visible names that place. No block attends to more than 2 images of one holder, and some block attends to exactly 2 images of one holder. `token_slot`: documents are 8192 tokens long and start at multiples of 8192; the first 32 tokens of every document, and any others before its first image, have -1. Within a text block the slot never falls and changes only at positions that are multiples of 32, by one at a time.
All inputs are finite; a program needn't handle non-finite values.
Results may differ from a plain program's by a relative error of at most 0.012.
Values may be sent and summed in bfloat16 or wider, within the bound.
No kernel may reach another device: no remote copies, remote signals or barrier semaphores. Data moves between devices by JAX's collectives and lax.ppermute only.
A program may use at most 128 MiB of HBM per device.

v0:
```python
import jax
import jax.numpy as jnp
from jax import lax
from jax.sharding import PartitionSpec as P

DH = 128
GAP = 32


NEG_FILL = -1e30


def local(queries, latents, key_weight, value_weight, visible, outbound, token_slot, grad_out):
    tokens_here = queries.shape[0]
    head_cols = queries.shape[1]
    heads_here = head_cols // DH
    seq_count = lax.axis_size("seq")
    slots_each = outbound.shape[2]
    images_each = latents.shape[0]
    latent_rows = latents.shape[1]
    latent_width = latents.shape[2]
    vis_count = visible.shape[1]
    score_scale = DH ** (-0.5)
    both_weights = jnp.concatenate([key_weight, value_weight], axis=1)
    send_place = visible[0]
    place_filled = send_place >= 0
    sent_image = outbound[0]
    sent_filled = sent_image >= 0
    sent_local = jnp.where(sent_filled, sent_image, 0)
    pool_rows = jnp.where(place_filled, send_place, 0)
    projected = jnp.dot(
        latents.reshape(images_each * latent_rows, latent_width),
        both_weights,
        preferred_element_type=jnp.float32,
    )
    projected = projected.astype(jnp.bfloat16).reshape(images_each, latent_rows, 2 * head_cols)
    arriving = lax.all_to_all(projected[sent_local], "seq", split_axis=0, concat_axis=0, tiled=True)
    kv_visible = arriving.reshape(seq_count * slots_each, latent_rows, 2 * head_cols)[pool_rows]
    block_rows = min(tokens_here, 4 * GAP)
    window = block_rows // GAP
    blocks = tokens_here // block_rows
    slot_rows = token_slot.reshape(blocks, block_rows)
    has_image = slot_rows >= 0
    window_first = jnp.minimum(jnp.maximum(slot_rows[:, 0], 0), vis_count - window)
    window_slots = window_first[:, None] + jnp.arange(window, dtype=jnp.int32)[None, :]
    kv_window = kv_visible[window_slots]
    key_count = window * latent_rows
    keys_win = kv_window[..., :head_cols].reshape(blocks, key_count, heads_here, DH)
    values_win = kv_window[..., head_cols:].reshape(blocks, key_count, heads_here, DH)
    key_slot = jnp.repeat(window_slots, latent_rows, axis=1)
    matches = (slot_rows[:, :, None] == key_slot[:, None, :])[:, None]
    query_four = queries.reshape(blocks, block_rows, heads_here, DH)
    scores = (
        jnp.einsum("bqhd,bkhd->bhqk", query_four, keys_win, preferred_element_type=jnp.float32)
        * score_scale
    )
    scores = jnp.where(matches, scores, NEG_FILL)
    row_peak = jnp.max(scores, axis=-1, keepdims=True)
    exp_terms = jnp.exp(scores - row_peak)
    prob_full = exp_terms / jnp.sum(exp_terms, axis=-1, keepdims=True)
    prob_low = prob_full.astype(jnp.bfloat16)
    mixed_out = jnp.einsum(
        "bhqk,bkhd->bqhd", prob_low, values_win, preferred_element_type=jnp.float32
    )
    token_mask = has_image[:, :, None, None]
    attended = (
        jnp.where(token_mask, mixed_out, 0.0).astype(jnp.bfloat16).reshape(tokens_here, head_cols)
    )
    grad_four = jnp.where(
        token_mask,
        grad_out.reshape(blocks, block_rows, heads_here, DH),
        jnp.zeros((), jnp.bfloat16),
    )
    grad_prob = jnp.einsum(
        "bqhd,bkhd->bhqk", grad_four, values_win, preferred_element_type=jnp.float32
    )
    row_inner = jnp.sum(prob_full * grad_prob, axis=-1, keepdims=True)
    grad_score = (prob_full * (grad_prob - row_inner) * score_scale).astype(jnp.bfloat16)
    grad_queries = jnp.einsum(
        "bhqk,bkhd->bqhd", grad_score, keys_win, preferred_element_type=jnp.float32
    )
    grad_queries = grad_queries.astype(jnp.bfloat16).reshape(tokens_here, head_cols)
    key_term = jnp.einsum(
        "bhqk,bqhd->bkhd", grad_score, query_four, preferred_element_type=jnp.float32
    )
    value_term = jnp.einsum(
        "bhqk,bqhd->bkhd", prob_low, grad_four, preferred_element_type=jnp.float32
    )
    window_grad = jnp.concatenate(
        [
            key_term.reshape(blocks * window, latent_rows, head_cols),
            value_term.reshape(blocks * window, latent_rows, head_cols),
        ],
        axis=2,
    )
    slot_match = (
        jnp.arange(vis_count, dtype=jnp.int32)[:, None] == window_slots.reshape(-1)[None, :]
    ).astype(jnp.float32)
    block_grad = jnp.dot(
        slot_match,
        window_grad.reshape(blocks * window, -1),
        precision=lax.Precision.HIGHEST,
        preferred_element_type=jnp.float32,
    ).astype(jnp.bfloat16)
    send_rows = jnp.where(place_filled, send_place, seq_count * slots_each)
    outgoing = jnp.zeros((seq_count * slots_each, latent_rows * 2 * head_cols), jnp.bfloat16)
    outgoing = outgoing.at[send_rows].set(block_grad, mode="drop")
    returned = lax.all_to_all(
        outgoing.reshape(seq_count, slots_each, latent_rows * 2 * head_cols),
        "seq",
        split_axis=0,
        concat_axis=0,
        tiled=True,
    )
    image_pick = (
        (jnp.arange(images_each, dtype=jnp.int32)[:, None] == sent_local.reshape(-1)[None, :])
        & sent_filled.reshape(-1)[None, :]
    ).astype(jnp.bfloat16)
    kv_grad = jnp.dot(
        image_pick, returned.reshape(seq_count * slots_each, -1), preferred_element_type=jnp.float32
    ).astype(jnp.bfloat16)
    kv_flat = kv_grad.reshape(images_each * latent_rows, 2 * head_cols)
    latent_part = lax.dot_general(
        kv_flat, both_weights, (((1,), (1,)), ((), ())), preferred_element_type=jnp.float32
    )
    grad_latents = lax.psum_scatter(
        latent_part.reshape(images_each, latent_rows, latent_width),
        "head",
        scatter_dimension=1,
        tiled=True,
    )
    latent_flat = latents.reshape(images_each * latent_rows, latent_width)
    weight_rows = lax.psum_scatter(
        lax.dot_general(
            latent_flat, kv_flat, (((0,), (0,)), ((), ())), preferred_element_type=jnp.float32
        ),
        "seq",
        scatter_dimension=0,
        tiled=True,
    )
    return (
        attended,
        grad_queries,
        grad_latents,
        weight_rows[:, :head_cols],
        weight_rows[:, head_cols:],
    )


def solution(mesh):
    in_specs = (
        P("seq", "head"),
        P("seq", None, None),
        P(None, "head"),
        P(None, "head"),
        P("seq", None),
        P("seq", None, None),
        P("seq"),
        P("seq", "head"),
    )
    out_specs = (
        P("seq", "head"),
        P("seq", "head"),
        P("seq", "head", None),
        P("seq", "head"),
        P("seq", "head"),
    )
    return jax.shard_map(local, mesh=mesh, in_specs=in_specs, out_specs=out_specs, check_vma=False)
```

profile of v0, /device:TPU:8, one launch (start us, length us, event | category | flops | bytes accessed | tf_op | source)
XLA Modules:
  0.0 855.7 jit_solution(17672010450841875463)
XLA Ops:
  7.2 2.7 constant_dynamic-update-slice_fusion.1
  11.4 3.9 convolution_convert_fusion.2
  15.3 5.4 gather_fusion
  20.7 11.9 %all-to-all-start = ((bf16[32,2,64,1024]{3,2,1,0:T(8,128)(2,1)}), bf16[32,2,64,1024]{3,2,1,0:T(8,128)(2,1)}, u32[]{:S(2)}, u32[]{:S(2)}) async-start(bf16[32,2,64,1024]{3,2,1,0:T(8,128)(2,1)} %bitcast.73), calls=%async_computation | async-start | bytes 16777216 | tf_op jit(solution)/shard_map/all_to_all | solution.py:37
  38.3 184.6 %all-to-all-done = bf16[32,2,64,1024]{3,2,1,0:T(8,128)(2,1)} async-done(((bf16[32,2,64,1024]{3,2,1,0:T(8,128)(2,1)}), bf16[32,2,64,1024]{3,2,1,0:T(8,128)(2,1)}, u32[]{:S(2)}, u32[]{:S(2)}) %all-to-all-start) | async-done | bytes 8388640 | tf_op jit(solution)/shard_map/all_to_all | solution.py:37
  222.9 5.4 gather_fusion.1
  228.4 3.6 gather_fusion.2
  232.0 2.8 fusion.62
  238.6 4.3 fusion.64
  246.8 2.9 copy.91
  249.6 3.1 reshape.230
  252.8 5.7 fusion.14
  258.4 4.2 copy.89
  262.7 15.2 %reshape.229 = f32[16,64,512]{2,1,0:T(8,128)} reshape(f32[4,256,4,128]{3,2,1,0:T(4,128)} %copy.89) | data formatting | bytes 4194304 | tf_op jit(solution)/shard_map/reshape | solution.py:91
  277.9 2.7 pad_maximum_fusion
  283.0 3.5 convolution_convert_fusion.1
  286.6 3.8 broadcast_in_dim.67
  290.3 42.7 %scatter_fusion = bf16[64,65536]{1,0:T(8,128)(2,1)} fusion(bf16[64,65536]{1,0:T(8,128)(2,1)} %broadcast_in_dim.67, s32[16]{0:T(128)S(1)} %copy-done.11, bf16[16,65536]{1,0:T(8,128)(2,1)} %convolution_convert_fusion.1), kind=kCustom, calls=%fused_computation.3 | custom fusion | bytes 6291520 | tf_op jit(solution)/shard_map/scatter | solution.py:107
  333.1 10.5 %reshape.232 = bf16[32,2,65536]{2,1,0:T(2,128)(2,1)} reshape(bf16[64,65536]{1,0:T(8,128)(2,1)} %scatter_fusion) | data formatting | bytes 16777216 | tf_op jit(solution)/shard_map/reshape | solution.py:109
  343.6 12.9 %all-to-all-start.1 = ((bf16[32,2,65536]{2,1,0:T(2,128)(2,1)}), bf16[32,2,65536]{2,1,0:T(2,128)(2,1)}, u32[]{:S(2)}, u32[]{:S(2)}) async-start(bf16[32,2,65536]{2,1,0:T(2,128)(2,1)} %reshape.232), calls=%async_computation.1 | async-start | bytes 16777216 | tf_op jit(solution)/shard_map/all_to_all | solution.py:108
  356.8 185.0 %all-to-all-done.1 = bf16[32,2,65536]{2,1,0:T(2,128)(2,1)} async-done(((bf16[32,2,65536]{2,1,0:T(2,128)(2,1)}), bf16[32,2,65536]{2,1,0:T(2,128)(2,1)}, u32[]{:S(2)}, u32[]{:S(2)}) %all-to-all-start.1) | async-done | bytes 8388640 | tf_op jit(solution)/shard_map/all_to_all | solution.py:108
  541.8 10.2 %reshape.233 = bf16[64,65536]{1,0:T(8,128)(2,1)} reshape(bf16[32,2,65536]{2,1,0:T(2,128)(2,1)} %all-to-all-done.1) | data formatting | bytes 16777216 | tf_op jit(solution)/shard_map/reshape | solution.py:120
  552.0 5.9 convolution_convert_fusion
  557.9 3.4 reshape.234
  561.3 5.9 convolution_bitcast_fusion
  567.2 6.0 copy.99
  573.2 2.9 copy.106
  576.1 4.1 fusion.2
  581.0 2.9 fusion.22
  586.2 5.2 fusion.23
  593.6 212.7 %reduce-scatter.7.cloned.1.call-done = f32[40,1024]{1,0:T(8,128)} async-done(((f32[1280,1024]{1,0:T(8,128)}), f32[40,1024]{1,0:T(8,128)}) %reduce-scatter.7.cloned.1.call-update) | async-done | bytes 163856
  807.9 40.6 %reduce-scatter.5.cloned.1.call-done = f32[12,8,1280]{2,1,0:T(8,128)} async-done(((f32[12,64,1280]{2,1,0:T(8,128)}), f32[12,8,1280]{2,1,0:T(8,128)}) %reduce-scatter.5.cloned.1.call-update) | async-done | bytes 491536 | tf_op jit(solution)/shard_map/reduce_scatter | solution.py:126
  (68 shorter events, 24.4 us)
Async XLA Ops:
  7.2 4.2 copy-start
  7.2 2.7 copy-start.9
  7.2 3.0 copy-start.2
  20.7 11.9 %copy-start.8 = (s32[512]{0:T(512)S(1)}, s32[512]{0:T(512)}, u32[]{:S(2)}) copy-start(s32[512]{0:T(512)} %param.14) | copy-start | bytes 6148
  20.7 13.0 %copy-start.5 = (bf16[512,512]{1,0:T(8,128)(2,1)S(1)}, bf16[512,512]{1,0:T(8,128)(2,1)}, u32[]{:S(2)}) copy-start(bf16[512,512]{1,0:T(8,128)(2,1)} %param.8) | copy-start | bytes 1572868
  20.7 13.9 %copy-start.6 = (bf16[512,512]{1,0:T(8,128)(2,1)S(1)}, bf16[512,512]{1,0:T(8,128)(2,1)}, u32[]{:S(2)}) copy-start(bf16[512,512]{1,0:T(8,128)(2,1)} %param.15) | copy-start | bytes 1572868
  20.7 202.2 %all-to-all-start = ((bf16[32,2,64,1024]{3,2,1,0:T(8,128)(2,1)}), bf16[32,2,64,1024]{3,2,1,0:T(8,128)(2,1)}, u32[]{:S(2)}, u32[]{:S(2)}) async-start(bf16[32,2,64,1024]{3,2,1,0:T(8,128)(2,1)} %bitcast.73), calls=%async_computation | async-start | bytes 16777216 | tf_op jit(solution)/shard_map/all_to_all | solution.py:37
  238.6 4.3 copy-start.1
  238.6 4.3 copy-start.10
  242.9 2.0 copy-start.12
  242.9 2.0 copy-start.13
  249.6 3.1 copy-start.7
  286.6 3.8 copy-start.11
  343.6 198.2 %all-to-all-start.1 = ((bf16[32,2,65536]{2,1,0:T(2,128)(2,1)}), bf16[32,2,65536]{2,1,0:T(2,128)(2,1)}, u32[]{:S(2)}, u32[]{:S(2)}) async-start(bf16[32,2,65536]{2,1,0:T(2,128)(2,1)} %reshape.232), calls=%async_computation.1 | async-start | bytes 16777216 | tf_op jit(solution)/shard_map/all_to_all | solution.py:108
  356.6 449.7 %reduce-scatter.7.cloned.1.call-start = ((), (), s32[]{:S(2)}) async-start(), calls=%async_computation.5 | async-start | bytes 5406720
  573.2 275.3 %reduce-scatter.5.cloned.1.call-start = ((), (), s32[]{:S(2)}) async-start(), calls=%async_computation.4 | async-start | bytes 4423680 | tf_op jit(solution)/shard_map/reduce_scatter | solution.py:126
  573.2 2.9 copy-start.4
  580.3 0.7 copy-start.14
  583.9 2.3 copy-start.3
Sparse Core Ops, SparseCore 0:
  573.3 232.9 reduce-scatter.6
  809.4 38.9 reduce-scatter.4
where the time goes:
time: 864 us; the launch traced here: 856 us
  waiting for transfers between devices  623 us (72%)
  local copies, waits for them, and re-layouts  142 us (16%)
  matrix products  45.1 us (5%)
  starting transfers between devices  24.9 us (3%)
  between operations  14.6 us (2%)
    unnamed x3, waiting for transfers between devices  213 us
    all_to_all x1, waiting for transfers between devices, local(): lax.all_to_all(outgoing.reshape(seq_count, slots_each, latent_rows * 2 *...  185 us
    all_to_all x1, waiting for transfers between devices, local(): lax.all_to_all(projected[sent_local], 'seq', split_axis=0, concat_axis=0,...  185 us
    scatter x1, local copies, waits for them, and re-layouts, local(): outgoing = outgoing.at[send_rows].set(block_grad, mode='drop')  42.7 us
    reduce_scatter x1, waiting for transfers between devices, local(): lax.psum_scatter(latent_part.reshape(images_each, latent_rows, latent_wid...  40.6 us
  transfers between devices with their start and end apart: 4, of which 4 were waited for; matrix products, arithmetic and copies ran while one was open for 3% of the time, Pallas kernels for 0%

commit v1 on v0

v1 whole, which is shorter than its diff:
```python
import jax
import jax.numpy as jnp
from jax import lax
from jax.experimental import pallas as pl
from jax.experimental.pallas import tpu as pltpu
from jax.sharding import Mesh
from jax.sharding import PartitionSpec as P

DH = 128
GAP = 32
WIN = 4
SUB = 8
NEG_FILL = -1e30
BF = jnp.bfloat16
F32 = jnp.float32

NN = (((1,), (0,)), ((), ()))
NT = (((1,), (1,)), ((), ()))
TN = (((0,), (0,)), ((), ()))


def mm(a, b, dims):
    return lax.dot_general(a, b, dims, preferred_element_type=F32)


def shift(v, axis, step, size):
    return lax.ppermute(v, axis, [(i, (i + step) % size) for i in range(size)])


def add2(a, b):
    return (a.astype(F32) + b.astype(F32)).astype(BF)


def vmem():
    return pl.BlockSpec(memory_space=pltpu.VMEM)


def smem():
    return pl.BlockSpec(memory_space=pltpu.SMEM)


def main_kernel(
    start_ref, mine_ref, other_ref, wk_ref, wv_ref, q_ref, g_ref, slot_ref,
    att_ref, dq_ref, bg_ref, lat_ref, dl_ref,
    k_ref, v_ref, acc_ref,
):
    vis = mine_ref.shape[1]
    rows = 2 * mine_ref.shape[0] * SUB
    width = mine_ref.shape[3]
    cols = wk_ref.shape[1]
    heads = cols // DH
    chunk = WIN * rows

    @pl.loop(0, vis // WIN)
    def _(i):
        mine = mine_ref[:, pl.ds(i * WIN, WIN)].astype(F32)
        other = other_ref[:, pl.ds(i * WIN, WIN)].astype(F32)
        parts = []
        for s in range(WIN):
            parts.append(mine[:, s].reshape(rows // 2, width))
            parts.append(other[:, s].reshape(rows // 2, width))
        x = jnp.concatenate(parts, axis=0).astype(BF)
        at = pl.ds(pl.multiple_of(i * chunk, chunk), chunk)
        lat_ref[at, :] = x
        k_ref[at, :] = mm(x, wk_ref[...], NN).astype(BF)
        v_ref[at, :] = mm(x, wv_ref[...], NN).astype(BF)
        acc_ref[at, :] = jnp.zeros((chunk, 2 * cols), F32)

    span = WIN * GAP
    scale = DH ** (-0.5)

    @pl.loop(0, q_ref.shape[0] // span)
    def _(w):
        first = start_ref[w]
        at = pl.ds(pl.multiple_of(first * rows, rows), chunk)
        tok = pl.ds(pl.multiple_of(w * span, span), span)
        slot = slot_ref[w]
        key_slot = first + lax.broadcasted_iota(jnp.int32, (chunk, span), 0) // rows
        match = key_slot == slot
        for h in range(heads):
            c = slice(h * DH, (h + 1) * DH)
            q = q_ref[tok, c]
            g = g_ref[tok, c]
            k = k_ref[at, c]
            v = v_ref[at, c]
            s = jnp.where(match, mm(k, q, NT) * scale, NEG_FILL)
            e = jnp.where(match, jnp.exp(s - jnp.max(s, axis=0, keepdims=True)), 0.0)
            total = jnp.sum(e, axis=0, keepdims=True)
            p = e / jnp.where(total > 0.0, total, 1.0)
            pb = p.astype(BF)
            att_ref[tok, c] = mm(pb, v, TN).astype(BF)
            dp = mm(v, g, NT)
            inner = jnp.sum(p * dp, axis=0, keepdims=True)
            ds = (p * (dp - inner) * scale).astype(BF)
            dq_ref[tok, c] = mm(ds, k, TN).astype(BF)
            acc_ref[at, c] += mm(ds, q, NN)
            acc_ref[at, slice(cols + h * DH, cols + (h + 1) * DH)] += mm(pb, g, NN)

    @pl.loop(0, vis // WIN)
    def _(i):
        at = pl.ds(pl.multiple_of(i * chunk, chunk), chunk)
        grad = acc_ref[at, :].astype(BF)
        bg_ref[at, :] = grad
        out = mm(grad[:, :cols], wk_ref[...], NT) + mm(grad[:, cols:], wv_ref[...], NT)
        for s in range(WIN):
            piece = out[s * rows:(s + 1) * rows].reshape(rows // SUB, SUB, width)
            dl_ref[:, i * WIN + s] = piece.astype(BF)


def weight_kernel(y_ref, lat_ref, bg_ref, out_ref, t_ref):
    ny, nz, part, cols = out_ref.shape
    half = t_ref.shape[0]
    step = 256
    me = y_ref[0]
    for j in range(lat_ref.shape[1] // half):
        t_ref[...] = lat_ref[:, j * half:(j + 1) * half].T

        @pl.loop(0, cols // step)
        def _(n):
            at = pl.ds(pl.multiple_of(n * step, step), step)
            r = mm(t_ref[...], bg_ref[:, at], NN).astype(BF)
            for b in range(half // part):
                piece = j * (half // part) + b
                rel = lax.rem(piece % ny - me + ny, ny)
                out_ref[rel, piece // ny, :, at] = r[b * part:(b + 1) * part]


def collect_kernel(sent_ref, got_ref, out_ref):
    out_ref[...] = jnp.zeros_like(out_ref)

    @pl.loop(0, got_ref.shape[0])
    def _(e):
        image = sent_ref[e]

        @pl.when(image >= 0)
        def _():
            out_ref[image] += got_ref[e].astype(F32)


def local(queries, latents, key_weight, value_weight, visible, outbound, token_slot, grad_out):
    seq = ("z", "y")
    head = ("x", "core")
    nz, ny, nx = (lax.axis_size(a) for a in ("z", "y", "x"))
    tokens, cols = queries.shape
    images, lat_rows, width = latents.shape
    vis = visible.shape[1]
    sent = outbound[0].reshape(-1)
    places = visible[0]
    slots_total = sent.shape[0]
    row_groups = lat_rows // SUB
    part = width // (nz * ny)
    params = pltpu.CompilerParams(vmem_limit_bytes=56 * 1024 * 1024)

    me = lax.axis_index(head)
    pick = jnp.maximum(sent, 0) * row_groups + me
    send = latents.reshape(images * row_groups, SUB, width)[pick]
    got = lax.all_to_all(send, seq, split_axis=0, concat_axis=0, tiled=True)
    own = got[jnp.maximum(places, 0)]

    left = shift(own, "x", 1, nx)
    right = shift(own, "x", -1, nx)
    half = vis // 2
    far_a = shift(left[:half], "x", 1, nx)
    far_b = shift(right[half:], "x", -1, nx)
    mine = jnp.concatenate([own, left, right, far_a, far_b], axis=0).reshape(nx, vis, SUB, width)
    other = shift(mine, "core", 1, 2)

    span = WIN * GAP
    windows = tokens // span
    slot_rows = token_slot.reshape(windows, 1, span)
    start = jnp.minimum(jnp.maximum(slot_rows[:, 0, 0], 0), vis - WIN)
    keys = vis * lat_rows
    att, dq, bg, lat_all, dl = pl.pallas_call(
        main_kernel,
        name="main",
        out_shape=(
            jax.ShapeDtypeStruct((tokens, cols), BF),
            jax.ShapeDtypeStruct((tokens, cols), BF),
            jax.ShapeDtypeStruct((keys, 2 * cols), BF),
            jax.ShapeDtypeStruct((keys, width), BF),
            jax.ShapeDtypeStruct((row_groups, vis, SUB, width), BF),
        ),
        in_specs=[smem()] + [vmem()] * 7,
        out_specs=tuple([vmem()] * 5),
        scratch_shapes=[
            pltpu.VMEM((keys, cols), BF),
            pltpu.VMEM((keys, cols), BF),
            pltpu.VMEM((keys, 2 * cols), F32),
        ],
        compiler_params=params,
        cost_estimate=pl.CostEstimate(
            flops=8 * keys * width * cols + 16 * keys * span * cols,
            bytes_accessed=16 * 1024 * 1024,
            transcendentals=tokens * 4 * 256,
        ),
    )(start, mine, other, key_weight, value_weight, queries, grad_out, slot_rows)

    swapped = shift(dl[nx:], "core", 1, 2)
    summed = add2(dl[:nx], swapped)
    up = shift(summed[3, :half], "x", 1, nx)
    down = shift(summed[3, half:], "x", -1, nx)
    to_right = jnp.concatenate([add2(summed[2, :half], up), summed[2, half:]], axis=0)
    to_left = jnp.concatenate([summed[1, :half], add2(summed[1, half:], down)], axis=0)
    from_left = shift(to_right, "x", 1, nx)
    from_right = shift(to_left, "x", -1, nx)
    dl_mine = (summed[0].astype(F32) + from_left.astype(F32) + from_right.astype(F32)).astype(BF)

    y_here = lax.axis_index("y")
    gw = pl.pallas_call(
        weight_kernel,
        name="weights",
        out_shape=jax.ShapeDtypeStruct((ny, nz, part, 2 * cols), BF),
        in_specs=[smem(), vmem(), vmem()],
        out_specs=vmem(),
        scratch_shapes=[pltpu.VMEM((width // 2, keys), BF)],
        compiler_params=params,
        cost_estimate=pl.CostEstimate(
            flops=4 * keys * width * cols, bytes_accessed=8 * 1024 * 1024, transcendentals=0
        ),
    )(y_here.reshape(1).astype(jnp.int32), lat_all, bg)

    zh = nz // 2
    gw_up = shift(gw[2, :zh], "y", 1, ny)
    gw_down = shift(gw[2, zh:], "y", -1, ny)
    gw_next = jnp.concatenate([add2(gw[1, :zh], gw_up), gw[1, zh:]], axis=0)
    gw_prev = jnp.concatenate([gw[3, :zh], add2(gw[3, zh:], gw_down)], axis=0)
    gw_l = shift(gw_next, "y", 1, ny)
    gw_r = shift(gw_prev, "y", -1, ny)
    gw_y = (gw[0].astype(F32) + gw_l.astype(F32) + gw_r.astype(F32)).astype(BF)

    hits = places[None, :] == jnp.arange(slots_total, dtype=jnp.int32)[:, None]
    back = dl_mine[jnp.argmax(hits, axis=1)]
    returned = lax.all_to_all(back, seq, split_axis=0, concat_axis=0, tiled=True)

    z_here = lax.axis_index("z")
    weights = lax.dynamic_index_in_dim(gw_y, z_here, 0, False).astype(F32)
    for step in (1, -1, 2, -2, 3, -3, 4):
        piece = lax.dynamic_index_in_dim(gw_y, lax.rem(z_here + step + nz, nz), 0, False)
        weights = weights + shift(piece, "z", step, nz).astype(F32)

    grad_latents = pl.pallas_call(
        collect_kernel,
        name="collect",
        out_shape=jax.ShapeDtypeStruct((images, SUB, width), F32),
        in_specs=[smem(), vmem()],
        out_specs=vmem(),
        compiler_params=params,
    )(sent, returned)
    return att, dq, grad_latents, weights[:, :cols], weights[:, cols:]


def solution(mesh):
    sizes = mesh.shape
    nz, ny, nx, core = 8, 4, 4, 2
    assert (sizes["seq"], sizes["head"]) == (nz * ny, nx * core)
    grid = Mesh(mesh.devices.reshape(nz, ny, nx, core), ("z", "y", "x", "core"))
    seq = ("z", "y")
    head = ("x", "core")
    in_specs = (
        P(seq, head),
        P(seq, None, None),
        P(None, head),
        P(None, head),
        P(seq, None),
        P(seq, None, None),
        P(seq),
        P(seq, head),
    )
    out_specs = (
        P(seq, head),
        P(seq, head),
        P(seq, head, None),
        P(seq, head),
        P(seq, head),
    )
    return jax.shard_map(local, mesh=grid, in_specs=in_specs, out_specs=out_specs, check_vma=False)
```

time: 864 us -> 196 us (0.23)
  waiting for transfers between devices: 623 us -> 80 us
  local copies, waits for them, and re-layouts: 142 us -> 17.1 us
  matrix products: 45.1 us -> 0 us
  Pallas kernels: 0 us -> 30.9 us
  starting transfers between devices: 24.9 us -> 53 us
  between operations: 14.6 us -> 0.92 us
    all_to_all x2, waiting for transfers between devices: 370 us -> 32.9 us  [the longest x1 32.9 us: local(): got = lax.all_to_all(send, seq, split_axis=0, concat_axis=0, tiled=True)]
    unnamed x3 -> x0, waiting for transfers between devices: 213 us -> none
    reshape x11 -> x0, local copies, waits for them, and re-layouts: 47.6 us -> none  [the longest x1 15.2 us: local(): key_term.reshape(blocks * window, latent_rows, head_cols)]
    ppermute x0 -> x21, waiting for transfers between devices: none -> 47.1 us  [shift(): return lax.ppermute(v, axis, [(i, (i + step) % size) for i in range(size)])]
    scatter x1 -> x0, local copies, waits for them, and re-layouts: 42.7 us -> none  [local(): outgoing = outgoing.at[send_rows].set(block_grad, mode='drop')]
    dot_general x10 -> x0, matrix products: 40.8 us -> none  [the longest x1 5.92 us: local(): lax.dot_general(latent_flat, kv_flat, (((0,), (0,)), ((), ())), preferred...]
    reduce_scatter x1 -> x0, waiting for transfers between devices: 40.6 us -> none  [local(): lax.psum_scatter(latent_part.reshape(images_each, latent_rows, latent_wid...]
    ppermute x0 -> x21, starting transfers between devices: none -> 34.6 us  [shift(): return lax.ppermute(v, axis, [(i, (i + step) % size) for i in range(size)])]
  transfers between devices with their start and end apart: 4 -> 23, of which waited for: 4 -> 10; matrix products, arithmetic and copies ran while one was open for 3% -> 8% of each run, Pallas kernels for 0% -> 5%
where the time goes in v1:
time: 196 us; the launch traced here: 194 us
  waiting for transfers between devices  80 us (41%)
  starting transfers between devices  53 us (27%)
  Pallas kernels  30.9 us (16%)
  local copies, waits for them, and re-layouts  17.1 us (9%)
  other arithmetic  12.2 us (6%)
    ppermute x21, waiting for transfers between devices, shift(): return lax.ppermute(v, axis, [(i, (i + step) % size) for i in range(size)])  47.1 us
    ppermute x21, starting transfers between devices, shift(): return lax.ppermute(v, axis, [(i, (i + step) % size) for i in range(size)])  34.6 us
    all_to_all x1, waiting for transfers between devices, local(): got = lax.all_to_all(send, seq, split_axis=0, concat_axis=0, tiled=True)  32.9 us
    pallas_call x1, Pallas kernels, local(): pl.pallas_call(main_kernel, name='main', out_shape=(jax.ShapeDtypeStruct(...  19 us
    all_to_all x1, starting transfers between devices, local(): got = lax.all_to_all(send, seq, split_axis=0, concat_axis=0, tiled=True)  11.8 us
    pallas_call x1, Pallas kernels, local(): pl.pallas_call(weight_kernel, name='weights', out_shape=jax.ShapeDtypeStr...  8.86 us
    all_to_all x1, starting transfers between devices, local(): lax.all_to_all(back, seq, split_axis=0, concat_axis=0, tiled=True)  6.51 us
    unnamed x33, local copies, waits for them, and re-layouts  5.33 us
  transfers between devices with their start and end apart: 23, of which 10 were waited for; matrix products, arithmetic and copies ran while one was open for 8% of the time, Pallas kernels for 5%

profile of v1, /device:TPU:8, one launch (start us, length us, event | category | flops | bytes accessed | tf_op | source)
XLA Modules:
  0.0 194.1 jit_solution(16549466138530315804)
XLA Ops:
  2.2 1.7 gather_fusion
  3.9 11.8 %all-to-all-start = ((bf16[64,8,1280]{2,1,0:T(8,128)(2,1)}), bf16[64,8,1280]{2,1,0:T(8,128)(2,1)S(1)}, u32[]{:S(2)}, u32[]{:S(2)}) async-start(bf16[64,8,1280]{2,1,0:T(8,128)(2,1)} %gather_fusion), calls=%async_computation | async-start | bytes 2621440 | tf_op jit(solution)/shard_map/all_to_all | solution.py:157
  15.8 32.9 %all-to-all-done = bf16[64,8,1280]{2,1,0:T(8,128)(2,1)S(1)} async-done(((bf16[64,8,1280]{2,1,0:T(8,128)(2,1)}), bf16[64,8,1280]{2,1,0:T(8,128)(2,1)S(1)}, u32[]{:S(2)}, u32[]{:S(2)}) %all-to-all-start) | async-done | bytes 1310752 | tf_op jit(solution)/shard_map/all_to_all | solution.py:157
  50.0 1.5 collective-permute-start
  51.4 1.7 collective-permute-start.1
  54.2 5.2 %collective-permute-done = bf16[16,8,1280]{2,1,0:T(8,128)(2,1)S(1)} collective-permute-done((bf16[16,8,1280]{2,1,0:T(8,128)(2,1)}, bf16[16,8,1280]{2,1,0:T(8,128)(2,1)S(1)}, u32[]{:S(2)}, u32[]{:S(2)}) %collective-permute-start) | collective-permute-done | bytes 327712 | tf_op jit(solution)/shard_map/ppermute | solution.py:27
  59.8 3.0 %collective-permute-start.3 = (bf16[8,8,1280]{2,1,0:T(8,128)(2,1)S(1)}, bf16[8,8,1280]{2,1,0:T(8,128)(2,1)S(1)}, u32[]{:S(2)}, u32[]{:S(2)}) collective-permute-start(bf16[8,8,1280]{2,1,0:T(8,128)(2,1)S(1)} %slice.92), channel_id=1, source_target_pairs={{0,6},{2,0},{4,2},{6,4},{1,7},{3,1},{5,3},{7,5},{8,14},{10,8},{12,... | collective-permute-start | bytes 491528 | tf_op jit(solution)/shard_map/ppermute | solution.py:27
  62.9 3.1 %collective-permute-done.2 = bf16[8,8,1280]{2,1,0:T(8,128)(2,1)S(1)} collective-permute-done((bf16[8,8,1280]{2,1,0:T(8,128)(2,1)S(1)}, bf16[8,8,1280]{2,1,0:T(8,128)(2,1)S(1)}, u32[]{:S(2)}, u32[]{:S(2)}) %collective-permute-start.2) | collective-permute-done | bytes 163872 | tf_op jit(solution)/shard_map/ppermute | solution.py:27
  67.0 2.2 %collective-permute-done.4.other_ref = bf16[4,16,8,1280]{3,2,1,0:T(8,128)(2,1)S(1)} collective-permute-done((bf16[4,16,8,1280]{3,2,1,0:T(8,128)(2,1)S(1)}, bf16[4,16,8,1280]{3,2,1,0:T(8,128)(2,1)S(1)}, u32[]{:S(2)}, u32[]{:S(2)}) %collective-permute-start.4) | collective-permute-done | bytes 1310752 | tf_op jit(solution)/shard_map/ppermute | solution.py:27
  70.3 19.0 %main.1 = (bf16[512,512]{1,0:T(8,128)(2,1)}, bf16[512,512]{1,0:T(8,128)(2,1)}, bf16[1024,1024]{1,0:T(8,128)(2,1)}, bf16[1024,1280]{1,0:T(8,128)(2,1)}, bf16[8,16,8,1280]{3,2,1,0:T(8,128)(2,1)}) custom-call(s32[4]{0:T(128)} %fusion.14.start_ref, bf16[4,16,8,1280]{3,2,1,0:T(8,128)(2,1)} %bitcast.74, bf16[4,16,8,1280]{3,2,1,0:T(8,128)(2,1)} %copy-done.12, ...), custom_call_target="tpu_custom_call" | custom-call | flops 6442450944 | bytes 16777216 | tf_op jit(solution)/shard_map/main/pallas_call | solution.py:173
  89.2 1.6 slice.67
  91.6 2.3 %collective-permute-done.5 = bf16[4,16,8,1280]{3,2,1,0:T(8,128)(2,1)S(1)} collective-permute-done((bf16[4,16,8,1280]{3,2,1,0:T(8,128)(2,1)S(1)}, bf16[4,16,8,1280]{3,2,1,0:T(8,128)(2,1)S(1)}, u32[]{:S(2)}, u32[]{:S(2)}) %collective-permute-start.5) | collective-permute-done | bytes 1310752 | tf_op jit(solution)/shard_map/ppermute | solution.py:27
  95.7 2.7 %collective-permute-start.8 = (bf16[8,8,1280]{2,1,0:T(8,128)(2,1)}, bf16[8,8,1280]{2,1,0:T(8,128)(2,1)}, u32[]{:S(2)}, u32[]{:S(2)}) collective-permute-start(bf16[8,8,1280]{2,1,0:T(8,128)(2,1)} %get-tuple-element.26), channel_id=1, source_target_pairs={{0,6},{2,0},{4,2},{6,4},{1,7},{3,1},{5,3},{7,5},{8,14},{10,8},{12,... | collective-permute-start | bytes 491528 | tf_op jit(solution)/shard_map/ppermute | solution.py:27
  98.4 4.8 %collective-permute-done.6 = bf16[8,8,1280]{2,1,0:T(8,128)(2,1)} collective-permute-done((bf16[8,8,1280]{2,1,0:T(8,128)(2,1)}, bf16[8,8,1280]{2,1,0:T(8,128)(2,1)}, u32[]{:S(2)}, u32[]{:S(2)}) %collective-permute-start.6) | collective-permute-done | bytes 163872 | tf_op jit(solution)/shard_map/ppermute | solution.py:27
  106.5 2.4 %collective-permute-start.9 = (bf16[16,8,1280]{2,1,0:T(8,128)(2,1)S(1)}, bf16[16,8,1280]{2,1,0:T(8,128)(2,1)S(1)}, u32[]{:S(2)}, u32[]{:S(2)}) collective-permute-start(bf16[16,8,1280]{2,1,0:T(8,128)(2,1)S(1)} %pad_maximum_fusion.3), channel_id=1, source_target_pairs={{0,6},{2,0},{4,2},{6,4},{1,7},{3,1},{5,3},{7,5},{8,14},{10,8},{12,... | collective-permute-start | bytes 983048 | tf_op jit(solution)/shard_map/ppermute | solution.py:27
  108.9 8.9 %weights.1 = bf16[4,8,40,1024]{3,2,1,0:T(8,128)(2,1)} custom-call(s32[1]{0:T(128)} %bitcast.13.y_ref, bf16[1024,1280]{1,0:T(8,128)(2,1)} %get-tuple-element.15.lat_ref, bf16[1024,1024]{1,0:T(8,128)(2,1)} %get-tuple-element.16.bg_ref), custom_call_target="tpu_custom_call" | custom-call | flops 2684354560 | bytes 8388608 | tf_op jit(solution)/shard_map/weights/pallas_call | solution.py:209
  117.7 2.4 %slice_bitcast_fusion.5 = (bf16[4,40,1024]{2,1,0:T(8,128)(2,1)}, bf16[4,40,1024]{2,1,0:T(8,128)(2,1)}, bf16[4,40,1024]{2,1,0:T(8,128)(2,1)}, bf16[4,40,1024]{2,1,0:T(8,128)(2,1)}) fusion(bf16[4,8,40,1024]{3,2,1,0:T(8,128)(2,1)} %weights.1), kind=kLoop, calls=%fused_computation.21 | loop fusion | bytes 2621440 | tf_op jit(solution)/shard_map/squeeze | solution.py:223
  120.1 2.2 %collective-permute-start.10 = (bf16[4,40,1024]{2,1,0:T(8,128)(2,1)}, bf16[4,40,1024]{2,1,0:T(8,128)(2,1)}, u32[]{:S(2)}, u32[]{:S(2)}) collective-permute-start(bf16[4,40,1024]{2,1,0:T(8,128)(2,1)} %get-tuple-element.19), channel_id=1, source_target_pairs={{0,8},{8,16},{16,24},{24,0},{1,9},{9,17},{17,25},{25,1},{2,10},{10... | collective-permute-start | bytes 983048 | tf_op jit(solution)/shard_map/ppermute | solution.py:27
  123.4 1.7 gather_fusion.2
  125.2 6.5 %all-to-all-start.1 = ((bf16[64,8,1280]{2,1,0:T(8,128)(2,1)}), bf16[64,8,1280]{2,1,0:T(8,128)(2,1)S(1)}, u32[]{:S(2)}, u32[]{:S(2)}) async-start(bf16[64,8,1280]{2,1,0:T(8,128)(2,1)} %gather_fusion.2), calls=%async_computation.1 | async-start | bytes 2621440 | tf_op jit(solution)/shard_map/all_to_all | solution.py:233
  131.7 1.6 fusion.3
  134.2 1.5 collective-permute-start.11
  137.1 23.1 %collective-permute-done.11 = bf16[8,40,1024]{2,1,0:T(8,128)(2,1)} collective-permute-done((bf16[8,40,1024]{2,1,0:T(8,128)(2,1)}, bf16[8,40,1024]{2,1,0:T(8,128)(2,1)}, u32[]{:S(2)}, u32[]{:S(2)}) %collective-permute-start.11) | collective-permute-done | bytes 655392 | tf_op jit(solution)/shard_map/ppermute | solution.py:27
  160.3 2.0 %collective-permute-done.13 = bf16[8,40,1024]{2,1,0:T(8,128)(2,1)} collective-permute-done((bf16[8,40,1024]{2,1,0:T(8,128)(2,1)}, bf16[8,40,1024]{2,1,0:T(8,128)(2,1)}, u32[]{:S(2)}, u32[]{:S(2)}) %collective-permute-start.13) | collective-permute-done | bytes 655392 | tf_op jit(solution)/shard_map/ppermute | solution.py:27
  162.3 1.8 fusion.1
  165.6 1.3 collective-permute-start.14
  166.9 1.9 collective-permute-start.15
  169.4 3.6 %collective-permute-start.17 = (bf16[40,1024]{1,0:T(8,128)(2,1)}, bf16[40,1024]{1,0:T(8,128)(2,1)}, u32[]{:S(2)}, u32[]{:S(2)}) collective-permute-start(bf16[40,1024]{1,0:T(8,128)(2,1)} %get-tuple-element.33), channel_id=1, source_target_pairs={{0,192},{32,224},{64,0},{96,32},{128,64},{160,96},{192,128},{224,1... | collective-permute-start | bytes 245768 | tf_op jit(solution)/shard_map/ppermute | solution.py:27
  173.3 4.8 %collective-permute-start.19 = (bf16[40,1024]{1,0:T(8,128)(2,1)S(1)}, bf16[40,1024]{1,0:T(8,128)(2,1)}, u32[]{:S(2)}, u32[]{:S(2)}) collective-permute-start(bf16[40,1024]{1,0:T(8,128)(2,1)S(1)} %get-tuple-element.31), channel_id=1, source_target_pairs={{0,160},{32,192},{64,224},{96,0},{128,32},{160,64},{192,96},{224,1... | collective-permute-start | bytes 245768 | tf_op jit(solution)/shard_map/ppermute | solution.py:27
  178.7 4.2 %collective-permute-start.20 = (bf16[40,1024]{1,0:T(8,128)(2,1)S(1)}, bf16[40,1024]{1,0:T(8,128)(2,1)}, u32[]{:S(2)}, u32[]{:S(2)}) collective-permute-start(bf16[40,1024]{1,0:T(8,128)(2,1)S(1)} %get-tuple-element.30), channel_id=1, source_target_pairs={{0,128},{32,160},{64,192},{96,224},{128,0},{160,32},{192,64},{224,... | collective-permute-start | bytes 245768 | tf_op jit(solution)/shard_map/ppermute | solution.py:27
  184.8 3.2 %collective-permute-done.20 = bf16[40,1024]{1,0:T(8,128)(2,1)} collective-permute-done((bf16[40,1024]{1,0:T(8,128)(2,1)S(1)}, bf16[40,1024]{1,0:T(8,128)(2,1)}, u32[]{:S(2)}, u32[]{:S(2)}) %collective-permute-start.20) | collective-permute-done | bytes 81952 | tf_op jit(solution)/shard_map/ppermute | solution.py:27
  191.0 3.1 %collect.1 = f32[12,8,1280]{2,1,0:T(8,128)} custom-call(s32[64]{0:T(128)} %reshape_squeeze.3.sent_ref, bf16[64,8,1280]{2,1,0:T(8,128)(2,1)} %copy-done.1), custom_call_target="tpu_custom_call" | custom-call | tf_op jit(solution)/shard_map/collect/pallas_call | solution.py:241
  (83 shorter events, 23.8 us)
Async XLA Ops:
  3.9 11.8 %copy-start.13 = (s32[1,16]{1,0:T(1,128)S(1)}, s32[1,16]{1,0:T(1,128)}, u32[]{:S(2)}) copy-start(s32[1,16]{1,0:T(1,128)} %param.12) | copy-start | bytes 196
  3.9 44.7 %all-to-all-start = ((bf16[64,8,1280]{2,1,0:T(8,128)(2,1)}), bf16[64,8,1280]{2,1,0:T(8,128)(2,1)S(1)}, u32[]{:S(2)}, u32[]{:S(2)}) async-start(bf16[64,8,1280]{2,1,0:T(8,128)(2,1)} %gather_fusion), calls=%async_computation | async-start | bytes 2621440 | tf_op jit(solution)/shard_map/all_to_all | solution.py:157
  50.0 9.4 %collective-permute-start = (bf16[16,8,1280]{2,1,0:T(8,128)(2,1)}, bf16[16,8,1280]{2,1,0:T(8,128)(2,1)S(1)}, u32[]{:S(2)}, u32[]{:S(2)}) collective-permute-start(bf16[16,8,1280]{2,1,0:T(8,128)(2,1)} %gather_fusion.1), channel_id=1, source_target_pairs={{0,2},{2,4},{4,6},{6,0},{1,3},{3,5},{5,7},{7,1},{8,10},{10,12},{12... | collective-permute-start | bytes 983048 | tf_op jit(solution)/shard_map/ppermute | solution.py:27
  51.4 8.3 %collective-permute-start.1 = (bf16[16,8,1280]{2,1,0:T(8,128)(2,1)}, bf16[16,8,1280]{2,1,0:T(8,128)(2,1)S(1)}, u32[]{:S(2)}, u32[]{:S(2)}) collective-permute-start(bf16[16,8,1280]{2,1,0:T(8,128)(2,1)} %gather_fusion.1), channel_id=1, source_target_pairs={{0,6},{2,0},{4,2},{6,4},{1,7},{3,1},{5,3},{7,5},{8,14},{10,8},{12,... | collective-permute-start | bytes 983048 | tf_op jit(solution)/shard_map/ppermute | solution.py:27
  54.2 12.0 %copy-start.11 = (s32[512]{0:T(512)S(1)}, s32[512]{0:T(512)}, u32[]{:S(2)}) copy-start(s32[512]{0:T(512)} %param.14) | copy-start | bytes 6148
  59.4 6.6 %collective-permute-start.2 = (bf16[8,8,1280]{2,1,0:T(8,128)(2,1)S(1)}, bf16[8,8,1280]{2,1,0:T(8,128)(2,1)S(1)}, u32[]{:S(2)}, u32[]{:S(2)}) collective-permute-start(bf16[8,8,1280]{2,1,0:T(8,128)(2,1)S(1)} %slice.91), channel_id=1, source_target_pairs={{0,2},{2,4},{4,6},{6,0},{1,3},{3,5},{5,7},{7,1},{8,10},{10,12},{12... | collective-permute-start | bytes 491528 | tf_op jit(solution)/shard_map/ppermute | solution.py:27
  59.8 6.2 %collective-permute-start.3 = (bf16[8,8,1280]{2,1,0:T(8,128)(2,1)S(1)}, bf16[8,8,1280]{2,1,0:T(8,128)(2,1)S(1)}, u32[]{:S(2)}, u32[]{:S(2)}) collective-permute-start(bf16[8,8,1280]{2,1,0:T(8,128)(2,1)S(1)} %slice.92), channel_id=1, source_target_pairs={{0,6},{2,0},{4,2},{6,4},{1,7},{3,1},{5,3},{7,5},{8,14},{10,8},{12,... | collective-permute-start | bytes 491528 | tf_op jit(solution)/shard_map/ppermute | solution.py:27
  66.1 3.1 %copy-start.7 = (bf16[64,8,1280]{2,1,0:T(8,128)(2,1)}, bf16[64,8,1280]{2,1,0:T(8,128)(2,1)S(1)}, u32[]{:S(2)}) copy-start(bf16[64,8,1280]{2,1,0:T(8,128)(2,1)S(1)} %constant_dynamic-update-slice_fusion) | copy-start | bytes 3932164
  66.1 3.1 %collective-permute-start.4 = (bf16[4,16,8,1280]{3,2,1,0:T(8,128)(2,1)S(1)}, bf16[4,16,8,1280]{3,2,1,0:T(8,128)(2,1)S(1)}, u32[]{:S(2)}, u32[]{:S(2)}) collective-permute-start(bf16[4,16,8,1280]{3,2,1,0:T(8,128)(2,1)S(1)} %bitcast.73), channel_id=1, source_target_pairs={{0,1},{1,0},{2,3},{3,2},{4,5},{5,4},{6,7},{7,6},{8,9},{9,8},{10,11... | collective-permute-start | bytes 3932168 | tf_op jit(solution)/shard_map/ppermute | solution.py:27
  89.2 4.7 %copy-start.4 = (bf16[8,16,8,1280]{3,2,1,0:T(8,128)(2,1)S(1)}, bf16[8,16,8,1280]{3,2,1,0:T(8,128)(2,1)}, u32[]{:S(2)}) copy-start(bf16[8,16,8,1280]{3,2,1,0:T(8,128)(2,1)} %get-tuple-element.13) | copy-start | bytes 7864324
  90.8 3.1 %collective-permute-start.5 = (bf16[4,16,8,1280]{3,2,1,0:T(8,128)(2,1)S(1)}, bf16[4,16,8,1280]{3,2,1,0:T(8,128)(2,1)S(1)}, u32[]{:S(2)}, u32[]{:S(2)}) collective-permute-start(bf16[4,16,8,1280]{3,2,1,0:T(8,128)(2,1)S(1)} %slice.67), channel_id=1, source_target_pairs={{0,1},{1,0},{2,3},{3,2},{4,5},{5,4},{6,7},{7,6},{8,9},{9,8},{10,11... | collective-permute-start | bytes 3932168 | tf_op jit(solution)/shard_map/ppermute | solution.py:27
  94.2 11.0 %copy-start.2 = (bf16[4,16,8,1280]{3,2,1,0:T(8,128)(2,1)}, bf16[4,16,8,1280]{3,2,1,0:T(8,128)(2,1)S(1)}, u32[]{:S(2)}) copy-start(bf16[4,16,8,1280]{3,2,1,0:T(8,128)(2,1)S(1)} %add_convert_fusion) | copy-start | bytes 3932164
  95.1 8.1 %collective-permute-start.6 = (bf16[8,8,1280]{2,1,0:T(8,128)(2,1)}, bf16[8,8,1280]{2,1,0:T(8,128)(2,1)}, u32[]{:S(2)}, u32[]{:S(2)}) collective-permute-start(bf16[8,8,1280]{2,1,0:T(8,128)(2,1)} %get-tuple-element.25), channel_id=1, source_target_pairs={{0,2},{2,4},{4,6},{6,0},{1,3},{3,5},{5,7},{7,1},{8,10},{10,12},{12... | collective-permute-start | bytes 491528 | tf_op jit(solution)/shard_map/ppermute | solution.py:27
  95.7 7.5 %collective-permute-start.8 = (bf16[8,8,1280]{2,1,0:T(8,128)(2,1)}, bf16[8,8,1280]{2,1,0:T(8,128)(2,1)}, u32[]{:S(2)}, u32[]{:S(2)}) collective-permute-start(bf16[8,8,1280]{2,1,0:T(8,128)(2,1)} %get-tuple-element.26), channel_id=1, source_target_pairs={{0,6},{2,0},{4,2},{6,4},{1,7},{3,1},{5,3},{7,5},{8,14},{10,8},{12,... | collective-permute-start | bytes 491528 | tf_op jit(solution)/shard_map/ppermute | solution.py:27
  105.3 17.1 %collective-permute-start.7 = (bf16[16,8,1280]{2,1,0:T(8,128)(2,1)S(1)}, bf16[16,8,1280]{2,1,0:T(8,128)(2,1)S(1)}, u32[]{:S(2)}, u32[]{:S(2)}) collective-permute-start(bf16[16,8,1280]{2,1,0:T(8,128)(2,1)S(1)} %pad_maximum_fusion.2), channel_id=1, source_target_pairs={{0,2},{2,4},{4,6},{6,0},{1,3},{3,5},{5,7},{7,1},{8,10},{10,12},{12... | collective-permute-start | bytes 983048 | tf_op jit(solution)/shard_map/ppermute | solution.py:27
  106.5 15.8 %collective-permute-start.9 = (bf16[16,8,1280]{2,1,0:T(8,128)(2,1)S(1)}, bf16[16,8,1280]{2,1,0:T(8,128)(2,1)S(1)}, u32[]{:S(2)}, u32[]{:S(2)}) collective-permute-start(bf16[16,8,1280]{2,1,0:T(8,128)(2,1)S(1)} %pad_maximum_fusion.3), channel_id=1, source_target_pairs={{0,6},{2,0},{4,2},{6,4},{1,7},{3,1},{5,3},{7,5},{8,14},{10,8},{12,... | collective-permute-start | bytes 983048 | tf_op jit(solution)/shard_map/ppermute | solution.py:27
  120.1 11.6 %collective-permute-start.10 = (bf16[4,40,1024]{2,1,0:T(8,128)(2,1)}, bf16[4,40,1024]{2,1,0:T(8,128)(2,1)}, u32[]{:S(2)}, u32[]{:S(2)}) collective-permute-start(bf16[4,40,1024]{2,1,0:T(8,128)(2,1)} %get-tuple-element.19), channel_id=1, source_target_pairs={{0,8},{8,16},{16,24},{24,0},{1,9},{9,17},{17,25},{25,1},{2,10},{10... | collective-permute-start | bytes 983048 | tf_op jit(solution)/shard_map/ppermute | solution.py:27
  122.3 9.4 %collective-permute-start.12 = (bf16[4,40,1024]{2,1,0:T(8,128)(2,1)}, bf16[4,40,1024]{2,1,0:T(8,128)(2,1)}, u32[]{:S(2)}, u32[]{:S(2)}) collective-permute-start(bf16[4,40,1024]{2,1,0:T(8,128)(2,1)} %get-tuple-element.20), channel_id=1, source_target_pairs={{0,24},{8,0},{16,8},{24,16},{1,25},{9,1},{17,9},{25,17},{2,26},{10... | collective-permute-start | bytes 983048 | tf_op jit(solution)/shard_map/ppermute | solution.py:27
  125.2 64.8 %all-to-all-start.1 = ((bf16[64,8,1280]{2,1,0:T(8,128)(2,1)}), bf16[64,8,1280]{2,1,0:T(8,128)(2,1)S(1)}, u32[]{:S(2)}, u32[]{:S(2)}) async-start(bf16[64,8,1280]{2,1,0:T(8,128)(2,1)} %gather_fusion.2), calls=%async_computation.1 | async-start | bytes 2621440 | tf_op jit(solution)/shard_map/all_to_all | solution.py:233
  131.7 1.6 copy-start.6
  131.7 4.0 %copy-start.5 = (bf16[4,40,1024]{2,1,0:T(8,128)(2,1)S(1)}, bf16[4,40,1024]{2,1,0:T(8,128)(2,1)}, u32[]{:S(2)}) copy-start(bf16[4,40,1024]{2,1,0:T(8,128)(2,1)} %get-tuple-element.21) | copy-start | bytes 983044
  134.2 26.1 %collective-permute-start.11 = (bf16[8,40,1024]{2,1,0:T(8,128)(2,1)}, bf16[8,40,1024]{2,1,0:T(8,128)(2,1)}, u32[]{:S(2)}, u32[]{:S(2)}) collective-permute-start(bf16[8,40,1024]{2,1,0:T(8,128)(2,1)} %pad_maximum_fusion), channel_id=1, source_target_pairs={{0,8},{8,16},{16,24},{24,0},{1,9},{9,17},{17,25},{25,1},{2,10},{10... | collective-permute-start | bytes 1966088 | tf_op jit(solution)/shard_map/ppermute | solution.py:27
  136.6 25.7 %collective-permute-start.13 = (bf16[8,40,1024]{2,1,0:T(8,128)(2,1)}, bf16[8,40,1024]{2,1,0:T(8,128)(2,1)}, u32[]{:S(2)}, u32[]{:S(2)}) collective-permute-start(bf16[8,40,1024]{2,1,0:T(8,128)(2,1)} %pad_maximum_fusion.1), channel_id=1, source_target_pairs={{0,24},{8,0},{16,8},{24,16},{1,25},{9,1},{17,9},{25,17},{2,26},{10... | collective-permute-start | bytes 1966088 | tf_op jit(solution)/shard_map/ppermute | solution.py:27
  137.1 45.7 %copy-start.10 = (s32[1,32,2]{1,2,0:T(2,128)S(1)}, s32[1,32,2]{1,2,0:T(2,128)}, u32[]{:S(2)}) copy-start(s32[1,32,2]{1,2,0:T(2,128)} %param.13) | copy-start | bytes 772
  165.6 7.6 %collective-permute-start.14 = (bf16[40,1024]{1,0:T(8,128)(2,1)S(1)}, bf16[40,1024]{1,0:T(8,128)(2,1)S(1)}, u32[]{:S(2)}, u32[]{:S(2)}) collective-permute-start(bf16[40,1024]{1,0:T(8,128)(2,1)S(1)} %get-tuple-element.29), channel_id=1, source_target_pairs={{0,32},{32,64},{64,96},{96,128},{128,160},{160,192},{192,224},{224... | collective-permute-start | bytes 245768 | tf_op jit(solution)/shard_map/ppermute | solution.py:27
  166.9 11.1 %collective-permute-start.15 = (bf16[40,1024]{1,0:T(8,128)(2,1)S(1)}, bf16[40,1024]{1,0:T(8,128)(2,1)S(1)}, u32[]{:S(2)}, u32[]{:S(2)}) collective-permute-start(bf16[40,1024]{1,0:T(8,128)(2,1)S(1)} %get-tuple-element.35), channel_id=1, source_target_pairs={{0,224},{32,0},{64,32},{96,64},{128,96},{160,128},{192,160},{224,1... | collective-permute-start | bytes 245768 | tf_op jit(solution)/shard_map/ppermute | solution.py:27
  168.8 14.8 %collective-permute-start.16 = (bf16[40,1024]{1,0:T(8,128)(2,1)}, bf16[40,1024]{1,0:T(8,128)(2,1)}, u32[]{:S(2)}, u32[]{:S(2)}) collective-permute-start(bf16[40,1024]{1,0:T(8,128)(2,1)} %get-tuple-element.34), channel_id=1, source_target_pairs={{0,64},{32,96},{64,128},{96,160},{128,192},{160,224},{192,0},{224,... | collective-permute-start | bytes 245768 | tf_op jit(solution)/shard_map/ppermute | solution.py:27
  169.4 14.2 %collective-permute-start.17 = (bf16[40,1024]{1,0:T(8,128)(2,1)}, bf16[40,1024]{1,0:T(8,128)(2,1)}, u32[]{:S(2)}, u32[]{:S(2)}) collective-permute-start(bf16[40,1024]{1,0:T(8,128)(2,1)} %get-tuple-element.33), channel_id=1, source_target_pairs={{0,192},{32,224},{64,0},{96,32},{128,64},{160,96},{192,128},{224,1... | collective-permute-start | bytes 245768 | tf_op jit(solution)/shard_map/ppermute | solution.py:27
  173.0 10.6 %collective-permute-start.18 = (bf16[40,1024]{1,0:T(8,128)(2,1)S(1)}, bf16[40,1024]{1,0:T(8,128)(2,1)}, u32[]{:S(2)}, u32[]{:S(2)}) collective-permute-start(bf16[40,1024]{1,0:T(8,128)(2,1)S(1)} %get-tuple-element.32), channel_id=1, source_target_pairs={{0,96},{32,128},{64,160},{96,192},{128,224},{160,0},{192,32},{224,... | collective-permute-start | bytes 245768 | tf_op jit(solution)/shard_map/ppermute | solution.py:27
  173.3 4.8 %copy-start.8 = (bf16[40,1024]{1,0:T(8,128)(2,1)}, bf16[40,1024]{1,0:T(8,128)(2,1)S(1)}, u32[]{:S(2)}) copy-start(bf16[40,1024]{1,0:T(8,128)(2,1)S(1)} %collective-permute-done.14) | copy-start | bytes 245764
  173.3 11.6 %collective-permute-start.19 = (bf16[40,1024]{1,0:T(8,128)(2,1)S(1)}, bf16[40,1024]{1,0:T(8,128)(2,1)}, u32[]{:S(2)}, u32[]{:S(2)}) collective-permute-start(bf16[40,1024]{1,0:T(8,128)(2,1)S(1)} %get-tuple-element.31), channel_id=1, source_target_pairs={{0,160},{32,192},{64,224},{96,0},{128,32},{160,64},{192,96},{224,1... | collective-permute-start | bytes 245768 | tf_op jit(solution)/shard_map/ppermute | solution.py:27
  178.7 9.3 %collective-permute-start.20 = (bf16[40,1024]{1,0:T(8,128)(2,1)S(1)}, bf16[40,1024]{1,0:T(8,128)(2,1)}, u32[]{:S(2)}, u32[]{:S(2)}) collective-permute-start(bf16[40,1024]{1,0:T(8,128)(2,1)S(1)} %get-tuple-element.30), channel_id=1, source_target_pairs={{0,128},{32,160},{64,192},{96,224},{128,0},{160,32},{192,64},{224,... | collective-permute-start | bytes 245768 | tf_op jit(solution)/shard_map/ppermute | solution.py:27
  (5 other events, 5.2 us)

commit v2 on v1

--- a/solution.py
+++ b/solution.py
@@ -31,6 +31,10 @@
     return (a.astype(F32) + b.astype(F32)).astype(BF)
 
 
+def grant(mib):
+    return pltpu.CompilerParams(vmem_limit_bytes=mib * 1024 * 1024)
+
+
 def vmem():
     return pl.BlockSpec(memory_space=pltpu.VMEM)
 
@@ -41,7 +45,7 @@
 
 def main_kernel(
     start_ref, mine_ref, other_ref, wk_ref, wv_ref, q_ref, g_ref, slot_ref,
-    att_ref, dq_ref, bg_ref, lat_ref, dl_ref,
+    att_ref, dq_ref, bg_ref, lat_ref, keep_ref, give_ref,
     k_ref, v_ref, acc_ref,
 ):
     vis = mine_ref.shape[1]
@@ -103,14 +107,17 @@
         bg_ref[at, :] = grad
         out = mm(grad[:, :cols], wk_ref[...], NT) + mm(grad[:, cols:], wv_ref[...], NT)
         for s in range(WIN):
-            piece = out[s * rows:(s + 1) * rows].reshape(rows // SUB, SUB, width)
-            dl_ref[:, i * WIN + s] = piece.astype(BF)
-
-
-def weight_kernel(y_ref, lat_ref, bg_ref, out_ref, t_ref):
-    ny, nz, part, cols = out_ref.shape
+            piece = out[s * rows:(s + 1) * rows].reshape(rows // SUB, SUB, width).astype(BF)
+            keep_ref[:, i * WIN + s] = piece[:rows // SUB // 2]
+            give_ref[:, i * WIN + s] = piece[rows // SUB // 2:]
+
+
+def weight_kernel(y_ref, lat_ref, bg_ref, own_ref, next_ref, fa_ref, fb_ref, prev_ref, t_ref, sum_ref):
+    nz, part, cols = own_ref.shape
+    ny = lat_ref.shape[1] // (nz * part)
     half = t_ref.shape[0]
     step = 256
+    zh = nz // 2
     me = y_ref[0]
     for j in range(lat_ref.shape[1] // half):
         t_ref[...] = lat_ref[:, j * half:(j + 1) * half].T
@@ -118,11 +125,20 @@
         @pl.loop(0, cols // step)
         def _(n):
             at = pl.ds(pl.multiple_of(n * step, step), step)
-            r = mm(t_ref[...], bg_ref[:, at], NN).astype(BF)
-            for b in range(half // part):
-                piece = j * (half // part) + b
-                rel = lax.rem(piece % ny - me + ny, ny)
-                out_ref[rel, piece // ny, :, at] = r[b * part:(b + 1) * part]
+            sum_ref[j * half:(j + 1) * half, at] = mm(t_ref[...], bg_ref[:, at], NN)
+
+    def block(z, rel):
+        there = lax.rem(me + rel, ny)
+        return sum_ref[pl.ds(pl.multiple_of((z * ny + there) * part, SUB), part), :].astype(BF)
+
+    for z in range(nz):
+        own_ref[z] = block(z, 0)
+        next_ref[z] = block(z, 1)
+        prev_ref[z] = block(z, 3)
+        if z < zh:
+            fa_ref[z] = block(z, 2)
+        else:
+            fb_ref[z - zh] = block(z, 2)
 
 
 def collect_kernel(sent_ref, got_ref, out_ref):
@@ -149,7 +165,6 @@
     slots_total = sent.shape[0]
     row_groups = lat_rows // SUB
     part = width // (nz * ny)
-    params = pltpu.CompilerParams(vmem_limit_bytes=56 * 1024 * 1024)
 
     me = lax.axis_index(head)
     pick = jnp.maximum(sent, 0) * row_groups + me
@@ -170,7 +185,7 @@
     slot_rows = token_slot.reshape(windows, 1, span)
     start = jnp.minimum(jnp.maximum(slot_rows[:, 0, 0], 0), vis - WIN)
     keys = vis * lat_rows
-    att, dq, bg, lat_all, dl = pl.pallas_call(
+    att, dq, bg, lat_all, keep, give = pl.pallas_call(
         main_kernel,
         name="main",
         out_shape=(
@@ -178,16 +193,17 @@
             jax.ShapeDtypeStruct((tokens, cols), BF),
             jax.ShapeDtypeStruct((keys, 2 * cols), BF),
             jax.ShapeDtypeStruct((keys, width), BF),
-            jax.ShapeDtypeStruct((row_groups, vis, SUB, width), BF),
+            jax.ShapeDtypeStruct((nx, vis, SUB, width), BF),
+            jax.ShapeDtypeStruct((nx, vis, SUB, width), BF),
         ),
         in_specs=[smem()] + [vmem()] * 7,
-        out_specs=tuple([vmem()] * 5),
+        out_specs=tuple([vmem()] * 6),
         scratch_shapes=[
             pltpu.VMEM((keys, cols), BF),
             pltpu.VMEM((keys, cols), BF),
             pltpu.VMEM((keys, 2 * cols), F32),
         ],
-        compiler_params=params,
+        compiler_params=grant(32),
         cost_estimate=pl.CostEstimate(
             flops=8 * keys * width * cols + 16 * keys * span * cols,
             bytes_accessed=16 * 1024 * 1024,
@@ -195,38 +211,48 @@
         ),
     )(start, mine, other, key_weight, value_weight, queries, grad_out, slot_rows)
 
-    swapped = shift(dl[nx:], "core", 1, 2)
-    summed = add2(dl[:nx], swapped)
-    up = shift(summed[3, :half], "x", 1, nx)
-    down = shift(summed[3, half:], "x", -1, nx)
-    to_right = jnp.concatenate([add2(summed[2, :half], up), summed[2, half:]], axis=0)
-    to_left = jnp.concatenate([summed[1, :half], add2(summed[1, half:], down)], axis=0)
-    from_left = shift(to_right, "x", 1, nx)
-    from_right = shift(to_left, "x", -1, nx)
-    dl_mine = (summed[0].astype(F32) + from_left.astype(F32) + from_right.astype(F32)).astype(BF)
+    swapped = shift(give, "core", 1, 2)
 
     y_here = lax.axis_index("y")
-    gw = pl.pallas_call(
+    zh = nz // 2
+    full = jax.ShapeDtypeStruct((nz, part, 2 * cols), BF)
+    split = jax.ShapeDtypeStruct((zh, part, 2 * cols), BF)
+    gw_own, gw_next, gw_fa, gw_fb, gw_prev = pl.pallas_call(
         weight_kernel,
         name="weights",
-        out_shape=jax.ShapeDtypeStruct((ny, nz, part, 2 * cols), BF),
+        out_shape=(full, full, split, split, full),
         in_specs=[smem(), vmem(), vmem()],
-        out_specs=vmem(),
-        scratch_shapes=[pltpu.VMEM((width // 2, keys), BF)],
-        compiler_params=params,
+        out_specs=tuple([vmem()] * 5),
+        scratch_shapes=[pltpu.VMEM((width // 2, keys), BF), pltpu.VMEM((width, 2 * cols), F32)],
+        compiler_params=grant(24),
         cost_estimate=pl.CostEstimate(
             flops=4 * keys * width * cols, bytes_accessed=8 * 1024 * 1024, transcendentals=0
         ),
     )(y_here.reshape(1).astype(jnp.int32), lat_all, bg)
 
-    zh = nz // 2
-    gw_up = shift(gw[2, :zh], "y", 1, ny)
-    gw_down = shift(gw[2, zh:], "y", -1, ny)
-    gw_next = jnp.concatenate([add2(gw[1, :zh], gw_up), gw[1, zh:]], axis=0)
-    gw_prev = jnp.concatenate([gw[3, :zh], add2(gw[3, zh:], gw_down)], axis=0)
+    swapped, gw_fa, gw_fb = lax.optimization_barrier((swapped, gw_fa, gw_fb))
+    gw_up = shift(gw_fa, "y", 1, ny)
+    gw_down = shift(gw_fb, "y", -1, ny)
+
+    up = shift(add2(keep[3, :half], swapped[3, :half]), "x", 1, nx)
+    down = shift(add2(keep[3, half:], swapped[3, half:]), "x", -1, nx)
+    to_right = (keep[2].astype(F32) + swapped[2].astype(F32)
+                + jnp.concatenate([up, jnp.zeros_like(up)], axis=0).astype(F32)).astype(BF)
+    to_left = (keep[1].astype(F32) + swapped[1].astype(F32)
+               + jnp.concatenate([jnp.zeros_like(down), down], axis=0).astype(F32)).astype(BF)
+    from_left = shift(to_right, "x", 1, nx)
+    from_right = shift(to_left, "x", -1, nx)
+    dl_mine = (
+        keep[0].astype(F32) + swapped[0].astype(F32) + from_left.astype(F32) + from_right.astype(F32)
+    ).astype(BF)
+
+    gw_next = (gw_next.astype(F32)
+               + jnp.concatenate([gw_up, jnp.zeros_like(gw_up)], axis=0).astype(F32)).astype(BF)
+    gw_prev = (gw_prev.astype(F32)
+               + jnp.concatenate([jnp.zeros_like(gw_down), gw_down], axis=0).astype(F32)).astype(BF)
     gw_l = shift(gw_next, "y", 1, ny)
     gw_r = shift(gw_prev, "y", -1, ny)
-    gw_y = (gw[0].astype(F32) + gw_l.astype(F32) + gw_r.astype(F32)).astype(BF)
+    gw_y = (gw_own.astype(F32) + gw_l.astype(F32) + gw_r.astype(F32)).astype(BF)
 
     hits = places[None, :] == jnp.arange(slots_total, dtype=jnp.int32)[:, None]
     back = dl_mine[jnp.argmax(hits, axis=1)]
@@ -244,7 +270,7 @@
         out_shape=jax.ShapeDtypeStruct((images, SUB, width), F32),
         in_specs=[smem(), vmem()],
         out_specs=vmem(),
-        compiler_params=params,
+        compiler_params=grant(8),
     )(sent, returned)
     return att, dq, grad_latents, weights[:, :cols], weights[:, cols:]
 

time: 196 us -> 200 us (1.020)
  Pallas kernels: 30.9 us -> 23.8 us
  starting transfers between devices: 53 us -> 58.1 us
  waiting for transfers between devices: 80 us -> 84.4 us
    convert_element_type x2 -> x5, other arithmetic: 2.9 us -> 8.05 us  [the longest x1 2.13 us: local(): gw_next = (gw_next.astype(F32) + jnp.concatenate([gw_up, jnp.zeros_like(g...]
    unnamed x33 -> x45, local copies, waits for them, and re-layouts: 5.33 us -> 10.4 us
    ppermute x21, starting transfers between devices: 34.6 us -> 39.6 us  [shift(): return lax.ppermute(v, axis, [(i, (i + step) % size) for i in range(size)])]
    ppermute x21, waiting for transfers between devices: 47.1 us -> 51.5 us  [shift(): return lax.ppermute(v, axis, [(i, (i + step) % size) for i in range(size)])]
    pallas_call x1, Pallas kernels: 19 us -> 15.5 us  [local(): pl.pallas_call(main_kernel, name='main', out_shape=(jax.ShapeDtypeStruct(...]
    squeeze x2 -> x0, local copies, waits for them, and re-layouts: 3.24 us -> none  [the longest x1 2.36 us: local(): gw_up = shift(gw[2, :zh], 'y', 1, ny)]
    pallas_call x1, Pallas kernels: 8.86 us -> 5.96 us  [local(): pl.pallas_call(weight_kernel, name='weights', out_shape=(full, full, spli...]
    concatenate x4 -> x0, other arithmetic: 2.8 us -> none  [the longest x1 0.95 us: local(): jnp.concatenate([add2(summed[2, :half], up), summed[2, half:]], axis=0)]
  transfers between devices with their start and end apart: 23 -> 23, of which waited for: 10 -> 10; matrix products, arithmetic and copies ran while one was open for 8% -> 7% of each run, Pallas kernels for 5% -> 3%
where the time goes in v2:
time: 200 us; the launch traced here: 197 us
  waiting for transfers between devices  84.4 us (42%)
  starting transfers between devices  58.1 us (29%)
  Pallas kernels  23.8 us (12%)
  local copies, waits for them, and re-layouts  17.8 us (9%)
  other arithmetic  12.4 us (6%)
    ppermute x21, waiting for transfers between devices, shift(): return lax.ppermute(v, axis, [(i, (i + step) % size) for i in range(size)])  51.5 us
    ppermute x21, starting transfers between devices, shift(): return lax.ppermute(v, axis, [(i, (i + step) % size) for i in range(size)])  39.6 us
    all_to_all x1, waiting for transfers between devices, local(): got = lax.all_to_all(send, seq, split_axis=0, concat_axis=0, tiled=True)  32.9 us
    pallas_call x1, Pallas kernels, local(): pl.pallas_call(main_kernel, name='main', out_shape=(jax.ShapeDtypeStruct(...  15.5 us
    all_to_all x1, starting transfers between devices, local(): got = lax.all_to_all(send, seq, split_axis=0, concat_axis=0, tiled=True)  11.8 us
    unnamed x45, local copies, waits for them, and re-layouts  10.4 us
    all_to_all x1, starting transfers between devices, local(): lax.all_to_all(back, seq, split_axis=0, concat_axis=0, tiled=True)  6.67 us
    pallas_call x1, Pallas kernels, local(): pl.pallas_call(weight_kernel, name='weights', out_shape=(full, full, spli...  5.96 us
  transfers between devices with their start and end apart: 23, of which 10 were waited for; matrix products, arithmetic and copies ran while one was open for 7% of the time, Pallas kernels for 3%

profile of v2, /device:TPU:8, one launch (start us, length us, event | category | flops | bytes accessed | tf_op | source)
XLA Modules:
  0.0 197.4 jit_solution(12727026495063622877)
XLA Ops:
  3.9 11.8 %all-to-all-start = ((bf16[64,8,1280]{2,1,0:T(8,128)(2,1)}), bf16[64,8,1280]{2,1,0:T(8,128)(2,1)S(1)}, u32[]{:S(2)}, u32[]{:S(2)}) async-start(bf16[64,8,1280]{2,1,0:T(8,128)(2,1)} %gather_fusion), calls=%async_computation | async-start | bytes 2621440 | tf_op jit(solution)/shard_map/all_to_all | solution.py:172
  15.8 32.9 %all-to-all-done = bf16[64,8,1280]{2,1,0:T(8,128)(2,1)S(1)} async-done(((bf16[64,8,1280]{2,1,0:T(8,128)(2,1)}), bf16[64,8,1280]{2,1,0:T(8,128)(2,1)S(1)}, u32[]{:S(2)}, u32[]{:S(2)}) %all-to-all-start) | async-done | bytes 1310752 | tf_op jit(solution)/shard_map/all_to_all | solution.py:172
  51.4 1.7 collective-permute-start.1
  54.3 5.1 %collective-permute-done = bf16[16,8,1280]{2,1,0:T(8,128)(2,1)S(1)} collective-permute-done((bf16[16,8,1280]{2,1,0:T(8,128)(2,1)}, bf16[16,8,1280]{2,1,0:T(8,128)(2,1)S(1)}, u32[]{:S(2)}, u32[]{:S(2)}) %collective-permute-start) | collective-permute-done | bytes 327712 | tf_op jit(solution)/shard_map/ppermute | solution.py:27
  59.8 3.0 %collective-permute-start.3 = (bf16[8,8,1280]{2,1,0:T(8,128)(2,1)S(1)}, bf16[8,8,1280]{2,1,0:T(8,128)(2,1)S(1)}, u32[]{:S(2)}, u32[]{:S(2)}) collective-permute-start(bf16[8,8,1280]{2,1,0:T(8,128)(2,1)S(1)} %slice.68), channel_id=1, source_target_pairs={{0,6},{2,0},{4,2},{6,4},{1,7},{3,1},{5,3},{7,5},{8,14},{10,8},{12,... | collective-permute-start | bytes 491528 | tf_op jit(solution)/shard_map/ppermute | solution.py:27
  62.9 3.1 %collective-permute-done.2 = bf16[8,8,1280]{2,1,0:T(8,128)(2,1)S(1)} collective-permute-done((bf16[8,8,1280]{2,1,0:T(8,128)(2,1)S(1)}, bf16[8,8,1280]{2,1,0:T(8,128)(2,1)S(1)}, u32[]{:S(2)}, u32[]{:S(2)}) %collective-permute-start.2) | collective-permute-done | bytes 163872 | tf_op jit(solution)/shard_map/ppermute | solution.py:27
  66.3 2.9 %collective-permute-done.4.other_ref = bf16[4,16,8,1280]{3,2,1,0:T(8,128)(2,1)S(1)} collective-permute-done((bf16[4,16,8,1280]{3,2,1,0:T(8,128)(2,1)S(1)}, bf16[4,16,8,1280]{3,2,1,0:T(8,128)(2,1)S(1)}, u32[]{:S(2)}, u32[]{:S(2)}) %collective-permute-start.4) | collective-permute-done | bytes 1310752 | tf_op jit(solution)/shard_map/ppermute | solution.py:27
  70.2 15.5 %main.1 = (bf16[512,512]{1,0:T(8,128)(2,1)}, bf16[512,512]{1,0:T(8,128)(2,1)}, bf16[1024,1024]{1,0:T(8,128)(2,1)S(1)}, bf16[1024,1280]{1,0:T(8,128)(2,1)S(1)}, b...) custom-call(s32[4]{0:T(128)S(1)} %fusion.12.start_ref, bf16[4,16,8,1280]{3,2,1,0:T(8,128)(2,1)S(1)} %bitcast.46, ...), custom_call_target="tpu_custom_call" | custom-call | flops 6442450944 | bytes 16777216 | tf_op jit(solution)/shard_map/main/pallas_call | solution.py:188
  92.1 6.0 %weights.1 = (bf16[8,40,1024]{2,1,0:T(8,128)(2,1)S(1)}, bf16[8,40,1024]{2,1,0:T(8,128)(2,1)S(1)}, bf16[4,40,1024]{2,1,0:T(8,128)(2,1)}, bf16[4,40,1024]{2,1,0:T(8,128)(2,1)S(1)}, bf16[8,40,1024]{2,1,0:T(8,128)(2,1)S(1)}) custom-call(s32[1]{0:T(128)} %bitcast.5.y_ref, bf16[1024,1280]{1,0:T(8,128)(2,1)S(1)} %copy-done.12, bf16[1024,1024]{1,0:T(8,128)(2,1)S(1)} %copy-done.14), custom_call_target="tpu_custom_call" | custom-call | flops 2684354560 | bytes 8388608 | tf_op jit(solution)/shard_map/weights/pallas_call | solution.py:220
  100.2 2.8 %collective-permute-start.8 = (bf16[8,8,1280]{2,1,0:T(8,128)(2,1)S(1)}, bf16[8,8,1280]{2,1,0:T(8,128)(2,1)S(1)}, u32[]{:S(2)}, u32[]{:S(2)}) collective-permute-start(bf16[8,8,1280]{2,1,0:T(8,128)(2,1)S(1)} %get-tuple-element.38), channel_id=1, source_target_pairs={{0,6},{2,0},{4,2},{6,4},{1,7},{3,1},{5,3},{7,5},{8,14},{10,8},{12,... | collective-permute-start | bytes 491528 | tf_op jit(solution)/shard_map/ppermute | solution.py:27
  103.6 4.1 %collective-permute-done.6 = bf16[8,8,1280]{2,1,0:T(8,128)(2,1)S(1)} collective-permute-done((bf16[8,8,1280]{2,1,0:T(8,128)(2,1)S(1)}, bf16[8,8,1280]{2,1,0:T(8,128)(2,1)S(1)}, u32[]{:S(2)}, u32[]{:S(2)}) %collective-permute-start.6) | collective-permute-done | bytes 163872 | tf_op jit(solution)/shard_map/ppermute | solution.py:27
  110.4 2.1 %collective-permute-start.9 = (bf16[16,8,1280]{2,1,0:T(8,128)(2,1)S(1)}, bf16[16,8,1280]{2,1,0:T(8,128)(2,1)S(1)}, u32[]{:S(2)}, u32[]{:S(2)}) collective-permute-start(bf16[16,8,1280]{2,1,0:T(8,128)(2,1)S(1)} %get-tuple-element.36), channel_id=1, source_target_pairs={{0,6},{2,0},{4,2},{6,4},{1,7},{3,1},{5,3},{7,5},{8,14},{10,8},{12,... | collective-permute-start | bytes 983048 | tf_op jit(solution)/shard_map/ppermute | solution.py:27
  112.5 2.3 %collective-permute-start.10 = (bf16[4,40,1024]{2,1,0:T(8,128)(2,1)}, bf16[4,40,1024]{2,1,0:T(8,128)(2,1)}, u32[]{:S(2)}, u32[]{:S(2)}) collective-permute-start(bf16[4,40,1024]{2,1,0:T(8,128)(2,1)} %get-tuple-element.32), channel_id=1, source_target_pairs={{0,8},{8,16},{16,24},{24,0},{1,9},{9,17},{17,25},{25,1},{2,10},{10... | collective-permute-start | bytes 983048 | tf_op jit(solution)/shard_map/ppermute | solution.py:27
  114.8 5.1 %collective-permute-done.7 = bf16[16,8,1280]{2,1,0:T(8,128)(2,1)S(1)} collective-permute-done((bf16[16,8,1280]{2,1,0:T(8,128)(2,1)S(1)}, bf16[16,8,1280]{2,1,0:T(8,128)(2,1)S(1)}, u32[]{:S(2)}, u32[]{:S(2)}) %collective-permute-start.7) | collective-permute-done | bytes 327712 | tf_op jit(solution)/shard_map/ppermute | solution.py:27
  119.9 1.9 fusion.3
  121.7 2.7 %gather_fusion.2 = bf16[64,8,1280]{2,1,0:T(8,128)(2,1)} fusion(bf16[16,8,1280]{2,1,0:T(8,128)(2,1)} %fusion.3, s32[1024]{0:T(1024)S(1)} %pad_clamp_fusion), kind=kCustom, calls=%fused_computation.2 | custom fusion | bytes 2621696 | tf_op jit(solution)/shard_map/gather | solution.py:258
  124.4 6.7 %all-to-all-start.1 = ((bf16[64,8,1280]{2,1,0:T(8,128)(2,1)}), bf16[64,8,1280]{2,1,0:T(8,128)(2,1)S(1)}, u32[]{:S(2)}, u32[]{:S(2)}) async-start(bf16[64,8,1280]{2,1,0:T(8,128)(2,1)} %gather_fusion.2), calls=%async_computation.1 | async-start | bytes 2621440 | tf_op jit(solution)/shard_map/all_to_all | solution.py:259
  131.4 2.1 %add_convert_fusion.2 = bf16[8,40,1024]{2,1,0:T(8,128)(2,1)} fusion(bf16[8,40,1024]{2,1,0:T(8,128)(2,1)} %copy-done.4, bf16[4,40,1024]{2,1,0:T(8,128)(2,1)} %collective-permute-done.10), kind=kLoop, calls=%fused_computation.5 | loop fusion | flops 1310720 | bytes 1638400 | tf_op jit(solution)/shard_map/convert_element_type | solution.py:250
  133.5 1.8 collective-permute-start.11
  135.3 10.3 %collective-permute-done.12 = bf16[4,40,1024]{2,1,0:T(8,128)(2,1)S(1)} collective-permute-done((bf16[4,40,1024]{2,1,0:T(8,128)(2,1)}, bf16[4,40,1024]{2,1,0:T(8,128)(2,1)S(1)}, u32[]{:S(2)}, u32[]{:S(2)}) %collective-permute-start.12) | collective-permute-done | bytes 327712 | tf_op jit(solution)/shard_map/ppermute | solution.py:27
  146.6 2.8 %collective-permute-start.13 = (bf16[8,40,1024]{2,1,0:T(8,128)(2,1)}, bf16[8,40,1024]{2,1,0:T(8,128)(2,1)}, u32[]{:S(2)}, u32[]{:S(2)}) collective-permute-start(bf16[8,40,1024]{2,1,0:T(8,128)(2,1)} %add_convert_fusion.1), channel_id=1, source_target_pairs={{0,24},{8,0},{16,8},{24,16},{1,25},{9,1},{17,9},{25,17},{2,26},{10... | collective-permute-start | bytes 1966088 | tf_op jit(solution)/shard_map/ppermute | solution.py:27
  149.4 11.3 %collective-permute-done.11 = bf16[8,40,1024]{2,1,0:T(8,128)(2,1)} collective-permute-done((bf16[8,40,1024]{2,1,0:T(8,128)(2,1)}, bf16[8,40,1024]{2,1,0:T(8,128)(2,1)}, u32[]{:S(2)}, u32[]{:S(2)}) %collective-permute-start.11) | collective-permute-done | bytes 655392 | tf_op jit(solution)/shard_map/ppermute | solution.py:27
  160.7 6.9 %collective-permute-done.13 = bf16[8,40,1024]{2,1,0:T(8,128)(2,1)} collective-permute-done((bf16[8,40,1024]{2,1,0:T(8,128)(2,1)}, bf16[8,40,1024]{2,1,0:T(8,128)(2,1)}, u32[]{:S(2)}, u32[]{:S(2)}) %collective-permute-start.13) | collective-permute-done | bytes 655392 | tf_op jit(solution)/shard_map/ppermute | solution.py:27
  167.6 1.8 add_convert_fusion
  170.9 2.1 %collective-permute-start.14 = (bf16[40,1024]{1,0:T(8,128)(2,1)S(1)}, bf16[40,1024]{1,0:T(8,128)(2,1)S(1)}, u32[]{:S(2)}, u32[]{:S(2)}) collective-permute-start(bf16[40,1024]{1,0:T(8,128)(2,1)S(1)} %get-tuple-element.39), channel_id=1, source_target_pairs={{0,32},{32,64},{64,96},{96,128},{128,160},{160,192},{192,224},{224... | collective-permute-start | bytes 245768 | tf_op jit(solution)/shard_map/ppermute | solution.py:27
  174.6 1.8 collective-permute-start.16
  176.4 2.3 %collective-permute-start.17 = (bf16[40,1024]{1,0:T(8,128)(2,1)}, bf16[40,1024]{1,0:T(8,128)(2,1)}, u32[]{:S(2)}, u32[]{:S(2)}) collective-permute-start(bf16[40,1024]{1,0:T(8,128)(2,1)} %get-tuple-element.43), channel_id=1, source_target_pairs={{0,192},{32,224},{64,0},{96,32},{128,64},{160,96},{192,128},{224,1... | collective-permute-start | bytes 245768 | tf_op jit(solution)/shard_map/ppermute | solution.py:27
  178.7 1.9 collective-permute-start.18
  180.6 3.1 %collective-permute-start.19 = (bf16[40,1024]{1,0:T(8,128)(2,1)S(1)}, bf16[40,1024]{1,0:T(8,128)(2,1)}, u32[]{:S(2)}, u32[]{:S(2)}) collective-permute-start(bf16[40,1024]{1,0:T(8,128)(2,1)S(1)} %get-tuple-element.41), channel_id=1, source_target_pairs={{0,160},{32,192},{64,224},{96,0},{128,32},{160,64},{192,96},{224,1... | collective-permute-start | bytes 245768 | tf_op jit(solution)/shard_map/ppermute | solution.py:27
  184.4 5.8 %collective-permute-start.20 = (bf16[40,1024]{1,0:T(8,128)(2,1)S(1)}, bf16[40,1024]{1,0:T(8,128)(2,1)}, u32[]{:S(2)}, u32[]{:S(2)}) collective-permute-start(bf16[40,1024]{1,0:T(8,128)(2,1)S(1)} %get-tuple-element.40), channel_id=1, source_target_pairs={{0,128},{32,160},{64,192},{96,224},{128,0},{160,32},{192,64},{224,... | collective-permute-start | bytes 245768 | tf_op jit(solution)/shard_map/ppermute | solution.py:27
  190.4 2.7 %collective-permute-done.20 = bf16[40,1024]{1,0:T(8,128)(2,1)} collective-permute-done((bf16[40,1024]{1,0:T(8,128)(2,1)S(1)}, bf16[40,1024]{1,0:T(8,128)(2,1)}, u32[]{:S(2)}, u32[]{:S(2)}) %collective-permute-start.20) | collective-permute-done | bytes 81952 | tf_op jit(solution)/shard_map/ppermute | solution.py:27
  195.1 2.3 %collect.1 = f32[12,8,1280]{2,1,0:T(8,128)} custom-call(s32[64]{0:T(128)S(1)} %reshape_squeeze.3.sent_ref, bf16[64,8,1280]{2,1,0:T(8,128)(2,1)S(1)} %all-to-all-done.1.got_ref), custom_call_target="tpu_custom_call" | custom-call | tf_op jit(solution)/shard_map/collect/pallas_call | solution.py:267
  (89 shorter events, 27.8 us)
Async XLA Ops:
  3.9 11.8 %copy-start.19 = (s32[1,16]{1,0:T(1,128)S(1)}, s32[1,16]{1,0:T(1,128)}, u32[]{:S(2)}) copy-start(s32[1,16]{1,0:T(1,128)} %param.12) | copy-start | bytes 196
  3.9 44.7 %all-to-all-start = ((bf16[64,8,1280]{2,1,0:T(8,128)(2,1)}), bf16[64,8,1280]{2,1,0:T(8,128)(2,1)S(1)}, u32[]{:S(2)}, u32[]{:S(2)}) async-start(bf16[64,8,1280]{2,1,0:T(8,128)(2,1)} %gather_fusion), calls=%async_computation | async-start | bytes 2621440 | tf_op jit(solution)/shard_map/all_to_all | solution.py:172
  49.9 9.4 %collective-permute-start = (bf16[16,8,1280]{2,1,0:T(8,128)(2,1)}, bf16[16,8,1280]{2,1,0:T(8,128)(2,1)S(1)}, u32[]{:S(2)}, u32[]{:S(2)}) collective-permute-start(bf16[16,8,1280]{2,1,0:T(8,128)(2,1)} %gather_fusion.1), channel_id=1, source_target_pairs={{0,2},{2,4},{4,6},{6,0},{1,3},{3,5},{5,7},{7,1},{8,10},{10,12},{12... | collective-permute-start | bytes 983048 | tf_op jit(solution)/shard_map/ppermute | solution.py:27
  51.4 8.3 %collective-permute-start.1 = (bf16[16,8,1280]{2,1,0:T(8,128)(2,1)}, bf16[16,8,1280]{2,1,0:T(8,128)(2,1)S(1)}, u32[]{:S(2)}, u32[]{:S(2)}) collective-permute-start(bf16[16,8,1280]{2,1,0:T(8,128)(2,1)} %gather_fusion.1), channel_id=1, source_target_pairs={{0,6},{2,0},{4,2},{6,4},{1,7},{3,1},{5,3},{7,5},{8,14},{10,8},{12,... | collective-permute-start | bytes 983048 | tf_op jit(solution)/shard_map/ppermute | solution.py:27
  53.2 16.0 %copy-start.8 = (bf16[512,512]{1,0:T(8,128)(2,1)S(1)}, bf16[512,512]{1,0:T(8,128)(2,1)}, u32[]{:S(2)}) copy-start(bf16[512,512]{1,0:T(8,128)(2,1)} %q_ref.1) | copy-start | bytes 1572868
  54.3 11.9 %copy-start.5 = (s32[512]{0:T(512)S(1)}, s32[512]{0:T(512)}, u32[]{:S(2)}) copy-start(s32[512]{0:T(512)} %param.14) | copy-start | bytes 6148
  54.3 14.9 %copy-start.6 = (bf16[1280,512]{1,0:T(8,128)(2,1)S(1)}, bf16[1280,512]{1,0:T(8,128)(2,1)}, u32[]{:S(2)}) copy-start(bf16[1280,512]{1,0:T(8,128)(2,1)} %wk_ref.1) | copy-start | bytes 3932164
  54.3 14.9 %copy-start.7 = (bf16[1280,512]{1,0:T(8,128)(2,1)S(1)}, bf16[1280,512]{1,0:T(8,128)(2,1)}, u32[]{:S(2)}) copy-start(bf16[1280,512]{1,0:T(8,128)(2,1)} %wv_ref.1) | copy-start | bytes 3932164
  59.4 6.6 %collective-permute-start.2 = (bf16[8,8,1280]{2,1,0:T(8,128)(2,1)S(1)}, bf16[8,8,1280]{2,1,0:T(8,128)(2,1)S(1)}, u32[]{:S(2)}, u32[]{:S(2)}) collective-permute-start(bf16[8,8,1280]{2,1,0:T(8,128)(2,1)S(1)} %slice.67), channel_id=1, source_target_pairs={{0,2},{2,4},{4,6},{6,0},{1,3},{3,5},{5,7},{7,1},{8,10},{10,12},{12... | collective-permute-start | bytes 491528 | tf_op jit(solution)/shard_map/ppermute | solution.py:27
  59.8 6.2 %collective-permute-start.3 = (bf16[8,8,1280]{2,1,0:T(8,128)(2,1)S(1)}, bf16[8,8,1280]{2,1,0:T(8,128)(2,1)S(1)}, u32[]{:S(2)}, u32[]{:S(2)}) collective-permute-start(bf16[8,8,1280]{2,1,0:T(8,128)(2,1)S(1)} %slice.68), channel_id=1, source_target_pairs={{0,6},{2,0},{4,2},{6,4},{1,7},{3,1},{5,3},{7,5},{8,14},{10,8},{12,... | collective-permute-start | bytes 491528 | tf_op jit(solution)/shard_map/ppermute | solution.py:27
  66.1 3.1 %collective-permute-start.4 = (bf16[4,16,8,1280]{3,2,1,0:T(8,128)(2,1)S(1)}, bf16[4,16,8,1280]{3,2,1,0:T(8,128)(2,1)S(1)}, u32[]{:S(2)}, u32[]{:S(2)}) collective-permute-start(bf16[4,16,8,1280]{3,2,1,0:T(8,128)(2,1)S(1)} %bitcast.45), channel_id=1, source_target_pairs={{0,1},{1,0},{2,3},{3,2},{4,5},{5,4},{6,7},{7,6},{8,9},{9,8},{10,11... | collective-permute-start | bytes 3932168 | tf_op jit(solution)/shard_map/ppermute | solution.py:27
  88.6 9.4 %collective-permute-start.5 = (bf16[4,16,8,1280]{3,2,1,0:T(8,128)(2,1)}, bf16[4,16,8,1280]{3,2,1,0:T(8,128)(2,1)}, u32[]{:S(2)}, u32[]{:S(2)}) collective-permute-start(bf16[4,16,8,1280]{3,2,1,0:T(8,128)(2,1)} %get-tuple-element.23), channel_id=1, source_target_pairs={{0,1},{1,0},{2,3},{3,2},{4,5},{5,4},{6,7},{7,6},{8,9},{9,8},{10,11... | collective-permute-start | bytes 3932168 | tf_op jit(solution)/shard_map/ppermute | solution.py:27
  98.0 10.9 %copy-start.4 = (bf16[8,40,1024]{2,1,0:T(8,128)(2,1)}, bf16[8,40,1024]{2,1,0:T(8,128)(2,1)S(1)}, u32[]{:S(2)}) copy-start(bf16[8,40,1024]{2,1,0:T(8,128)(2,1)S(1)} %get-tuple-element.31) | copy-start | bytes 1966084
  98.0 10.9 %copy-start.10 = (bf16[4,40,1024]{2,1,0:T(8,128)(2,1)}, bf16[4,40,1024]{2,1,0:T(8,128)(2,1)S(1)}, u32[]{:S(2)}) copy-start(bf16[4,40,1024]{2,1,0:T(8,128)(2,1)S(1)} %get-tuple-element.34) | copy-start | bytes 983044
  99.5 8.1 %collective-permute-start.6 = (bf16[8,8,1280]{2,1,0:T(8,128)(2,1)S(1)}, bf16[8,8,1280]{2,1,0:T(8,128)(2,1)S(1)}, u32[]{:S(2)}, u32[]{:S(2)}) collective-permute-start(bf16[8,8,1280]{2,1,0:T(8,128)(2,1)S(1)} %get-tuple-element.37), channel_id=1, source_target_pairs={{0,2},{2,4},{4,6},{6,0},{1,3},{3,5},{5,7},{7,1},{8,10},{10,12},{12... | collective-permute-start | bytes 491528 | tf_op jit(solution)/shard_map/ppermute | solution.py:27
  100.2 7.4 %collective-permute-start.8 = (bf16[8,8,1280]{2,1,0:T(8,128)(2,1)S(1)}, bf16[8,8,1280]{2,1,0:T(8,128)(2,1)S(1)}, u32[]{:S(2)}, u32[]{:S(2)}) collective-permute-start(bf16[8,8,1280]{2,1,0:T(8,128)(2,1)S(1)} %get-tuple-element.38), channel_id=1, source_target_pairs={{0,6},{2,0},{4,2},{6,4},{1,7},{3,1},{5,3},{7,5},{8,14},{10,8},{12,... | collective-permute-start | bytes 491528 | tf_op jit(solution)/shard_map/ppermute | solution.py:27
  109.0 10.9 %collective-permute-start.7 = (bf16[16,8,1280]{2,1,0:T(8,128)(2,1)S(1)}, bf16[16,8,1280]{2,1,0:T(8,128)(2,1)S(1)}, u32[]{:S(2)}, u32[]{:S(2)}) collective-permute-start(bf16[16,8,1280]{2,1,0:T(8,128)(2,1)S(1)} %get-tuple-element.35), channel_id=1, source_target_pairs={{0,2},{2,4},{4,6},{6,0},{1,3},{3,5},{5,7},{7,1},{8,10},{10,12},{12... | collective-permute-start | bytes 983048 | tf_op jit(solution)/shard_map/ppermute | solution.py:27
  110.4 9.5 %collective-permute-start.9 = (bf16[16,8,1280]{2,1,0:T(8,128)(2,1)S(1)}, bf16[16,8,1280]{2,1,0:T(8,128)(2,1)S(1)}, u32[]{:S(2)}, u32[]{:S(2)}) collective-permute-start(bf16[16,8,1280]{2,1,0:T(8,128)(2,1)S(1)} %get-tuple-element.36), channel_id=1, source_target_pairs={{0,6},{2,0},{4,2},{6,4},{1,7},{3,1},{5,3},{7,5},{8,14},{10,8},{12,... | collective-permute-start | bytes 983048 | tf_op jit(solution)/shard_map/ppermute | solution.py:27
  112.5 18.9 %collective-permute-start.10 = (bf16[4,40,1024]{2,1,0:T(8,128)(2,1)}, bf16[4,40,1024]{2,1,0:T(8,128)(2,1)}, u32[]{:S(2)}, u32[]{:S(2)}) collective-permute-start(bf16[4,40,1024]{2,1,0:T(8,128)(2,1)} %get-tuple-element.32), channel_id=1, source_target_pairs={{0,8},{8,16},{16,24},{24,0},{1,9},{9,17},{17,25},{25,1},{2,10},{10... | collective-permute-start | bytes 983048 | tf_op jit(solution)/shard_map/ppermute | solution.py:27
  124.4 70.7 %all-to-all-start.1 = ((bf16[64,8,1280]{2,1,0:T(8,128)(2,1)}), bf16[64,8,1280]{2,1,0:T(8,128)(2,1)S(1)}, u32[]{:S(2)}, u32[]{:S(2)}) async-start(bf16[64,8,1280]{2,1,0:T(8,128)(2,1)} %gather_fusion.2), calls=%async_computation.1 | async-start | bytes 2621440 | tf_op jit(solution)/shard_map/all_to_all | solution.py:259
  131.1 14.6 %copy-start.3 = (bf16[8,40,1024]{2,1,0:T(8,128)(2,1)S(1)}, bf16[8,40,1024]{2,1,0:T(8,128)(2,1)}, u32[]{:S(2)}) copy-start(bf16[8,40,1024]{2,1,0:T(8,128)(2,1)} %copy-done.2) | copy-start | bytes 1966084
  131.1 14.6 %collective-permute-start.12 = (bf16[4,40,1024]{2,1,0:T(8,128)(2,1)}, bf16[4,40,1024]{2,1,0:T(8,128)(2,1)S(1)}, u32[]{:S(2)}, u32[]{:S(2)}) collective-permute-start(bf16[4,40,1024]{2,1,0:T(8,128)(2,1)} %copy-done.10), channel_id=1, source_target_pairs={{0,24},{8,0},{16,8},{24,16},{1,25},{9,1},{17,9},{25,17},{2,26},{10... | collective-permute-start | bytes 983048 | tf_op jit(solution)/shard_map/ppermute | solution.py:27
  133.5 27.2 %collective-permute-start.11 = (bf16[8,40,1024]{2,1,0:T(8,128)(2,1)}, bf16[8,40,1024]{2,1,0:T(8,128)(2,1)}, u32[]{:S(2)}, u32[]{:S(2)}) collective-permute-start(bf16[8,40,1024]{2,1,0:T(8,128)(2,1)} %add_convert_fusion.2), channel_id=1, source_target_pairs={{0,8},{8,16},{16,24},{24,0},{1,9},{9,17},{17,25},{25,1},{2,10},{10... | collective-permute-start | bytes 1966088 | tf_op jit(solution)/shard_map/ppermute | solution.py:27
  146.6 20.9 %collective-permute-start.13 = (bf16[8,40,1024]{2,1,0:T(8,128)(2,1)}, bf16[8,40,1024]{2,1,0:T(8,128)(2,1)}, u32[]{:S(2)}, u32[]{:S(2)}) collective-permute-start(bf16[8,40,1024]{2,1,0:T(8,128)(2,1)} %add_convert_fusion.1), channel_id=1, source_target_pairs={{0,24},{8,0},{16,8},{24,16},{1,25},{9,1},{17,9},{25,17},{2,26},{10... | collective-permute-start | bytes 1966088 | tf_op jit(solution)/shard_map/ppermute | solution.py:27
  167.6 22.6 %copy-start.18 = (s32[1,32,2]{1,2,0:T(2,128)S(1)}, s32[1,32,2]{1,2,0:T(2,128)}, u32[]{:S(2)}) copy-start(s32[1,32,2]{1,2,0:T(2,128)} %param.13) | copy-start | bytes 772
  170.9 9.7 %collective-permute-start.14 = (bf16[40,1024]{1,0:T(8,128)(2,1)S(1)}, bf16[40,1024]{1,0:T(8,128)(2,1)S(1)}, u32[]{:S(2)}, u32[]{:S(2)}) collective-permute-start(bf16[40,1024]{1,0:T(8,128)(2,1)S(1)} %get-tuple-element.39), channel_id=1, source_target_pairs={{0,32},{32,64},{64,96},{96,128},{128,160},{160,192},{192,224},{224... | collective-permute-start | bytes 245768 | tf_op jit(solution)/shard_map/ppermute | solution.py:27
  173.1 10.7 %collective-permute-start.15 = (bf16[40,1024]{1,0:T(8,128)(2,1)S(1)}, bf16[40,1024]{1,0:T(8,128)(2,1)S(1)}, u32[]{:S(2)}, u32[]{:S(2)}) collective-permute-start(bf16[40,1024]{1,0:T(8,128)(2,1)S(1)} %get-tuple-element.45), channel_id=1, source_target_pairs={{0,224},{32,0},{64,32},{96,64},{128,96},{160,128},{192,160},{224,1... | collective-permute-start | bytes 245768 | tf_op jit(solution)/shard_map/ppermute | solution.py:27
  174.6 15.8 %collective-permute-start.16 = (bf16[40,1024]{1,0:T(8,128)(2,1)}, bf16[40,1024]{1,0:T(8,128)(2,1)}, u32[]{:S(2)}, u32[]{:S(2)}) collective-permute-start(bf16[40,1024]{1,0:T(8,128)(2,1)} %get-tuple-element.44), channel_id=1, source_target_pairs={{0,64},{32,96},{64,128},{96,160},{128,192},{160,224},{192,0},{224,... | collective-permute-start | bytes 245768 | tf_op jit(solution)/shard_map/ppermute | solution.py:27
  176.4 14.0 %collective-permute-start.17 = (bf16[40,1024]{1,0:T(8,128)(2,1)}, bf16[40,1024]{1,0:T(8,128)(2,1)}, u32[]{:S(2)}, u32[]{:S(2)}) collective-permute-start(bf16[40,1024]{1,0:T(8,128)(2,1)} %get-tuple-element.43), channel_id=1, source_target_pairs={{0,192},{32,224},{64,0},{96,32},{128,64},{160,96},{192,128},{224,1... | collective-permute-start | bytes 245768 | tf_op jit(solution)/shard_map/ppermute | solution.py:27
  178.7 11.7 %collective-permute-start.18 = (bf16[40,1024]{1,0:T(8,128)(2,1)S(1)}, bf16[40,1024]{1,0:T(8,128)(2,1)}, u32[]{:S(2)}, u32[]{:S(2)}) collective-permute-start(bf16[40,1024]{1,0:T(8,128)(2,1)S(1)} %get-tuple-element.42), channel_id=1, source_target_pairs={{0,96},{32,128},{64,160},{96,192},{128,224},{160,0},{192,32},{224,... | collective-permute-start | bytes 245768 | tf_op jit(solution)/shard_map/ppermute | solution.py:27
  180.6 9.8 %collective-permute-start.19 = (bf16[40,1024]{1,0:T(8,128)(2,1)S(1)}, bf16[40,1024]{1,0:T(8,128)(2,1)}, u32[]{:S(2)}, u32[]{:S(2)}) collective-permute-start(bf16[40,1024]{1,0:T(8,128)(2,1)S(1)} %get-tuple-element.41), channel_id=1, source_target_pairs={{0,160},{32,192},{64,224},{96,0},{128,32},{160,64},{192,96},{224,1... | collective-permute-start | bytes 245768 | tf_op jit(solution)/shard_map/ppermute | solution.py:27
  184.4 8.7 %collective-permute-start.20 = (bf16[40,1024]{1,0:T(8,128)(2,1)S(1)}, bf16[40,1024]{1,0:T(8,128)(2,1)}, u32[]{:S(2)}, u32[]{:S(2)}) collective-permute-start(bf16[40,1024]{1,0:T(8,128)(2,1)S(1)} %get-tuple-element.40), channel_id=1, source_target_pairs={{0,128},{32,160},{64,192},{96,224},{128,0},{160,32},{192,64},{224,... | collective-permute-start | bytes 245768 | tf_op jit(solution)/shard_map/ppermute | solution.py:27
  (11 other events, 35.2 us)

commit v3 on v2

--- a/solution.py
+++ b/solution.py
@@ -10,6 +10,7 @@
 GAP = 32
 WIN = 4
 SUB = 8
+OFFSETS = (0, 3, 1, 2)
 NEG_FILL = -1e30
 BF = jnp.bfloat16
 F32 = jnp.float32
@@ -43,10 +44,16 @@
     return pl.BlockSpec(memory_space=pltpu.SMEM)
 
 
+def spread_kernel(sent_ref, me_ref, lat_ref, out_ref):
+    @pl.loop(0, out_ref.shape[0], unroll=4)
+    def _(e):
+        out_ref[e] = lat_ref[jnp.maximum(sent_ref[e], 0)]
+
+
 def main_kernel(
-    start_ref, mine_ref, other_ref, wk_ref, wv_ref, q_ref, g_ref, slot_ref,
-    att_ref, dq_ref, bg_ref, lat_ref, keep_ref, give_ref,
-    k_ref, v_ref, acc_ref,
+    start_ref, pos_ref, mine_ref, other_ref, wk_ref, wv_ref, q_ref, g_ref, slot_ref,
+    att_ref, dq_ref, keep_ref, give_ref, own_ref, next_ref, fa_ref, fb_ref, prev_ref,
+    lat_ref, k_ref, v_ref, acc_ref, bg_ref, t_ref, sum_ref,
 ):
     vis = mine_ref.shape[1]
     rows = 2 * mine_ref.shape[0] * SUB
@@ -54,6 +61,9 @@
     cols = wk_ref.shape[1]
     heads = cols // DH
     chunk = WIN * rows
+    nx = mine_ref.shape[0]
+    my_x = pos_ref[0]
+    my_y = pos_ref[1]
 
     @pl.loop(0, vis // WIN)
     def _(i):
@@ -108,27 +118,26 @@
         out = mm(grad[:, :cols], wk_ref[...], NT) + mm(grad[:, cols:], wv_ref[...], NT)
         for s in range(WIN):
             piece = out[s * rows:(s + 1) * rows].reshape(rows // SUB, SUB, width).astype(BF)
-            keep_ref[:, i * WIN + s] = piece[:rows // SUB // 2]
-            give_ref[:, i * WIN + s] = piece[rows // SUB // 2:]
-
-
-def weight_kernel(y_ref, lat_ref, bg_ref, own_ref, next_ref, fa_ref, fb_ref, prev_ref, t_ref, sum_ref):
-    nz, part, cols = own_ref.shape
-    ny = lat_ref.shape[1] // (nz * part)
+            for r, off in enumerate(OFFSETS):
+                there = lax.rem(my_x + off, nx)
+                keep_ref[there, i * WIN + s] = piece[r]
+                give_ref[there, i * WIN + s] = piece[nx + r]
+
+    nz, part, _ = own_ref.shape
+    ny = width // (nz * part)
     half = t_ref.shape[0]
     step = 256
     zh = nz // 2
-    me = y_ref[0]
-    for j in range(lat_ref.shape[1] // half):
+    for j in range(width // half):
         t_ref[...] = lat_ref[:, j * half:(j + 1) * half].T
 
-        @pl.loop(0, cols // step)
+        @pl.loop(0, 2 * cols // step)
         def _(n):
             at = pl.ds(pl.multiple_of(n * step, step), step)
             sum_ref[j * half:(j + 1) * half, at] = mm(t_ref[...], bg_ref[:, at], NN)
 
     def block(z, rel):
-        there = lax.rem(me + rel, ny)
+        there = lax.rem(my_y + rel, ny)
         return sum_ref[pl.ds(pl.multiple_of((z * ny + there) * part, SUB), part), :].astype(BF)
 
     for z in range(nz):
@@ -139,6 +148,19 @@
             fa_ref[z] = block(z, 2)
         else:
             fb_ref[z - zh] = block(z, 2)
+
+
+def pack_kernel(place_ref, got_ref, out_ref):
+    total = got_ref[0].astype(F32)
+    for r in range(1, got_ref.shape[0]):
+        total = total + got_ref[r].astype(F32)
+    total = total.astype(BF)
+    for v in range(total.shape[0]):
+        place = place_ref[v]
+
+        @pl.when(place >= 0)
+        def _():
+            out_ref[place] = total[v]
 
 
 def collect_kernel(sent_ref, got_ref, out_ref):
@@ -163,12 +185,21 @@
     sent = outbound[0].reshape(-1)
     places = visible[0]
     slots_total = sent.shape[0]
-    row_groups = lat_rows // SUB
     part = width // (nz * ny)
 
-    me = lax.axis_index(head)
-    pick = jnp.maximum(sent, 0) * row_groups + me
-    send = latents.reshape(images * row_groups, SUB, width)[pick]
+    me = lax.axis_index(head).reshape(1).astype(jnp.int32)
+    send = pl.pallas_call(
+        spread_kernel,
+        name="spread",
+        grid_spec=pltpu.PrefetchScalarGridSpec(
+            num_scalar_prefetch=2,
+            grid=(1,),
+            in_specs=[pl.BlockSpec((images, SUB, width), lambda i, a, b: (0, b[0], 0))],
+            out_specs=pl.BlockSpec((slots_total, SUB, width), lambda i, a, b: (0, 0, 0)),
+        ),
+        out_shape=jax.ShapeDtypeStruct((slots_total, SUB, width), BF),
+        compiler_params=grant(8),
+    )(sent, me, latents)
     got = lax.all_to_all(send, seq, split_axis=0, concat_axis=0, tiled=True)
     own = got[jnp.maximum(places, 0)]
 
@@ -185,66 +216,39 @@
     slot_rows = token_slot.reshape(windows, 1, span)
     start = jnp.minimum(jnp.maximum(slot_rows[:, 0, 0], 0), vis - WIN)
     keys = vis * lat_rows
-    att, dq, bg, lat_all, keep, give = pl.pallas_call(
+    zh = nz // 2
+    here = jnp.stack([lax.axis_index("x"), lax.axis_index("y")]).astype(jnp.int32)
+    tokens_out = jax.ShapeDtypeStruct((tokens, cols), BF)
+    rows_out = jax.ShapeDtypeStruct((nx, vis, SUB, width), BF)
+    full = jax.ShapeDtypeStruct((nz, part, 2 * cols), BF)
+    split = jax.ShapeDtypeStruct((zh, part, 2 * cols), BF)
+    att, dq, keep, give, gw_own, gw_next, gw_fa, gw_fb, gw_prev = pl.pallas_call(
         main_kernel,
         name="main",
-        out_shape=(
-            jax.ShapeDtypeStruct((tokens, cols), BF),
-            jax.ShapeDtypeStruct((tokens, cols), BF),
-            jax.ShapeDtypeStruct((keys, 2 * cols), BF),
-            jax.ShapeDtypeStruct((keys, width), BF),
-            jax.ShapeDtypeStruct((nx, vis, SUB, width), BF),
-            jax.ShapeDtypeStruct((nx, vis, SUB, width), BF),
-        ),
-        in_specs=[smem()] + [vmem()] * 7,
-        out_specs=tuple([vmem()] * 6),
+        out_shape=(tokens_out, tokens_out, rows_out, rows_out, full, full, split, split, full),
+        in_specs=[smem(), smem()] + [vmem()] * 7,
+        out_specs=tuple([vmem()] * 9),
         scratch_shapes=[
+            pltpu.VMEM((keys, width), BF),
             pltpu.VMEM((keys, cols), BF),
             pltpu.VMEM((keys, cols), BF),
             pltpu.VMEM((keys, 2 * cols), F32),
+            pltpu.VMEM((keys, 2 * cols), BF),
+            pltpu.VMEM((width // 2, keys), BF),
+            pltpu.VMEM((width, 2 * cols), F32),
         ],
-        compiler_params=grant(32),
+        compiler_params=grant(26),
         cost_estimate=pl.CostEstimate(
-            flops=8 * keys * width * cols + 16 * keys * span * cols,
+            flops=12 * keys * width * cols + 16 * keys * span * cols,
             bytes_accessed=16 * 1024 * 1024,
             transcendentals=tokens * 4 * 256,
         ),
-    )(start, mine, other, key_weight, value_weight, queries, grad_out, slot_rows)
+    )(start, here, mine, other, key_weight, value_weight, queries, grad_out, slot_rows)
 
     swapped = shift(give, "core", 1, 2)
-
-    y_here = lax.axis_index("y")
-    zh = nz // 2
-    full = jax.ShapeDtypeStruct((nz, part, 2 * cols), BF)
-    split = jax.ShapeDtypeStruct((zh, part, 2 * cols), BF)
-    gw_own, gw_next, gw_fa, gw_fb, gw_prev = pl.pallas_call(
-        weight_kernel,
-        name="weights",
-        out_shape=(full, full, split, split, full),
-        in_specs=[smem(), vmem(), vmem()],
-        out_specs=tuple([vmem()] * 5),
-        scratch_shapes=[pltpu.VMEM((width // 2, keys), BF), pltpu.VMEM((width, 2 * cols), F32)],
-        compiler_params=grant(24),
-        cost_estimate=pl.CostEstimate(
-            flops=4 * keys * width * cols, bytes_accessed=8 * 1024 * 1024, transcendentals=0
-        ),
-    )(y_here.reshape(1).astype(jnp.int32), lat_all, bg)
-
-    swapped, gw_fa, gw_fb = lax.optimization_barrier((swapped, gw_fa, gw_fb))
     gw_up = shift(gw_fa, "y", 1, ny)
     gw_down = shift(gw_fb, "y", -1, ny)
-
-    up = shift(add2(keep[3, :half], swapped[3, :half]), "x", 1, nx)
-    down = shift(add2(keep[3, half:], swapped[3, half:]), "x", -1, nx)
-    to_right = (keep[2].astype(F32) + swapped[2].astype(F32)
-                + jnp.concatenate([up, jnp.zeros_like(up)], axis=0).astype(F32)).astype(BF)
-    to_left = (keep[1].astype(F32) + swapped[1].astype(F32)
-               + jnp.concatenate([jnp.zeros_like(down), down], axis=0).astype(F32)).astype(BF)
-    from_left = shift(to_right, "x", 1, nx)
-    from_right = shift(to_left, "x", -1, nx)
-    dl_mine = (
-        keep[0].astype(F32) + swapped[0].astype(F32) + from_left.astype(F32) + from_right.astype(F32)
-    ).astype(BF)
+    crossed = lax.all_to_all(add2(keep, swapped), "x", split_axis=0, concat_axis=0, tiled=True)
 
     gw_next = (gw_next.astype(F32)
                + jnp.concatenate([gw_up, jnp.zeros_like(gw_up)], axis=0).astype(F32)).astype(BF)
@@ -254,15 +258,22 @@
     gw_r = shift(gw_prev, "y", -1, ny)
     gw_y = (gw_own.astype(F32) + gw_l.astype(F32) + gw_r.astype(F32)).astype(BF)
 
-    hits = places[None, :] == jnp.arange(slots_total, dtype=jnp.int32)[:, None]
-    back = dl_mine[jnp.argmax(hits, axis=1)]
+    back = pl.pallas_call(
+        pack_kernel,
+        name="pack",
+        out_shape=jax.ShapeDtypeStruct((slots_total, SUB, width), BF),
+        in_specs=[smem(), vmem()],
+        out_specs=vmem(),
+        compiler_params=grant(8),
+    )(places, crossed)
     returned = lax.all_to_all(back, seq, split_axis=0, concat_axis=0, tiled=True)
 
     z_here = lax.axis_index("z")
     weights = lax.dynamic_index_in_dim(gw_y, z_here, 0, False).astype(F32)
-    for step in (1, -1, 2, -2, 3, -3, 4):
+    arrived = []
+    for step in (4, 3, -3, 2, -2, 1, -1):
         piece = lax.dynamic_index_in_dim(gw_y, lax.rem(z_here + step + nz, nz), 0, False)
-        weights = weights + shift(piece, "z", step, nz).astype(F32)
+        arrived.append(shift(piece, "z", step, nz))
 
     grad_latents = pl.pallas_call(
         collect_kernel,
@@ -272,6 +283,9 @@
         out_specs=vmem(),
         compiler_params=grant(8),
     )(sent, returned)
+    arrived, grad_latents = lax.optimization_barrier((arrived, grad_latents))
+    for piece in arrived:
+        weights = weights + piece.astype(F32)
     return att, dq, grad_latents, weights[:, :cols], weights[:, cols:]
 
 

time: 200 us -> 196 us (0.980)
  blocking collectives: 0 us -> 22.6 us
  starting transfers between devices: 58.1 us -> 49.4 us
  other arithmetic: 12.4 us -> 4.04 us
  local copies, waits for them, and re-layouts: 17.8 us -> 10.9 us
  waiting for transfers between devices: 84.4 us -> 78.3 us
  Pallas kernels: 23.8 us -> 26.6 us
    all_to_all x0 -> x1, blocking collectives: none -> 22.6 us  [local(): lax.all_to_all(add2(keep, swapped), 'x', split_axis=0, concat_axis=0, til...]
    ppermute x21 -> x17, starting transfers between devices: 39.6 us -> 30.9 us  [shift(): return lax.ppermute(v, axis, [(i, (i + step) % size) for i in range(size)])]
    ppermute x21 -> x17, waiting for transfers between devices: 51.5 us -> 45.4 us  [shift(): return lax.ppermute(v, axis, [(i, (i + step) % size) for i in range(size)])]
    gather x2 -> x0, local copies, waits for them, and re-layouts: 4.38 us -> none  [the longest x1 2.68 us: local(): back = dl_mine[jnp.argmax(hits, axis=1)]]
    convert_element_type x2 -> x0, other arithmetic: 3.12 us -> none  [the longest x1 1.86 us: local(): dl_mine = (keep[0].astype(F32) + swapped[0].astype(F32) + from_left.astyp...]
    pallas_call x2 -> x3, Pallas kernels: 21.5 us -> 24.3 us  [the longest x1 20.5 us: local(): pl.pallas_call(main_kernel, name='main', out_shape=(tokens_out, tokens_ou...]
    unnamed x45 -> x27, local copies, waits for them, and re-layouts: 10.4 us -> 9.51 us
  transfers between devices with their start and end apart: 23 -> 19, of which waited for: 10 -> 9; matrix products, arithmetic and copies ran while one was open for 7% -> 2% of each run, Pallas kernels for 3% -> 1%
where the time goes in v3:
time: 196 us; the launch traced here: 193 us
  waiting for transfers between devices  78.3 us (40%)
  starting transfers between devices  49.4 us (25%)
  Pallas kernels  26.6 us (14%)
  blocking collectives  22.6 us (12%)
  local copies, waits for them, and re-layouts  10.9 us (6%)
  other arithmetic  4.04 us (2%)
    ppermute x17, waiting for transfers between devices, shift(): return lax.ppermute(v, axis, [(i, (i + step) % size) for i in range(size)])  45.4 us
    all_to_all x1, waiting for transfers between devices, local(): got = lax.all_to_all(send, seq, split_axis=0, concat_axis=0, tiled=True)  32.9 us
    ppermute x17, starting transfers between devices, shift(): return lax.ppermute(v, axis, [(i, (i + step) % size) for i in range(size)])  30.9 us
    all_to_all x1, blocking collectives, local(): lax.all_to_all(add2(keep, swapped), 'x', split_axis=0, concat_axis=0, til...  22.6 us
    pallas_call x1, Pallas kernels, local(): pl.pallas_call(main_kernel, name='main', out_shape=(tokens_out, tokens_ou...  20.5 us
    all_to_all x1, starting transfers between devices, local(): got = lax.all_to_all(send, seq, split_axis=0, concat_axis=0, tiled=True)  11.8 us
    unnamed x27, local copies, waits for them, and re-layouts  9.51 us
    all_to_all x1, starting transfers between devices, local(): lax.all_to_all(back, seq, split_axis=0, concat_axis=0, tiled=True)  6.72 us
  transfers between devices with their start and end apart: 19, of which 9 were waited for; matrix products, arithmetic and copies ran while one was open for 2% of the time, Pallas kernels for 1%

profile of v3, /device:TPU:8, one launch (start us, length us, event | category | flops | bytes accessed | tf_op | source)
XLA Modules:
  0.0 192.7 jit_solution(10774387492647854144)
XLA Ops:
  1.5 1.5 copy-done
  3.1 1.8 spread.1
  4.9 11.8 %all-to-all-start = ((bf16[64,8,1280]{2,1,0:T(8,128)(2,1)}), bf16[64,8,1280]{2,1,0:T(8,128)(2,1)S(1)}, u32[]{:S(2)}, u32[]{:S(2)}) async-start(bf16[64,8,1280]{2,1,0:T(8,128)(2,1)} %spread.1), calls=%async_computation | async-start | bytes 2621440 | tf_op jit(solution)/shard_map/all_to_all | solution.py:203
  16.8 32.9 %all-to-all-done = bf16[64,8,1280]{2,1,0:T(8,128)(2,1)S(1)} async-done(((bf16[64,8,1280]{2,1,0:T(8,128)(2,1)}), bf16[64,8,1280]{2,1,0:T(8,128)(2,1)S(1)}, u32[]{:S(2)}, u32[]{:S(2)}) %all-to-all-start) | async-done | bytes 1310752 | tf_op jit(solution)/shard_map/all_to_all | solution.py:203
  50.2 1.6 collective-permute-start
  51.8 1.7 collective-permute-start.1
  53.6 6.0 %collective-permute-done = bf16[16,8,1280]{2,1,0:T(8,128)(2,1)S(1)} collective-permute-done((bf16[16,8,1280]{2,1,0:T(8,128)(2,1)S(1)}, bf16[16,8,1280]{2,1,0:T(8,128)(2,1)S(1)}, u32[]{:S(2)}, u32[]{:S(2)}) %collective-permute-start) | collective-permute-done | bytes 327712 | tf_op jit(solution)/shard_map/ppermute | solution.py:28
  59.9 3.0 %collective-permute-start.3 = (bf16[8,8,1280]{2,1,0:T(8,128)(2,1)S(1)}, bf16[8,8,1280]{2,1,0:T(8,128)(2,1)S(1)}, u32[]{:S(2)}, u32[]{:S(2)}) collective-permute-start(bf16[8,8,1280]{2,1,0:T(8,128)(2,1)S(1)} %slice.24), channel_id=1, source_target_pairs={{0,6},{2,0},{4,2},{6,4},{1,7},{3,1},{5,3},{7,5},{8,14},{10,8},{12,... | collective-permute-start | bytes 491528 | tf_op jit(solution)/shard_map/ppermute | solution.py:28
  63.0 3.1 %collective-permute-done.2 = bf16[8,8,1280]{2,1,0:T(8,128)(2,1)S(1)} collective-permute-done((bf16[8,8,1280]{2,1,0:T(8,128)(2,1)S(1)}, bf16[8,8,1280]{2,1,0:T(8,128)(2,1)S(1)}, u32[]{:S(2)}, u32[]{:S(2)}) %collective-permute-start.2) | collective-permute-done | bytes 163872 | tf_op jit(solution)/shard_map/ppermute | solution.py:28
  66.5 2.8 %collective-permute-done.4.other_ref = bf16[4,16,8,1280]{3,2,1,0:T(8,128)(2,1)S(1)} collective-permute-done((bf16[4,16,8,1280]{3,2,1,0:T(8,128)(2,1)S(1)}, bf16[4,16,8,1280]{3,2,1,0:T(8,128)(2,1)S(1)}, u32[]{:S(2)}, u32[]{:S(2)}) %collective-permute-start.4) | collective-permute-done | bytes 1310752 | tf_op jit(solution)/shard_map/ppermute | solution.py:28
  70.4 1.3 copy-done.3
  71.7 1.3 copy-done.4
  73.0 1.3 copy-done.6
  76.4 20.5 %main.1 = (bf16[512,512]{1,0:T(8,128)(2,1)}, bf16[512,512]{1,0:T(8,128)(2,1)}, bf16[4,16,8,1280]{3,2,1,0:T(8,128)(2,1)S(1)}, bf16[4,16,8,1280]{3,2,1,0:T(8,128)(...) custom-call(s32[4]{0:T(128)S(1)} %fusion.6.start_ref, ...), custom_call_target="tpu_custom_call" | custom-call | flops 9126805504 | bytes 16777216 | tf_op jit(solution)/shard_map/main/pallas_call | solution.py:225
  97.1 2.9 %collective-permute-done.16 = bf16[4,16,8,1280]{3,2,1,0:T(8,128)(2,1)S(1)} collective-permute-done((bf16[4,16,8,1280]{3,2,1,0:T(8,128)(2,1)S(1)}, bf16[4,16,8,1280]{3,2,1,0:T(8,128)(2,1)S(1)}, u32[]{:S(2)}, u32[]{:S(2)}) %collective-permute-start.16) | collective-permute-done | bytes 1310752 | tf_op jit(solution)/shard_map/ppermute | solution.py:28
  100.3 22.6 %all_to_all.15.got_ref = bf16[4,16,8,1280]{3,2,1,0:T(8,128)(2,1)S(1)} all-to-all(bf16[4,16,8,1280]{3,2,1,0:T(8,128)(2,1)S(1)} %add_convert_fusion), channel_id=1, replica_groups=mesh['z'=8,'y'=4,'x'=4,'core'=2] {'x'}, dimensions={0} | all-to-all | bytes 2621440 | tf_op jit(solution)/shard_map/all_to_all | solution.py:251
  122.9 2.0 %pack.1 = bf16[64,8,1280]{2,1,0:T(8,128)(2,1)} custom-call(s32[16]{0:T(128)S(1)} %bitcast.29, bf16[4,16,8,1280]{3,2,1,0:T(8,128)(2,1)S(1)} %all_to_all.15.got_ref), custom_call_target="tpu_custom_call" | custom-call | tf_op jit(solution)/shard_map/pack/pallas_call | solution.py:261
  124.9 6.7 %all-to-all-start.2 = ((bf16[64,8,1280]{2,1,0:T(8,128)(2,1)}), bf16[64,8,1280]{2,1,0:T(8,128)(2,1)S(1)}, u32[]{:S(2)}, u32[]{:S(2)}) async-start(bf16[64,8,1280]{2,1,0:T(8,128)(2,1)} %pack.1), calls=%async_computation.2 | async-start | bytes 2621440 | tf_op jit(solution)/shard_map/all_to_all | solution.py:269
  131.6 1.5 collective-permute-start.5
  133.8 12.1 %collective-permute-done.5 = bf16[4,40,1024]{2,1,0:T(8,128)(2,1)S(1)} collective-permute-done((bf16[4,40,1024]{2,1,0:T(8,128)(2,1)}, bf16[4,40,1024]{2,1,0:T(8,128)(2,1)S(1)}, u32[]{:S(2)}, u32[]{:S(2)}) %collective-permute-start.5) | collective-permute-done | bytes 327712 | tf_op jit(solution)/shard_map/ppermute | solution.py:28
  146.8 1.5 collective-permute-start.6
  149.2 1.6 collective-permute-start.8
  150.8 16.2 %collective-permute-done.6 = bf16[8,40,1024]{2,1,0:T(8,128)(2,1)S(1)} collective-permute-done((bf16[8,40,1024]{2,1,0:T(8,128)(2,1)}, bf16[8,40,1024]{2,1,0:T(8,128)(2,1)S(1)}, u32[]{:S(2)}, u32[]{:S(2)}) %collective-permute-start.6) | collective-permute-done | bytes 655392 | tf_op jit(solution)/shard_map/ppermute | solution.py:28
  167.0 1.8 collective-permute-done.8
  168.8 1.4 add_convert_fusion.1
  170.3 4.2 %collective-permute-start.10 = (bf16[40,1024]{1,0:T(8,128)(2,1)S(1)}, bf16[40,1024]{1,0:T(8,128)(2,1)S(1)}, u32[]{:S(2)}, u32[]{:S(2)}) collective-permute-start(bf16[40,1024]{1,0:T(8,128)(2,1)S(1)} %get-tuple-element.44), channel_id=1, source_target_pairs={{0,96},{32,128},{64,160},{96,192},{128,224},{160,0},{192,32},{224,... | collective-permute-start | bytes 245768 | tf_op jit(solution)/shard_map/ppermute | solution.py:28
  174.5 1.3 collective-permute-start.11
  175.8 3.1 %collective-permute-start.12 = (bf16[40,1024]{1,0:T(8,128)(2,1)S(1)}, bf16[40,1024]{1,0:T(8,128)(2,1)S(1)}, u32[]{:S(2)}, u32[]{:S(2)}) collective-permute-start(bf16[40,1024]{1,0:T(8,128)(2,1)S(1)} %get-tuple-element.42), channel_id=1, source_target_pairs={{0,64},{32,96},{64,128},{96,160},{128,192},{160,224},{192,0},{224,... | collective-permute-start | bytes 245768 | tf_op jit(solution)/shard_map/ppermute | solution.py:28
  180.1 1.8 collective-permute-start.14
  181.9 1.4 collective-permute-start.15
  183.4 5.7 %collective-permute-start.9 = (bf16[40,1024]{1,0:T(8,128)(2,1)S(1)}, bf16[40,1024]{1,0:T(8,128)(2,1)S(1)}, u32[]{:S(2)}, u32[]{:S(2)}) collective-permute-start(bf16[40,1024]{1,0:T(8,128)(2,1)S(1)} %get-tuple-element.45), channel_id=1, source_target_pairs={{0,128},{32,160},{64,192},{96,224},{128,0},{160,32},{192,64},{224,... | collective-permute-start | bytes 245768 | tf_op jit(solution)/shard_map/ppermute | solution.py:28
  189.1 2.3 %collect.1 = f32[12,8,1280]{2,1,0:T(8,128)} custom-call(s32[64]{0:T(128)S(1)} %reshape_squeeze.3.sent_ref, bf16[64,8,1280]{2,1,0:T(8,128)(2,1)S(1)} %all-to-all-done.2.got_ref), custom_call_target="tpu_custom_call" | custom-call | tf_op jit(solution)/shard_map/collect/pallas_call | solution.py:278
  (54 shorter events, 11.1 us)
Async XLA Ops:
  1.5 1.5 copy-start
  4.9 11.8 %copy-start.2 = (s32[1,16]{1,0:T(1,128)S(1)}, s32[1,16]{1,0:T(1,128)}, u32[]{:S(2)}) copy-start(s32[1,16]{1,0:T(1,128)} %param.12) | copy-start | bytes 196
  4.9 44.7 %all-to-all-start = ((bf16[64,8,1280]{2,1,0:T(8,128)(2,1)}), bf16[64,8,1280]{2,1,0:T(8,128)(2,1)S(1)}, u32[]{:S(2)}, u32[]{:S(2)}) async-start(bf16[64,8,1280]{2,1,0:T(8,128)(2,1)} %spread.1), calls=%async_computation | async-start | bytes 2621440 | tf_op jit(solution)/shard_map/all_to_all | solution.py:203
  50.2 9.3 %collective-permute-start = (bf16[16,8,1280]{2,1,0:T(8,128)(2,1)S(1)}, bf16[16,8,1280]{2,1,0:T(8,128)(2,1)S(1)}, u32[]{:S(2)}, u32[]{:S(2)}) collective-permute-start(bf16[16,8,1280]{2,1,0:T(8,128)(2,1)S(1)} %gather_fusion), channel_id=1, source_target_pairs={{0,2},{2,4},{4,6},{6,0},{1,3},{3,5},{5,7},{7,1},{8,10},{10,12},{12... | collective-permute-start | bytes 983048 | tf_op jit(solution)/shard_map/ppermute | solution.py:28
  51.8 8.1 %collective-permute-start.1 = (bf16[16,8,1280]{2,1,0:T(8,128)(2,1)S(1)}, bf16[16,8,1280]{2,1,0:T(8,128)(2,1)S(1)}, u32[]{:S(2)}, u32[]{:S(2)}) collective-permute-start(bf16[16,8,1280]{2,1,0:T(8,128)(2,1)S(1)} %gather_fusion), channel_id=1, source_target_pairs={{0,6},{2,0},{4,2},{6,4},{1,7},{3,1},{5,3},{7,5},{8,14},{10,8},{12,... | collective-permute-start | bytes 983048 | tf_op jit(solution)/shard_map/ppermute | solution.py:28
  53.6 12.8 %copy-start.1 = (s32[512]{0:T(512)S(1)}, s32[512]{0:T(512)}, u32[]{:S(2)}) copy-start(s32[512]{0:T(512)} %param.14) | copy-start | bytes 6148
  59.5 6.6 %collective-permute-start.2 = (bf16[8,8,1280]{2,1,0:T(8,128)(2,1)S(1)}, bf16[8,8,1280]{2,1,0:T(8,128)(2,1)S(1)}, u32[]{:S(2)}, u32[]{:S(2)}) collective-permute-start(bf16[8,8,1280]{2,1,0:T(8,128)(2,1)S(1)} %slice.23), channel_id=1, source_target_pairs={{0,2},{2,4},{4,6},{6,0},{1,3},{3,5},{5,7},{7,1},{8,10},{10,12},{12... | collective-permute-start | bytes 491528 | tf_op jit(solution)/shard_map/ppermute | solution.py:28
  59.9 6.2 %collective-permute-start.3 = (bf16[8,8,1280]{2,1,0:T(8,128)(2,1)S(1)}, bf16[8,8,1280]{2,1,0:T(8,128)(2,1)S(1)}, u32[]{:S(2)}, u32[]{:S(2)}) collective-permute-start(bf16[8,8,1280]{2,1,0:T(8,128)(2,1)S(1)} %slice.24), channel_id=1, source_target_pairs={{0,6},{2,0},{4,2},{6,4},{1,7},{3,1},{5,3},{7,5},{8,14},{10,8},{12,... | collective-permute-start | bytes 491528 | tf_op jit(solution)/shard_map/ppermute | solution.py:28
  66.2 3.1 %collective-permute-start.4 = (bf16[4,16,8,1280]{3,2,1,0:T(8,128)(2,1)S(1)}, bf16[4,16,8,1280]{3,2,1,0:T(8,128)(2,1)S(1)}, u32[]{:S(2)}, u32[]{:S(2)}) collective-permute-start(bf16[4,16,8,1280]{3,2,1,0:T(8,128)(2,1)S(1)} %bitcast.25), channel_id=1, source_target_pairs={{0,1},{1,0},{2,3},{3,2},{4,5},{5,4},{6,7},{7,6},{8,9},{9,8},{10,11... | collective-permute-start | bytes 3932168 | tf_op jit(solution)/shard_map/ppermute | solution.py:28
  69.3 1.1 copy-start.5
  70.4 1.3 copy-start.3
  71.7 1.3 copy-start.4
  73.0 1.3 copy-start.6
  74.4 1.0 copy-start.7
  75.4 1.0 copy-start.8
  96.9 3.4 %copy-start.9 = (bf16[4,40,1024]{2,1,0:T(8,128)(2,1)}, bf16[4,40,1024]{2,1,0:T(8,128)(2,1)S(1)}, u32[]{:S(2)}) copy-start(bf16[4,40,1024]{2,1,0:T(8,128)(2,1)S(1)} %get-tuple-element.28) | copy-start | bytes 983044
  96.9 26.0 %copy-start.10 = (bf16[4,40,1024]{2,1,0:T(8,128)(2,1)}, bf16[4,40,1024]{2,1,0:T(8,128)(2,1)S(1)}, u32[]{:S(2)}) copy-start(bf16[4,40,1024]{2,1,0:T(8,128)(2,1)S(1)} %get-tuple-element.26) | copy-start | bytes 983044
  96.9 3.0 %collective-permute-start.16 = (bf16[4,16,8,1280]{3,2,1,0:T(8,128)(2,1)S(1)}, bf16[4,16,8,1280]{3,2,1,0:T(8,128)(2,1)S(1)}, u32[]{:S(2)}, u32[]{:S(2)}) collective-permute-start(bf16[4,16,8,1280]{3,2,1,0:T(8,128)(2,1)S(1)} %get-tuple-element.30), channel_id=1, source_target_pairs={{0,1},{1,0},{2,3},{3,2},{4,5},{5,4},{6,7},{7,6},{8,9},{9,8},{10,11... | collective-permute-start | bytes 3932168 | tf_op jit(solution)/shard_map/ppermute | solution.py:28
  124.9 64.2 %all-to-all-start.2 = ((bf16[64,8,1280]{2,1,0:T(8,128)(2,1)}), bf16[64,8,1280]{2,1,0:T(8,128)(2,1)S(1)}, u32[]{:S(2)}, u32[]{:S(2)}) async-start(bf16[64,8,1280]{2,1,0:T(8,128)(2,1)} %pack.1), calls=%async_computation.2 | async-start | bytes 2621440 | tf_op jit(solution)/shard_map/all_to_all | solution.py:269
  131.6 14.2 %collective-permute-start.5 = (bf16[4,40,1024]{2,1,0:T(8,128)(2,1)}, bf16[4,40,1024]{2,1,0:T(8,128)(2,1)S(1)}, u32[]{:S(2)}, u32[]{:S(2)}) collective-permute-start(bf16[4,40,1024]{2,1,0:T(8,128)(2,1)} %copy-done.10), channel_id=1, source_target_pairs={{0,8},{8,16},{16,24},{24,0},{1,9},{9,17},{17,25},{25,1},{2,10},{10... | collective-permute-start | bytes 983048 | tf_op jit(solution)/shard_map/ppermute | solution.py:28
  133.2 15.1 %collective-permute-start.7 = (bf16[4,40,1024]{2,1,0:T(8,128)(2,1)}, bf16[4,40,1024]{2,1,0:T(8,128)(2,1)S(1)}, u32[]{:S(2)}, u32[]{:S(2)}) collective-permute-start(bf16[4,40,1024]{2,1,0:T(8,128)(2,1)} %copy-done.9), channel_id=1, source_target_pairs={{0,24},{8,0},{16,8},{24,16},{1,25},{9,1},{17,9},{25,17},{2,26},{10... | collective-permute-start | bytes 983048 | tf_op jit(solution)/shard_map/ppermute | solution.py:28
  146.8 20.2 %collective-permute-start.6 = (bf16[8,40,1024]{2,1,0:T(8,128)(2,1)}, bf16[8,40,1024]{2,1,0:T(8,128)(2,1)S(1)}, u32[]{:S(2)}, u32[]{:S(2)}) collective-permute-start(bf16[8,40,1024]{2,1,0:T(8,128)(2,1)} %add_convert_fusion.3), channel_id=1, source_target_pairs={{0,8},{8,16},{16,24},{24,0},{1,9},{9,17},{17,25},{25,1},{2,10},{10... | collective-permute-start | bytes 1966088 | tf_op jit(solution)/shard_map/ppermute | solution.py:28
  149.2 19.5 %collective-permute-start.8 = (bf16[8,40,1024]{2,1,0:T(8,128)(2,1)}, bf16[8,40,1024]{2,1,0:T(8,128)(2,1)}, u32[]{:S(2)}, u32[]{:S(2)}) collective-permute-start(bf16[8,40,1024]{2,1,0:T(8,128)(2,1)} %add_convert_fusion.2), channel_id=1, source_target_pairs={{0,24},{8,0},{16,8},{24,16},{1,25},{9,1},{17,9},{25,17},{2,26},{10... | collective-permute-start | bytes 1966088 | tf_op jit(solution)/shard_map/ppermute | solution.py:28
  170.3 11.7 %collective-permute-start.10 = (bf16[40,1024]{1,0:T(8,128)(2,1)S(1)}, bf16[40,1024]{1,0:T(8,128)(2,1)S(1)}, u32[]{:S(2)}, u32[]{:S(2)}) collective-permute-start(bf16[40,1024]{1,0:T(8,128)(2,1)S(1)} %get-tuple-element.44), channel_id=1, source_target_pairs={{0,96},{32,128},{64,160},{96,192},{128,224},{160,0},{192,32},{224,... | collective-permute-start | bytes 245768 | tf_op jit(solution)/shard_map/ppermute | solution.py:28
  174.5 8.9 %collective-permute-start.11 = (bf16[40,1024]{1,0:T(8,128)(2,1)S(1)}, bf16[40,1024]{1,0:T(8,128)(2,1)S(1)}, u32[]{:S(2)}, u32[]{:S(2)}) collective-permute-start(bf16[40,1024]{1,0:T(8,128)(2,1)S(1)} %get-tuple-element.43), channel_id=1, source_target_pairs={{0,160},{32,192},{64,224},{96,0},{128,32},{160,64},{192,96},{224,1... | collective-permute-start | bytes 245768 | tf_op jit(solution)/shard_map/ppermute | solution.py:28
  175.8 15.6 %collective-permute-start.12 = (bf16[40,1024]{1,0:T(8,128)(2,1)S(1)}, bf16[40,1024]{1,0:T(8,128)(2,1)S(1)}, u32[]{:S(2)}, u32[]{:S(2)}) collective-permute-start(bf16[40,1024]{1,0:T(8,128)(2,1)S(1)} %get-tuple-element.42), channel_id=1, source_target_pairs={{0,64},{32,96},{64,128},{96,160},{128,192},{160,224},{192,0},{224,... | collective-permute-start | bytes 245768 | tf_op jit(solution)/shard_map/ppermute | solution.py:28
  178.8 12.6 %collective-permute-start.13 = (bf16[40,1024]{1,0:T(8,128)(2,1)S(1)}, bf16[40,1024]{1,0:T(8,128)(2,1)S(1)}, u32[]{:S(2)}, u32[]{:S(2)}) collective-permute-start(bf16[40,1024]{1,0:T(8,128)(2,1)S(1)} %get-tuple-element.41), channel_id=1, source_target_pairs={{0,192},{32,224},{64,0},{96,32},{128,64},{160,96},{192,128},{224,1... | collective-permute-start | bytes 245768 | tf_op jit(solution)/shard_map/ppermute | solution.py:28
  180.1 11.3 %collective-permute-start.14 = (bf16[40,1024]{1,0:T(8,128)(2,1)S(1)}, bf16[40,1024]{1,0:T(8,128)(2,1)S(1)}, u32[]{:S(2)}, u32[]{:S(2)}) collective-permute-start(bf16[40,1024]{1,0:T(8,128)(2,1)S(1)} %get-tuple-element.40), channel_id=1, source_target_pairs={{0,32},{32,64},{64,96},{96,128},{128,160},{160,192},{192,224},{224... | collective-permute-start | bytes 245768 | tf_op jit(solution)/shard_map/ppermute | solution.py:28
  181.9 9.5 %collective-permute-start.15 = (bf16[40,1024]{1,0:T(8,128)(2,1)S(1)}, bf16[40,1024]{1,0:T(8,128)(2,1)S(1)}, u32[]{:S(2)}, u32[]{:S(2)}) collective-permute-start(bf16[40,1024]{1,0:T(8,128)(2,1)S(1)} %get-tuple-element.39), channel_id=1, source_target_pairs={{0,224},{32,0},{64,32},{96,64},{128,96},{160,128},{192,160},{224,1... | collective-permute-start | bytes 245768 | tf_op jit(solution)/shard_map/ppermute | solution.py:28
  183.4 8.6 %collective-permute-start.9 = (bf16[40,1024]{1,0:T(8,128)(2,1)S(1)}, bf16[40,1024]{1,0:T(8,128)(2,1)S(1)}, u32[]{:S(2)}, u32[]{:S(2)}) collective-permute-start(bf16[40,1024]{1,0:T(8,128)(2,1)S(1)} %get-tuple-element.45), channel_id=1, source_target_pairs={{0,128},{32,160},{64,192},{96,224},{128,0},{160,32},{192,64},{224,... | collective-permute-start | bytes 245768 | tf_op jit(solution)/shard_map/ppermute | solution.py:28

commit v4 on v3

--- a/solution.py
+++ b/solution.py
@@ -11,6 +11,9 @@
 WIN = 4
 SUB = 8
 OFFSETS = (0, 3, 1, 2)
+MAIN_MIB = 36
+WEIGHT_MIB = 24
+SHELF = 16384
 NEG_FILL = -1e30
 BF = jnp.bfloat16
 F32 = jnp.float32
@@ -38,6 +41,14 @@
 
 def vmem():
     return pl.BlockSpec(memory_space=pltpu.VMEM)
+
+
+def anywhere():
+    return pl.BlockSpec(memory_space=pl.ANY)
+
+
+def far():
+    return pl.BlockSpec(memory_space=pltpu.HBM)
 
 
 def smem():
@@ -51,22 +62,52 @@
 
 
 def main_kernel(
-    start_ref, pos_ref, mine_ref, other_ref, wk_ref, wv_ref, q_ref, g_ref, slot_ref,
-    att_ref, dq_ref, keep_ref, give_ref, own_ref, next_ref, fa_ref, fb_ref, prev_ref,
-    lat_ref, k_ref, v_ref, acc_ref, bg_ref, t_ref, sum_ref,
+    start_ref, pos_ref, mine_any, other_any, wk_any, wv_any, q_any, g_any, slot_ref,
+    att_ref, dq_ref, keep_ref, give_ref, shelf_any,
+    mine_ref, other_ref, wk_ref, wv_ref, q_ref, g_ref,
+    lat_ref, k_ref, v_ref, acc_ref, bg_ref, in_sem, mine_sem, other_sem, lat_sem, bg_sem,
 ):
-    vis = mine_ref.shape[1]
-    rows = 2 * mine_ref.shape[0] * SUB
+    nx, vis = mine_ref.shape[:2]
+    rows = 2 * nx * SUB
     width = mine_ref.shape[3]
     cols = wk_ref.shape[1]
     heads = cols // DH
     chunk = WIN * rows
-    nx = mine_ref.shape[0]
+    chunks = vis // WIN
     my_x = pos_ref[0]
-    my_y = pos_ref[1]
-
-    @pl.loop(0, vis // WIN)
+
+    def part_in(src, dst, sem, i):
+        at = pl.ds(i * WIN, WIN)
+        return pltpu.make_async_copy(src.at[:, at], dst.at[:, at], sem.at[i])
+
+    def part_out(src, base, sem, i):
+        at = pl.ds(pl.multiple_of(i * chunk, chunk), chunk)
+        to = pl.ds(pl.multiple_of(base + i * chunk, chunk), chunk)
+        return pltpu.make_async_copy(src.at[at], shelf_any.at[to, pl.ds(0, src.shape[1])], sem.at[i])
+
+    whole = [
+        pltpu.make_async_copy(src, dst, in_sem.at[n])
+        for n, (src, dst) in enumerate(
+            ((wk_any, wk_ref), (wv_any, wv_ref), (q_any, q_ref), (g_any, g_ref))
+        )
+    ]
+    whole[0].start()
+    part_in(mine_any, mine_ref, mine_sem, 0).start()
+    part_in(other_any, other_ref, other_sem, 0).start()
+    whole[1].start()
+    for n in range(1, chunks):
+        part_in(mine_any, mine_ref, mine_sem, n).start()
+        part_in(other_any, other_ref, other_sem, n).start()
+    whole[2].start()
+    whole[3].start()
+    acc_ref[...] = jnp.zeros_like(acc_ref)
+    whole[0].wait()
+    whole[1].wait()
+
+    @pl.loop(0, chunks)
     def _(i):
+        part_in(mine_any, mine_ref, mine_sem, i).wait()
+        part_in(other_any, other_ref, other_sem, i).wait()
         mine = mine_ref[:, pl.ds(i * WIN, WIN)].astype(F32)
         other = other_ref[:, pl.ds(i * WIN, WIN)].astype(F32)
         parts = []
@@ -78,8 +119,10 @@
         lat_ref[at, :] = x
         k_ref[at, :] = mm(x, wk_ref[...], NN).astype(BF)
         v_ref[at, :] = mm(x, wv_ref[...], NN).astype(BF)
-        acc_ref[at, :] = jnp.zeros((chunk, 2 * cols), F32)
-
+        part_out(lat_ref, 0, lat_sem, i).start()
+
+    whole[2].wait()
+    whole[3].wait()
     span = WIN * GAP
     scale = DH ** (-0.5)
 
@@ -110,11 +153,12 @@
             acc_ref[at, c] += mm(ds, q, NN)
             acc_ref[at, slice(cols + h * DH, cols + (h + 1) * DH)] += mm(pb, g, NN)
 
-    @pl.loop(0, vis // WIN)
+    @pl.loop(0, chunks)
     def _(i):
         at = pl.ds(pl.multiple_of(i * chunk, chunk), chunk)
         grad = acc_ref[at, :].astype(BF)
         bg_ref[at, :] = grad
+        part_out(bg_ref, vis * rows, bg_sem, i).start()
         out = mm(grad[:, :cols], wk_ref[...], NT) + mm(grad[:, cols:], wv_ref[...], NT)
         for s in range(WIN):
             piece = out[s * rows:(s + 1) * rows].reshape(rows // SUB, SUB, width).astype(BF)
@@ -123,15 +167,39 @@
                 keep_ref[there, i * WIN + s] = piece[r]
                 give_ref[there, i * WIN + s] = piece[nx + r]
 
-    nz, part, _ = own_ref.shape
-    ny = width // (nz * part)
-    half = t_ref.shape[0]
+    for n in range(chunks):
+        part_out(lat_ref, 0, lat_sem, n).wait()
+        part_out(bg_ref, vis * rows, bg_sem, n).wait()
+
+
+def weight_kernel(
+    y_ref, shelf_any, own_ref, next_ref, fa_ref, fb_ref, prev_ref,
+    lat_ref, bg_ref, t_ref, sum_ref, lat_sem, bg_sem,
+):
+    nz, part, cols = own_ref.shape
+    halves, keys, half = lat_ref.shape
+    ny = halves * half // (nz * part)
+    my_y = y_ref[0]
     step = 256
     zh = nz // 2
-    for j in range(width // half):
-        t_ref[...] = lat_ref[:, j * half:(j + 1) * half].T
-
-        @pl.loop(0, 2 * cols // step)
+    loads = [
+        pltpu.make_async_copy(
+            shelf_any.at[pl.ds(0, keys), pl.ds(j * half, half)], lat_ref.at[j], lat_sem.at[j]
+        )
+        for j in range(halves)
+    ]
+    rest = pltpu.make_async_copy(shelf_any.at[pl.ds(keys, keys), pl.ds(0, cols)], bg_ref, bg_sem)
+    loads[0].start()
+    rest.start()
+    for load in loads[1:]:
+        load.start()
+    for j in range(halves):
+        loads[j].wait()
+        t_ref[...] = lat_ref[j].T
+        if j == 0:
+            rest.wait()
+
+        @pl.loop(0, cols // step)
         def _(n):
             at = pl.ds(pl.multiple_of(n * step, step), step)
             sum_ref[j * half:(j + 1) * half, at] = mm(t_ref[...], bg_ref[:, at], NN)
@@ -217,38 +285,71 @@
     start = jnp.minimum(jnp.maximum(slot_rows[:, 0, 0], 0), vis - WIN)
     keys = vis * lat_rows
     zh = nz // 2
-    here = jnp.stack([lax.axis_index("x"), lax.axis_index("y")]).astype(jnp.int32)
+    x_here = lax.axis_index("x").reshape(1).astype(jnp.int32)
+    y_here = lax.axis_index("y").reshape(1).astype(jnp.int32)
     tokens_out = jax.ShapeDtypeStruct((tokens, cols), BF)
     rows_out = jax.ShapeDtypeStruct((nx, vis, SUB, width), BF)
     full = jax.ShapeDtypeStruct((nz, part, 2 * cols), BF)
     split = jax.ShapeDtypeStruct((zh, part, 2 * cols), BF)
-    att, dq, keep, give, gw_own, gw_next, gw_fa, gw_fb, gw_prev = pl.pallas_call(
+    chunks = vis // WIN
+    att, dq, keep, give, shelf = pl.pallas_call(
         main_kernel,
         name="main",
-        out_shape=(tokens_out, tokens_out, rows_out, rows_out, full, full, split, split, full),
-        in_specs=[smem(), smem()] + [vmem()] * 7,
-        out_specs=tuple([vmem()] * 9),
+        out_shape=(
+            tokens_out, tokens_out, rows_out, rows_out,
+            jax.ShapeDtypeStruct((SHELF, width), BF),
+        ),
+        in_specs=[smem(), smem()] + [anywhere()] * 2 + [far()] * 4 + [vmem()],
+        out_specs=(vmem(), vmem(), vmem(), vmem(), far()),
         scratch_shapes=[
+            pltpu.VMEM((nx, vis, SUB, width), BF),
+            pltpu.VMEM((nx, vis, SUB, width), BF),
+            pltpu.VMEM((width, cols), BF),
+            pltpu.VMEM((width, cols), BF),
+            pltpu.VMEM((tokens, cols), BF),
+            pltpu.VMEM((tokens, cols), BF),
             pltpu.VMEM((keys, width), BF),
             pltpu.VMEM((keys, cols), BF),
             pltpu.VMEM((keys, cols), BF),
             pltpu.VMEM((keys, 2 * cols), F32),
             pltpu.VMEM((keys, 2 * cols), BF),
-            pltpu.VMEM((width // 2, keys), BF),
-            pltpu.VMEM((width, 2 * cols), F32),
+            pltpu.SemaphoreType.DMA((4,)),
+            pltpu.SemaphoreType.DMA((chunks,)),
+            pltpu.SemaphoreType.DMA((chunks,)),
+            pltpu.SemaphoreType.DMA((chunks,)),
+            pltpu.SemaphoreType.DMA((chunks,)),
         ],
-        compiler_params=grant(26),
+        compiler_params=grant(MAIN_MIB),
         cost_estimate=pl.CostEstimate(
-            flops=12 * keys * width * cols + 16 * keys * span * cols,
+            flops=8 * keys * width * cols + 16 * keys * span * cols,
             bytes_accessed=16 * 1024 * 1024,
             transcendentals=tokens * 4 * 256,
         ),
-    )(start, here, mine, other, key_weight, value_weight, queries, grad_out, slot_rows)
+    )(start, x_here, mine, other, key_weight, value_weight, queries, grad_out, slot_rows)
 
     swapped = shift(give, "core", 1, 2)
+    crossed = lax.all_to_all(add2(keep, swapped), "x", split_axis=0, concat_axis=0, tiled=True)
+    gw_own, gw_next, gw_fa, gw_fb, gw_prev = pl.pallas_call(
+        weight_kernel,
+        name="weights",
+        out_shape=(full, full, split, split, full),
+        in_specs=[smem(), far()],
+        out_specs=tuple([vmem()] * 5),
+        scratch_shapes=[
+            pltpu.VMEM((2, keys, width // 2), BF),
+            pltpu.VMEM((keys, 2 * cols), BF),
+            pltpu.VMEM((width // 2, keys), BF),
+            pltpu.VMEM((width, 2 * cols), F32),
+            pltpu.SemaphoreType.DMA((2,)),
+            pltpu.SemaphoreType.DMA,
+        ],
+        compiler_params=grant(WEIGHT_MIB),
+        cost_estimate=pl.CostEstimate(
+            flops=4 * keys * width * cols, bytes_accessed=8 * 1024 * 1024, transcendentals=0
+        ),
+    )(y_here, shelf)
     gw_up = shift(gw_fa, "y", 1, ny)
     gw_down = shift(gw_fb, "y", -1, ny)
-    crossed = lax.all_to_all(add2(keep, swapped), "x", split_axis=0, concat_axis=0, tiled=True)
 
     gw_next = (gw_next.astype(F32)
                + jnp.concatenate([gw_up, jnp.zeros_like(gw_up)], axis=0).astype(F32)).astype(BF)

time: 196 us -> 188 us (0.959)
  local copies, waits for them, and re-layouts: 10.9 us -> 3.85 us
  starting transfers between devices: 49.4 us -> 45.3 us
  Pallas kernels: 26.6 us -> 29.6 us
    unnamed x27 -> x19, local copies, waits for them, and re-layouts: 9.51 us -> 2.41 us
    pallas_call x0 -> x1, Pallas kernels: none -> 6.85 us  [local(): pl.pallas_call(weight_kernel, name='weights', out_shape=(full, full, spli...]
    ppermute x17, starting transfers between devices: 30.9 us -> 26.7 us  [shift(): return lax.ppermute(v, axis, [(i, (i + step) % size) for i in range(size)])]
    pallas_call x1, Pallas kernels: 20.5 us -> 16.6 us  [local(): pl.pallas_call(main_kernel, name='main', out_shape=(tokens_out, tokens_ou...]
  transfers between devices with their start and end apart: 19 -> 19, of which waited for: 9 -> 10; matrix products, arithmetic and copies ran while one was open for 2% -> 2% of each run, Pallas kernels for 1% -> 5%
where the time goes in v4:
time: 188 us; the launch traced here: 185 us
  waiting for transfers between devices  79.8 us (42%)
  starting transfers between devices  45.3 us (24%)
  Pallas kernels  29.6 us (16%)
  blocking collectives  22.6 us (12%)
  local copies, waits for them, and re-layouts  3.85 us (2%)
  other arithmetic  3.09 us (2%)
    ppermute x17, waiting for transfers between devices, shift(): return lax.ppermute(v, axis, [(i, (i + step) % size) for i in range(size)])  46.9 us
    all_to_all x1, waiting for transfers between devices, local(): got = lax.all_to_all(send, seq, split_axis=0, concat_axis=0, tiled=True)  32.9 us
    ppermute x17, starting transfers between devices, shift(): return lax.ppermute(v, axis, [(i, (i + step) % size) for i in range(size)])  26.7 us
    all_to_all x1, blocking collectives, local(): lax.all_to_all(add2(keep, swapped), 'x', split_axis=0, concat_axis=0, til...  22.6 us
    pallas_call x1, Pallas kernels, local(): pl.pallas_call(main_kernel, name='main', out_shape=(tokens_out, tokens_ou...  16.6 us
    all_to_all x1, starting transfers between devices, local(): got = lax.all_to_all(send, seq, split_axis=0, concat_axis=0, tiled=True)  11.8 us
    pallas_call x1, Pallas kernels, local(): pl.pallas_call(weight_kernel, name='weights', out_shape=(full, full, spli...  6.85 us
    all_to_all x1, starting transfers between devices, local(): lax.all_to_all(back, seq, split_axis=0, concat_axis=0, tiled=True)  6.7 us
  transfers between devices with their start and end apart: 19, of which 10 were waited for; matrix products, arithmetic and copies ran while one was open for 2% of the time, Pallas kernels for 5%

profile of v4, /device:TPU:8, one launch (start us, length us, event | category | flops | bytes accessed | tf_op | source)
XLA Modules:
  0.0 185.0 jit_solution(2149344196394263988)
XLA Ops:
  1.5 1.5 copy-done
  3.1 1.8 spread.1
  4.9 11.8 %all-to-all-start = ((bf16[64,8,1280]{2,1,0:T(8,128)(2,1)}), bf16[64,8,1280]{2,1,0:T(8,128)(2,1)S(1)}, u32[]{:S(2)}, u32[]{:S(2)}) async-start(bf16[64,8,1280]{2,1,0:T(8,128)(2,1)} %spread.1), calls=%async_computation | async-start | bytes 2621440 | tf_op jit(solution)/shard_map/all_to_all | solution.py:271
  16.8 32.9 %all-to-all-done = bf16[64,8,1280]{2,1,0:T(8,128)(2,1)S(1)} async-done(((bf16[64,8,1280]{2,1,0:T(8,128)(2,1)}), bf16[64,8,1280]{2,1,0:T(8,128)(2,1)S(1)}, u32[]{:S(2)}, u32[]{:S(2)}) %all-to-all-start) | async-done | bytes 1310752 | tf_op jit(solution)/shard_map/all_to_all | solution.py:271
  50.2 1.6 collective-permute-start
  51.8 1.7 collective-permute-start.1
  53.6 5.9 %collective-permute-done = bf16[16,8,1280]{2,1,0:T(8,128)(2,1)S(1)} collective-permute-done((bf16[16,8,1280]{2,1,0:T(8,128)(2,1)S(1)}, bf16[16,8,1280]{2,1,0:T(8,128)(2,1)S(1)}, u32[]{:S(2)}, u32[]{:S(2)}) %collective-permute-start) | collective-permute-done | bytes 327712 | tf_op jit(solution)/shard_map/ppermute | solution.py:31
  59.9 3.0 %collective-permute-start.3 = (bf16[8,8,1280]{2,1,0:T(8,128)(2,1)S(1)}, bf16[8,8,1280]{2,1,0:T(8,128)(2,1)S(1)}, u32[]{:S(2)}, u32[]{:S(2)}) collective-permute-start(bf16[8,8,1280]{2,1,0:T(8,128)(2,1)S(1)} %slice.24), channel_id=1, source_target_pairs={{0,6},{2,0},{4,2},{6,4},{1,7},{3,1},{5,3},{7,5},{8,14},{10,8},{12,... | collective-permute-start | bytes 491528 | tf_op jit(solution)/shard_map/ppermute | solution.py:31
  63.0 3.1 %collective-permute-done.2 = bf16[8,8,1280]{2,1,0:T(8,128)(2,1)S(1)} collective-permute-done((bf16[8,8,1280]{2,1,0:T(8,128)(2,1)S(1)}, bf16[8,8,1280]{2,1,0:T(8,128)(2,1)S(1)}, u32[]{:S(2)}, u32[]{:S(2)}) %collective-permute-start.2) | collective-permute-done | bytes 163872 | tf_op jit(solution)/shard_map/ppermute | solution.py:31
  66.5 2.9 %collective-permute-done.4.other_any = bf16[4,16,8,1280]{3,2,1,0:T(8,128)(2,1)S(1)} collective-permute-done((bf16[4,16,8,1280]{3,2,1,0:T(8,128)(2,1)S(1)}, bf16[4,16,8,1280]{3,2,1,0:T(8,128)(2,1)S(1)}, u32[]{:S(2)}, u32[]{:S(2)}) %collective-permute-start.4) | collective-permute-done | bytes 1310752 | tf_op jit(solution)/shard_map/ppermute | solution.py:31
  69.3 16.6 %main.1 = (bf16[512,512]{1,0:T(8,128)(2,1)}, bf16[512,512]{1,0:T(8,128)(2,1)}, bf16[4,16,8,1280]{3,2,1,0:T(8,128)(2,1)S(1)}, bf16[4,16,8,1280]{3,2,1,0:T(8,128)(2,1)S(1)}, bf16[16384,1280]{1,0:T(8,128)(2,1)}) custom-call(s32[4]{0:T(128)S(1)} %fusion.6.start_ref, s32[1]{0:T(128)} %bitcast.1.pos_ref, bf16[4,16,8,1280]{3,2,1,0:T(8,128)(2,1)S(1)} %bitcast.26, ...), custom_call_target="tpu_custom_call" | custom-call | flops 6442450944 | bytes 16777216 | tf_op jit(solution)/shard_map/main/pallas_call | solution.py:295
  86.1 2.9 %collective-permute-done.16 = bf16[4,16,8,1280]{3,2,1,0:T(8,128)(2,1)S(1)} collective-permute-done((bf16[4,16,8,1280]{3,2,1,0:T(8,128)(2,1)S(1)}, bf16[4,16,8,1280]{3,2,1,0:T(8,128)(2,1)S(1)}, u32[]{:S(2)}, u32[]{:S(2)}) %collective-permute-start.16) | collective-permute-done | bytes 1310752 | tf_op jit(solution)/shard_map/ppermute | solution.py:31
  89.3 22.6 %all_to_all.15.got_ref = bf16[4,16,8,1280]{3,2,1,0:T(8,128)(2,1)S(1)} all-to-all(bf16[4,16,8,1280]{3,2,1,0:T(8,128)(2,1)S(1)} %add_convert_fusion), channel_id=1, replica_groups=mesh['z'=8,'y'=4,'x'=4,'core'=2] {'x'}, dimensions={0} | all-to-all | bytes 2621440 | tf_op jit(solution)/shard_map/all_to_all | solution.py:331
  111.9 2.0 %pack.1 = bf16[64,8,1280]{2,1,0:T(8,128)(2,1)} custom-call(s32[16]{0:T(128)S(1)} %bitcast.29, bf16[4,16,8,1280]{3,2,1,0:T(8,128)(2,1)S(1)} %all_to_all.15.got_ref), custom_call_target="tpu_custom_call" | custom-call | tf_op jit(solution)/shard_map/pack/pallas_call | solution.py:362
  113.9 6.7 %all-to-all-start.2 = ((bf16[64,8,1280]{2,1,0:T(8,128)(2,1)}), bf16[64,8,1280]{2,1,0:T(8,128)(2,1)S(1)}, u32[]{:S(2)}, u32[]{:S(2)}) async-start(bf16[64,8,1280]{2,1,0:T(8,128)(2,1)} %pack.1), calls=%async_computation.2 | async-start | bytes 2621440 | tf_op jit(solution)/shard_map/all_to_all | solution.py:370
  120.7 6.8 %weights.1 = (bf16[8,40,1024]{2,1,0:T(8,128)(2,1)S(1)}, bf16[8,40,1024]{2,1,0:T(8,128)(2,1)S(1)}, bf16[4,40,1024]{2,1,0:T(8,128)(2,1)S(1)}, bf16[4,40,1024]{2,1,0:T(8,128)(2,1)S(1)}, bf16[8,40,1024]{2,1,0:T(8,128)(2,1)S(1)}) custom-call(s32[1]{0:T(128)} %bitcast.5.y_ref, bf16[16384,1280]{1,0:T(8,128)(2,1)} %get-tuple-element.25.shelf_any), custom_call_target="tpu_custom_call" | custom-call | flops 2684354560 | bytes 8388608 | tf_op jit(solution)/shard_map/weights/pallas_call | solution.py:332
  127.5 1.5 collective-permute-start.5
  129.6 11.0 %collective-permute-done.5 = bf16[4,40,1024]{2,1,0:T(8,128)(2,1)S(1)} collective-permute-done((bf16[4,40,1024]{2,1,0:T(8,128)(2,1)S(1)}, bf16[4,40,1024]{2,1,0:T(8,128)(2,1)S(1)}, u32[]{:S(2)}, u32[]{:S(2)}) %collective-permute-start.5) | collective-permute-done | bytes 327712 | tf_op jit(solution)/shard_map/ppermute | solution.py:31
  140.8 2.4 %collective-permute-start.6 = (bf16[8,40,1024]{2,1,0:T(8,128)(2,1)S(1)}, bf16[8,40,1024]{2,1,0:T(8,128)(2,1)S(1)}, u32[]{:S(2)}, u32[]{:S(2)}) collective-permute-start(bf16[8,40,1024]{2,1,0:T(8,128)(2,1)S(1)} %add_convert_fusion.3), channel_id=1, source_target_pairs={{0,8},{8,16},{16,24},{24,0},{1,9},{9,17},{17,25},{25,1},{2,10},{10... | collective-permute-start | bytes 1966088 | tf_op jit(solution)/shard_map/ppermute | solution.py:31
  143.2 1.0 add_convert_fusion.2
  144.2 15.6 %collective-permute-done.6 = bf16[8,40,1024]{2,1,0:T(8,128)(2,1)S(1)} collective-permute-done((bf16[8,40,1024]{2,1,0:T(8,128)(2,1)S(1)}, bf16[8,40,1024]{2,1,0:T(8,128)(2,1)S(1)}, u32[]{:S(2)}, u32[]{:S(2)}) %collective-permute-start.6) | collective-permute-done | bytes 655392 | tf_op jit(solution)/shard_map/ppermute | solution.py:31
  159.8 2.0 %collective-permute-done.8 = bf16[8,40,1024]{2,1,0:T(8,128)(2,1)} collective-permute-done((bf16[8,40,1024]{2,1,0:T(8,128)(2,1)}, bf16[8,40,1024]{2,1,0:T(8,128)(2,1)}, u32[]{:S(2)}, u32[]{:S(2)}) %collective-permute-start.8) | collective-permute-done | bytes 655392 | tf_op jit(solution)/shard_map/ppermute | solution.py:31
  161.8 1.4 add_convert_fusion.1
  163.3 2.2 %collective-permute-start.10 = (bf16[40,1024]{1,0:T(8,128)(2,1)S(1)}, bf16[40,1024]{1,0:T(8,128)(2,1)S(1)}, u32[]{:S(2)}, u32[]{:S(2)}) collective-permute-start(bf16[40,1024]{1,0:T(8,128)(2,1)S(1)} %get-tuple-element.46), channel_id=1, source_target_pairs={{0,96},{32,128},{64,160},{96,192},{128,224},{160,0},{192,32},{224,... | collective-permute-start | bytes 245768 | tf_op jit(solution)/shard_map/ppermute | solution.py:31
  165.5 2.9 %collective-permute-start.11 = (bf16[40,1024]{1,0:T(8,128)(2,1)S(1)}, bf16[40,1024]{1,0:T(8,128)(2,1)S(1)}, u32[]{:S(2)}, u32[]{:S(2)}) collective-permute-start(bf16[40,1024]{1,0:T(8,128)(2,1)S(1)} %get-tuple-element.45), channel_id=1, source_target_pairs={{0,160},{32,192},{64,224},{96,0},{128,32},{160,64},{192,96},{224,1... | collective-permute-start | bytes 245768 | tf_op jit(solution)/shard_map/ppermute | solution.py:31
  168.4 1.2 collective-permute-start.12
  169.6 2.9 %collective-permute-start.13 = (bf16[40,1024]{1,0:T(8,128)(2,1)S(1)}, bf16[40,1024]{1,0:T(8,128)(2,1)S(1)}, u32[]{:S(2)}, u32[]{:S(2)}) collective-permute-start(bf16[40,1024]{1,0:T(8,128)(2,1)S(1)} %get-tuple-element.43), channel_id=1, source_target_pairs={{0,192},{32,224},{64,0},{96,32},{128,64},{160,96},{192,128},{224,1... | collective-permute-start | bytes 245768 | tf_op jit(solution)/shard_map/ppermute | solution.py:31
  172.5 0.8 collective-permute-start.14
  174.1 1.7 collective-permute-start.15
  175.8 3.4 %collective-permute-start.9 = (bf16[40,1024]{1,0:T(8,128)(2,1)S(1)}, bf16[40,1024]{1,0:T(8,128)(2,1)S(1)}, u32[]{:S(2)}, u32[]{:S(2)}) collective-permute-start(bf16[40,1024]{1,0:T(8,128)(2,1)S(1)} %get-tuple-element.47), channel_id=1, source_target_pairs={{0,128},{32,160},{64,192},{96,224},{128,0},{160,32},{192,64},{224,... | collective-permute-start | bytes 245768 | tf_op jit(solution)/shard_map/ppermute | solution.py:31
  179.2 2.3 %collect.1 = f32[12,8,1280]{2,1,0:T(8,128)} custom-call(s32[64]{0:T(128)S(1)} %reshape_squeeze.3.sent_ref, bf16[64,8,1280]{2,1,0:T(8,128)(2,1)S(1)} %all-to-all-done.2.got_ref), custom_call_target="tpu_custom_call" | custom-call | tf_op jit(solution)/shard_map/collect/pallas_call | solution.py:379
  181.6 2.7 %collective-permute-done.9 = bf16[40,1024]{1,0:T(8,128)(2,1)S(1)} collective-permute-done((bf16[40,1024]{1,0:T(8,128)(2,1)S(1)}, bf16[40,1024]{1,0:T(8,128)(2,1)S(1)}, u32[]{:S(2)}, u32[]{:S(2)}) %collective-permute-start.9) | collective-permute-done | bytes 81952 | tf_op jit(solution)/shard_map/ppermute | solution.py:31
  (46 shorter events, 5.0 us)
Async XLA Ops:
  1.5 1.5 copy-start
  4.9 11.8 %copy-start.2 = (s32[1,16]{1,0:T(1,128)S(1)}, s32[1,16]{1,0:T(1,128)}, u32[]{:S(2)}) copy-start(s32[1,16]{1,0:T(1,128)} %param.12) | copy-start | bytes 196
  4.9 44.7 %all-to-all-start = ((bf16[64,8,1280]{2,1,0:T(8,128)(2,1)}), bf16[64,8,1280]{2,1,0:T(8,128)(2,1)S(1)}, u32[]{:S(2)}, u32[]{:S(2)}) async-start(bf16[64,8,1280]{2,1,0:T(8,128)(2,1)} %spread.1), calls=%async_computation | async-start | bytes 2621440 | tf_op jit(solution)/shard_map/all_to_all | solution.py:271
  49.6 19.7 %copy-start.6 = (bf16[512,512]{1,0:T(8,128)(2,1)S(1)}, bf16[512,512]{1,0:T(8,128)(2,1)}, u32[]{:S(2)}) copy-start(bf16[512,512]{1,0:T(8,128)(2,1)} %g_any.1) | copy-start | bytes 1572868
  50.2 9.3 %collective-permute-start = (bf16[16,8,1280]{2,1,0:T(8,128)(2,1)S(1)}, bf16[16,8,1280]{2,1,0:T(8,128)(2,1)S(1)}, u32[]{:S(2)}, u32[]{:S(2)}) collective-permute-start(bf16[16,8,1280]{2,1,0:T(8,128)(2,1)S(1)} %gather_fusion), channel_id=1, source_target_pairs={{0,2},{2,4},{4,6},{6,0},{1,3},{3,5},{5,7},{7,1},{8,10},{10,12},{12... | collective-permute-start | bytes 983048 | tf_op jit(solution)/shard_map/ppermute | solution.py:31
  51.8 8.1 %collective-permute-start.1 = (bf16[16,8,1280]{2,1,0:T(8,128)(2,1)S(1)}, bf16[16,8,1280]{2,1,0:T(8,128)(2,1)S(1)}, u32[]{:S(2)}, u32[]{:S(2)}) collective-permute-start(bf16[16,8,1280]{2,1,0:T(8,128)(2,1)S(1)} %gather_fusion), channel_id=1, source_target_pairs={{0,6},{2,0},{4,2},{6,4},{1,7},{3,1},{5,3},{7,5},{8,14},{10,8},{12,... | collective-permute-start | bytes 983048 | tf_op jit(solution)/shard_map/ppermute | solution.py:31
  53.5 15.8 %copy-start.5 = (bf16[512,512]{1,0:T(8,128)(2,1)S(1)}, bf16[512,512]{1,0:T(8,128)(2,1)}, u32[]{:S(2)}) copy-start(bf16[512,512]{1,0:T(8,128)(2,1)} %q_any.1) | copy-start | bytes 1572868
  53.6 12.7 %copy-start.1 = (s32[512]{0:T(512)S(1)}, s32[512]{0:T(512)}, u32[]{:S(2)}) copy-start(s32[512]{0:T(512)} %param.14) | copy-start | bytes 6148
  53.6 15.8 %copy-start.3 = (bf16[1280,512]{1,0:T(8,128)(2,1)S(1)}, bf16[1280,512]{1,0:T(8,128)(2,1)}, u32[]{:S(2)}) copy-start(bf16[1280,512]{1,0:T(8,128)(2,1)} %wk_any.1) | copy-start | bytes 3932164
  53.6 15.7 %copy-start.4 = (bf16[1280,512]{1,0:T(8,128)(2,1)S(1)}, bf16[1280,512]{1,0:T(8,128)(2,1)}, u32[]{:S(2)}) copy-start(bf16[1280,512]{1,0:T(8,128)(2,1)} %wv_any.1) | copy-start | bytes 3932164
  59.5 6.6 %collective-permute-start.2 = (bf16[8,8,1280]{2,1,0:T(8,128)(2,1)S(1)}, bf16[8,8,1280]{2,1,0:T(8,128)(2,1)S(1)}, u32[]{:S(2)}, u32[]{:S(2)}) collective-permute-start(bf16[8,8,1280]{2,1,0:T(8,128)(2,1)S(1)} %slice.23), channel_id=1, source_target_pairs={{0,2},{2,4},{4,6},{6,0},{1,3},{3,5},{5,7},{7,1},{8,10},{10,12},{12... | collective-permute-start | bytes 491528 | tf_op jit(solution)/shard_map/ppermute | solution.py:31
  59.9 6.2 %collective-permute-start.3 = (bf16[8,8,1280]{2,1,0:T(8,128)(2,1)S(1)}, bf16[8,8,1280]{2,1,0:T(8,128)(2,1)S(1)}, u32[]{:S(2)}, u32[]{:S(2)}) collective-permute-start(bf16[8,8,1280]{2,1,0:T(8,128)(2,1)S(1)} %slice.24), channel_id=1, source_target_pairs={{0,6},{2,0},{4,2},{6,4},{1,7},{3,1},{5,3},{7,5},{8,14},{10,8},{12,... | collective-permute-start | bytes 491528 | tf_op jit(solution)/shard_map/ppermute | solution.py:31
  66.2 3.1 %collective-permute-start.4 = (bf16[4,16,8,1280]{3,2,1,0:T(8,128)(2,1)S(1)}, bf16[4,16,8,1280]{3,2,1,0:T(8,128)(2,1)S(1)}, u32[]{:S(2)}, u32[]{:S(2)}) collective-permute-start(bf16[4,16,8,1280]{3,2,1,0:T(8,128)(2,1)S(1)} %bitcast.25), channel_id=1, source_target_pairs={{0,1},{1,0},{2,3},{3,2},{4,5},{5,4},{6,7},{7,6},{8,9},{9,8},{10,11... | collective-permute-start | bytes 3932168 | tf_op jit(solution)/shard_map/ppermute | solution.py:31
  85.9 3.1 %collective-permute-start.16 = (bf16[4,16,8,1280]{3,2,1,0:T(8,128)(2,1)S(1)}, bf16[4,16,8,1280]{3,2,1,0:T(8,128)(2,1)S(1)}, u32[]{:S(2)}, u32[]{:S(2)}) collective-permute-start(bf16[4,16,8,1280]{3,2,1,0:T(8,128)(2,1)S(1)} %get-tuple-element.32), channel_id=1, source_target_pairs={{0,1},{1,0},{2,3},{3,2},{4,5},{5,4},{6,7},{7,6},{8,9},{9,8},{10,11... | collective-permute-start | bytes 3932168 | tf_op jit(solution)/shard_map/ppermute | solution.py:31
  113.9 65.3 %all-to-all-start.2 = ((bf16[64,8,1280]{2,1,0:T(8,128)(2,1)}), bf16[64,8,1280]{2,1,0:T(8,128)(2,1)S(1)}, u32[]{:S(2)}, u32[]{:S(2)}) async-start(bf16[64,8,1280]{2,1,0:T(8,128)(2,1)} %pack.1), calls=%async_computation.2 | async-start | bytes 2621440 | tf_op jit(solution)/shard_map/all_to_all | solution.py:370
  127.5 13.1 %collective-permute-start.5 = (bf16[4,40,1024]{2,1,0:T(8,128)(2,1)S(1)}, bf16[4,40,1024]{2,1,0:T(8,128)(2,1)S(1)}, u32[]{:S(2)}, u32[]{:S(2)}) collective-permute-start(bf16[4,40,1024]{2,1,0:T(8,128)(2,1)S(1)} %get-tuple-element.28), channel_id=1, source_target_pairs={{0,8},{8,16},{16,24},{24,0},{1,9},{9,17},{17,25},{25,1},{2,10},{10... | collective-permute-start | bytes 983048 | tf_op jit(solution)/shard_map/ppermute | solution.py:31
  129.1 14.1 %collective-permute-start.7 = (bf16[4,40,1024]{2,1,0:T(8,128)(2,1)S(1)}, bf16[4,40,1024]{2,1,0:T(8,128)(2,1)S(1)}, u32[]{:S(2)}, u32[]{:S(2)}) collective-permute-start(bf16[4,40,1024]{2,1,0:T(8,128)(2,1)S(1)} %get-tuple-element.30), channel_id=1, source_target_pairs={{0,24},{8,0},{16,8},{24,16},{1,25},{9,1},{17,9},{25,17},{2,26},{10... | collective-permute-start | bytes 983048 | tf_op jit(solution)/shard_map/ppermute | solution.py:31
  140.8 19.0 %collective-permute-start.6 = (bf16[8,40,1024]{2,1,0:T(8,128)(2,1)S(1)}, bf16[8,40,1024]{2,1,0:T(8,128)(2,1)S(1)}, u32[]{:S(2)}, u32[]{:S(2)}) collective-permute-start(bf16[8,40,1024]{2,1,0:T(8,128)(2,1)S(1)} %add_convert_fusion.3), channel_id=1, source_target_pairs={{0,8},{8,16},{16,24},{24,0},{1,9},{9,17},{17,25},{25,1},{2,10},{10... | collective-permute-start | bytes 1966088 | tf_op jit(solution)/shard_map/ppermute | solution.py:31
  144.2 17.6 %collective-permute-start.8 = (bf16[8,40,1024]{2,1,0:T(8,128)(2,1)}, bf16[8,40,1024]{2,1,0:T(8,128)(2,1)}, u32[]{:S(2)}, u32[]{:S(2)}) collective-permute-start(bf16[8,40,1024]{2,1,0:T(8,128)(2,1)} %add_convert_fusion.2), channel_id=1, source_target_pairs={{0,24},{8,0},{16,8},{24,16},{1,25},{9,1},{17,9},{25,17},{2,26},{10... | collective-permute-start | bytes 1966088 | tf_op jit(solution)/shard_map/ppermute | solution.py:31
  163.3 10.8 %collective-permute-start.10 = (bf16[40,1024]{1,0:T(8,128)(2,1)S(1)}, bf16[40,1024]{1,0:T(8,128)(2,1)S(1)}, u32[]{:S(2)}, u32[]{:S(2)}) collective-permute-start(bf16[40,1024]{1,0:T(8,128)(2,1)S(1)} %get-tuple-element.46), channel_id=1, source_target_pairs={{0,96},{32,128},{64,160},{96,192},{128,224},{160,0},{192,32},{224,... | collective-permute-start | bytes 245768 | tf_op jit(solution)/shard_map/ppermute | solution.py:31
  165.5 10.3 %collective-permute-start.11 = (bf16[40,1024]{1,0:T(8,128)(2,1)S(1)}, bf16[40,1024]{1,0:T(8,128)(2,1)S(1)}, u32[]{:S(2)}, u32[]{:S(2)}) collective-permute-start(bf16[40,1024]{1,0:T(8,128)(2,1)S(1)} %get-tuple-element.45), channel_id=1, source_target_pairs={{0,160},{32,192},{64,224},{96,0},{128,32},{160,64},{192,96},{224,1... | collective-permute-start | bytes 245768 | tf_op jit(solution)/shard_map/ppermute | solution.py:31
  168.4 13.1 %collective-permute-start.12 = (bf16[40,1024]{1,0:T(8,128)(2,1)S(1)}, bf16[40,1024]{1,0:T(8,128)(2,1)S(1)}, u32[]{:S(2)}, u32[]{:S(2)}) collective-permute-start(bf16[40,1024]{1,0:T(8,128)(2,1)S(1)} %get-tuple-element.44), channel_id=1, source_target_pairs={{0,64},{32,96},{64,128},{96,160},{128,192},{160,224},{192,0},{224,... | collective-permute-start | bytes 245768 | tf_op jit(solution)/shard_map/ppermute | solution.py:31
  169.6 11.9 %collective-permute-start.13 = (bf16[40,1024]{1,0:T(8,128)(2,1)S(1)}, bf16[40,1024]{1,0:T(8,128)(2,1)S(1)}, u32[]{:S(2)}, u32[]{:S(2)}) collective-permute-start(bf16[40,1024]{1,0:T(8,128)(2,1)S(1)} %get-tuple-element.43), channel_id=1, source_target_pairs={{0,192},{32,224},{64,0},{96,32},{128,64},{160,96},{192,128},{224,1... | collective-permute-start | bytes 245768 | tf_op jit(solution)/shard_map/ppermute | solution.py:31
  172.5 9.0 %collective-permute-start.14 = (bf16[40,1024]{1,0:T(8,128)(2,1)S(1)}, bf16[40,1024]{1,0:T(8,128)(2,1)S(1)}, u32[]{:S(2)}, u32[]{:S(2)}) collective-permute-start(bf16[40,1024]{1,0:T(8,128)(2,1)S(1)} %get-tuple-element.42), channel_id=1, source_target_pairs={{0,32},{32,64},{64,96},{96,128},{128,160},{160,192},{192,224},{224... | collective-permute-start | bytes 245768 | tf_op jit(solution)/shard_map/ppermute | solution.py:31
  174.1 7.5 %collective-permute-start.15 = (bf16[40,1024]{1,0:T(8,128)(2,1)S(1)}, bf16[40,1024]{1,0:T(8,128)(2,1)S(1)}, u32[]{:S(2)}, u32[]{:S(2)}) collective-permute-start(bf16[40,1024]{1,0:T(8,128)(2,1)S(1)} %get-tuple-element.41), channel_id=1, source_target_pairs={{0,224},{32,0},{64,32},{96,64},{128,96},{160,128},{192,160},{224,1... | collective-permute-start | bytes 245768 | tf_op jit(solution)/shard_map/ppermute | solution.py:31
  175.8 8.5 %collective-permute-start.9 = (bf16[40,1024]{1,0:T(8,128)(2,1)S(1)}, bf16[40,1024]{1,0:T(8,128)(2,1)S(1)}, u32[]{:S(2)}, u32[]{:S(2)}) collective-permute-start(bf16[40,1024]{1,0:T(8,128)(2,1)S(1)} %get-tuple-element.47), channel_id=1, source_target_pairs={{0,128},{32,160},{64,192},{96,224},{128,0},{160,32},{192,64},{224,... | collective-permute-start | bytes 245768 | tf_op jit(solution)/shard_map/ppermute | solution.py:31

commit v5 on v4

--- a/solution.py
+++ b/solution.py
@@ -1,3 +1,5 @@
+import functools
+
 import jax
 import jax.numpy as jnp
 from jax import lax
@@ -10,7 +12,6 @@
 GAP = 32
 WIN = 4
 SUB = 8
-OFFSETS = (0, 3, 1, 2)
 MAIN_MIB = 36
 WEIGHT_MIB = 24
 SHELF = 16384
@@ -55,14 +56,19 @@
     return pl.BlockSpec(memory_space=pltpu.SMEM)
 
 
-def spread_kernel(sent_ref, me_ref, lat_ref, out_ref):
+def spread_kernel(sent_ref, me_ref, lat_any, out_ref, lat_ref, sem):
+    at = pl.ds(pl.multiple_of(me_ref[0] * SUB, SUB), SUB)
+    load = pltpu.make_async_copy(lat_any.at[:, at], lat_ref, sem)
+    load.start()
+    load.wait()
+
     @pl.loop(0, out_ref.shape[0], unroll=4)
     def _(e):
         out_ref[e] = lat_ref[jnp.maximum(sent_ref[e], 0)]
 
 
 def main_kernel(
-    start_ref, pos_ref, mine_any, other_any, wk_any, wv_any, q_any, g_any, slot_ref,
+    start_ref, mine_any, other_any, wk_any, wv_any, q_any, g_any, slot_ref,
     att_ref, dq_ref, keep_ref, give_ref, shelf_any,
     mine_ref, other_ref, wk_ref, wv_ref, q_ref, g_ref,
     lat_ref, k_ref, v_ref, acc_ref, bg_ref, in_sem, mine_sem, other_sem, lat_sem, bg_sem,
@@ -74,7 +80,6 @@
     heads = cols // DH
     chunk = WIN * rows
     chunks = vis // WIN
-    my_x = pos_ref[0]
 
     def part_in(src, dst, sem, i):
         at = pl.ds(i * WIN, WIN)
@@ -162,10 +167,8 @@
         out = mm(grad[:, :cols], wk_ref[...], NT) + mm(grad[:, cols:], wv_ref[...], NT)
         for s in range(WIN):
             piece = out[s * rows:(s + 1) * rows].reshape(rows // SUB, SUB, width).astype(BF)
-            for r, off in enumerate(OFFSETS):
-                there = lax.rem(my_x + off, nx)
-                keep_ref[there, i * WIN + s] = piece[r]
-                give_ref[there, i * WIN + s] = piece[nx + r]
+            keep_ref[:, i * WIN + s] = piece[:nx]
+            give_ref[:, i * WIN + s] = piece[nx:]
 
     for n in range(chunks):
         part_out(lat_ref, 0, lat_sem, n).wait()
@@ -173,55 +176,38 @@
 
 
 def weight_kernel(
-    y_ref, shelf_any, own_ref, next_ref, fa_ref, fb_ref, prev_ref,
+    base, y_ref, shelf_any, own_ref, next_ref, far_ref, prev_ref,
     lat_ref, bg_ref, t_ref, sum_ref, lat_sem, bg_sem,
 ):
     nz, part, cols = own_ref.shape
-    halves, keys, half = lat_ref.shape
-    ny = halves * half // (nz * part)
+    keys, half = lat_ref.shape
+    ny = half // (nz * part)
     my_y = y_ref[0]
     step = 256
-    zh = nz // 2
-    loads = [
-        pltpu.make_async_copy(
-            shelf_any.at[pl.ds(0, keys), pl.ds(j * half, half)], lat_ref.at[j], lat_sem.at[j]
-        )
-        for j in range(halves)
-    ]
+    load = pltpu.make_async_copy(shelf_any.at[pl.ds(0, keys), pl.ds(base, half)], lat_ref, lat_sem)
     rest = pltpu.make_async_copy(shelf_any.at[pl.ds(keys, keys), pl.ds(0, cols)], bg_ref, bg_sem)
-    loads[0].start()
+    load.start()
     rest.start()
-    for load in loads[1:]:
-        load.start()
-    for j in range(halves):
-        loads[j].wait()
-        t_ref[...] = lat_ref[j].T
-        if j == 0:
-            rest.wait()
-
-        @pl.loop(0, cols // step)
-        def _(n):
-            at = pl.ds(pl.multiple_of(n * step, step), step)
-            sum_ref[j * half:(j + 1) * half, at] = mm(t_ref[...], bg_ref[:, at], NN)
-
-    def block(z, rel):
+    load.wait()
+    t_ref[...] = lat_ref[...].T
+    rest.wait()
+
+    @pl.loop(0, cols // step)
+    def _(n):
+        at = pl.ds(pl.multiple_of(n * step, step), step)
+        sum_ref[:, at] = mm(t_ref[...], bg_ref[:, at], NN)
+
+    for rel, out_ref in enumerate((own_ref, next_ref, far_ref, prev_ref)):
         there = lax.rem(my_y + rel, ny)
-        return sum_ref[pl.ds(pl.multiple_of((z * ny + there) * part, SUB), part), :].astype(BF)
-
-    for z in range(nz):
-        own_ref[z] = block(z, 0)
-        next_ref[z] = block(z, 1)
-        prev_ref[z] = block(z, 3)
-        if z < zh:
-            fa_ref[z] = block(z, 2)
-        else:
-            fb_ref[z - zh] = block(z, 2)
-
-
-def pack_kernel(place_ref, got_ref, out_ref):
-    total = got_ref[0].astype(F32)
-    for r in range(1, got_ref.shape[0]):
-        total = total + got_ref[r].astype(F32)
+        for z in range(nz):
+            rows = pl.ds(pl.multiple_of((z * ny + there) * part, SUB), part)
+            out_ref[z] = sum_ref[rows, :].astype(BF)
+
+
+def pack_kernel(place_ref, own_ref, left_ref, right_ref, far_ref, out_ref):
+    total = own_ref[...].astype(F32)
+    for got_ref in (left_ref, right_ref, far_ref):
+        total = total + got_ref[...].astype(F32)
     total = total.astype(BF)
     for v in range(total.shape[0]):
         place = place_ref[v]
@@ -259,12 +245,9 @@
     send = pl.pallas_call(
         spread_kernel,
         name="spread",
-        grid_spec=pltpu.PrefetchScalarGridSpec(
-            num_scalar_prefetch=2,
-            grid=(1,),
-            in_specs=[pl.BlockSpec((images, SUB, width), lambda i, a, b: (0, b[0], 0))],
-            out_specs=pl.BlockSpec((slots_total, SUB, width), lambda i, a, b: (0, 0, 0)),
-        ),
+        in_specs=[smem(), smem(), far()],
+        out_specs=vmem(),
+        scratch_shapes=[pltpu.VMEM((images, SUB, width), BF), pltpu.SemaphoreType.DMA],
         out_shape=jax.ShapeDtypeStruct((slots_total, SUB, width), BF),
         compiler_params=grant(8),
     )(sent, me, latents)
@@ -285,11 +268,9 @@
     start = jnp.minimum(jnp.maximum(slot_rows[:, 0, 0], 0), vis - WIN)
     keys = vis * lat_rows
     zh = nz // 2
-    x_here = lax.axis_index("x").reshape(1).astype(jnp.int32)
     y_here = lax.axis_index("y").reshape(1).astype(jnp.int32)
     tokens_out = jax.ShapeDtypeStruct((tokens, cols), BF)
     rows_out = jax.ShapeDtypeStruct((nx, vis, SUB, width), BF)
-    full = jax.ShapeDtypeStruct((nz, part, 2 * cols), BF)
     split = jax.ShapeDtypeStruct((zh, part, 2 * cols), BF)
     chunks = vis // WIN
     att, dq, keep, give, shelf = pl.pallas_call(
@@ -299,7 +280,7 @@
             tokens_out, tokens_out, rows_out, rows_out,
             jax.ShapeDtypeStruct((SHELF, width), BF),
         ),
-        in_specs=[smem(), smem()] + [anywhere()] * 2 + [far()] * 4 + [vmem()],
+        in_specs=[smem()] + [anywhere()] * 2 + [far()] * 4 + [vmem()],
         out_specs=(vmem(), vmem(), vmem(), vmem(), far()),
         scratch_shapes=[
             pltpu.VMEM((nx, vis, SUB, width), BF),
@@ -325,48 +306,54 @@
             bytes_accessed=16 * 1024 * 1024,
             transcendentals=tokens * 4 * 256,
         ),
-    )(start, x_here, mine, other, key_weight, value_weight, queries, grad_out, slot_rows)
+    )(start, mine, other, key_weight, value_weight, queries, grad_out, slot_rows)
 
     swapped = shift(give, "core", 1, 2)
-    crossed = lax.all_to_all(add2(keep, swapped), "x", split_axis=0, concat_axis=0, tiled=True)
-    gw_own, gw_next, gw_fa, gw_fb, gw_prev = pl.pallas_call(
-        weight_kernel,
-        name="weights",
-        out_shape=(full, full, split, split, full),
-        in_specs=[smem(), far()],
-        out_specs=tuple([vmem()] * 5),
-        scratch_shapes=[
-            pltpu.VMEM((2, keys, width // 2), BF),
-            pltpu.VMEM((keys, 2 * cols), BF),
-            pltpu.VMEM((width // 2, keys), BF),
-            pltpu.VMEM((width, 2 * cols), F32),
-            pltpu.SemaphoreType.DMA((2,)),
-            pltpu.SemaphoreType.DMA,
-        ],
-        compiler_params=grant(WEIGHT_MIB),
-        cost_estimate=pl.CostEstimate(
-            flops=4 * keys * width * cols, bytes_accessed=8 * 1024 * 1024, transcendentals=0
-        ),
-    )(y_here, shelf)
-    gw_up = shift(gw_fa, "y", 1, ny)
-    gw_down = shift(gw_fb, "y", -1, ny)
-
-    gw_next = (gw_next.astype(F32)
-               + jnp.concatenate([gw_up, jnp.zeros_like(gw_up)], axis=0).astype(F32)).astype(BF)
-    gw_prev = (gw_prev.astype(F32)
-               + jnp.concatenate([jnp.zeros_like(gw_down), gw_down], axis=0).astype(F32)).astype(BF)
+
+    def heavy(n):
+        return pl.pallas_call(
+            functools.partial(weight_kernel, n * (width // 2)),
+            out_shape=(split,) * 4,
+            in_specs=[smem(), far()],
+            out_specs=(vmem(),) * 4,
+            scratch_shapes=[
+                pltpu.VMEM((keys, width // 2), BF),
+                pltpu.VMEM((keys, 2 * cols), BF),
+                pltpu.VMEM((width // 2, keys), BF),
+                pltpu.VMEM((width // 2, 2 * cols), F32),
+                pltpu.SemaphoreType.DMA,
+                pltpu.SemaphoreType.DMA,
+            ],
+            compiler_params=grant(WEIGHT_MIB),
+            cost_estimate=pl.CostEstimate(
+                flops=2 * keys * width * cols, bytes_accessed=6 * 1024 * 1024, transcendentals=0
+            ),
+        )(y_here, shelf)
+
+    own_a, next_a, far_a, prev_a = heavy(0)
+    own_b, next_b, far_b, prev_b = heavy(1)
+    summed = [add2(keep[r], swapped[r]) for r in range(nx)]
+    from_far = shift(summed[3], "x", 2, nx)
+    from_left = shift(summed[2], "x", 1, nx)
+    from_right = shift(summed[1], "x", -1, nx)
+
+    gw_up = shift(far_a, "y", 1, ny)
+    gw_down = shift(far_b, "y", -1, ny)
+    gw_next = jnp.concatenate([add2(next_a, gw_up), next_b], axis=0)
+    gw_prev = jnp.concatenate([prev_a, add2(prev_b, gw_down)], axis=0)
     gw_l = shift(gw_next, "y", 1, ny)
     gw_r = shift(gw_prev, "y", -1, ny)
+    gw_own = jnp.concatenate([own_a, own_b], axis=0)
     gw_y = (gw_own.astype(F32) + gw_l.astype(F32) + gw_r.astype(F32)).astype(BF)
 
     back = pl.pallas_call(
         pack_kernel,
         name="pack",
         out_shape=jax.ShapeDtypeStruct((slots_total, SUB, width), BF),
-        in_specs=[smem(), vmem()],
+        in_specs=[smem()] + [vmem()] * 4,
         out_specs=vmem(),
         compiler_params=grant(8),
-    )(places, crossed)
+    )(places, summed[0], from_left, from_right, from_far)
     returned = lax.all_to_all(back, seq, split_axis=0, concat_axis=0, tiled=True)
 
     z_here = lax.axis_index("z")

time: 188 us -> 185 us (0.984); the launches traced: 185 us -> 184 us
  blocking collectives: 22.6 us -> 0 us
  waiting for transfers between devices: 79.8 us -> 91.4 us
  starting transfers between devices: 45.3 us -> 51.8 us
    all_to_all x1 -> x0, blocking collectives: 22.6 us -> none  [local(): lax.all_to_all(add2(keep, swapped), 'x', split_axis=0, concat_axis=0, til...]
    ppermute x17 -> x20, waiting for transfers between devices: 46.9 us -> 58.6 us  [shift(): return lax.ppermute(v, axis, [(i, (i + step) % size) for i in range(size)])]
    ppermute x17 -> x20, starting transfers between devices: 26.7 us -> 33.3 us  [shift(): return lax.ppermute(v, axis, [(i, (i + step) % size) for i in range(size)])]
    pallas_call x2 -> x3, Pallas kernels: 8.68 us -> 10.3 us  [the longest x2 8.4 us: heavy(): pl.pallas_call(functools.partial(weight_kernel, n * (width // 2)), out_sh...]
  transfers between devices with their start and end apart: 19 -> 22, of which waited for: 10 -> 13; matrix products, arithmetic and copies ran while one was open for 2% -> 2% of each run, Pallas kernels for 5% -> 6%
where the time goes in v5:
time: 185 us; the launch traced here: 184 us
  waiting for transfers between devices  91.4 us (49%)
  starting transfers between devices  51.8 us (28%)
  Pallas kernels  31.3 us (17%)
  local copies, waits for them, and re-layouts  4.69 us (3%)
  other arithmetic  4.02 us (2%)
    ppermute x20, waiting for transfers between devices, shift(): return lax.ppermute(v, axis, [(i, (i + step) % size) for i in range(size)])  58.6 us
    ppermute x20, starting transfers between devices, shift(): return lax.ppermute(v, axis, [(i, (i + step) % size) for i in range(size)])  33.3 us
    all_to_all x1, waiting for transfers between devices, local(): got = lax.all_to_all(send, seq, split_axis=0, concat_axis=0, tiled=True)  32.9 us
    pallas_call x1, Pallas kernels, local(): pl.pallas_call(main_kernel, name='main', out_shape=(tokens_out, tokens_ou...  16.7 us
    all_to_all x1, starting transfers between devices, local(): got = lax.all_to_all(send, seq, split_axis=0, concat_axis=0, tiled=True)  11.7 us
    pallas_call x2, Pallas kernels, heavy(): pl.pallas_call(functools.partial(weight_kernel, n * (width // 2)), out_sh...  8.4 us
    all_to_all x1, starting transfers between devices, local(): lax.all_to_all(back, seq, split_axis=0, concat_axis=0, tiled=True)  6.71 us
  transfers between devices with their start and end apart: 22, of which 13 were waited for; matrix products, arithmetic and copies ran while one was open for 2% of the time, Pallas kernels for 6%

profile of v5, /device:TPU:8, one launch (start us, length us, event | category | flops | bytes accessed | tf_op | source)
XLA Modules:
  0.0 184.1 jit_solution(3334840630053967749)
XLA Ops:
  3.1 1.9 %spread.1 = bf16[64,8,1280]{2,1,0:T(8,128)(2,1)} custom-call(s32[64]{0:T(128)S(1)} %reshape_squeeze.3.sent_ref, s32[1]{0:T(128)} %bitcast.1.me_ref, bf16[12,64,1280]{2,1,0:T(8,128)(2,1)S(1)} %copy-done), custom_call_target="tpu_custom_call" | custom-call | tf_op jit(solution)/shard_map/spread/pallas_call | solution.py:245
  4.9 11.7 %all-to-all-start = ((bf16[64,8,1280]{2,1,0:T(8,128)(2,1)}), bf16[64,8,1280]{2,1,0:T(8,128)(2,1)S(1)}, u32[]{:S(2)}, u32[]{:S(2)}) async-start(bf16[64,8,1280]{2,1,0:T(8,128)(2,1)} %spread.1), calls=%async_computation | async-start | bytes 2621440 | tf_op jit(solution)/shard_map/all_to_all | solution.py:254
  16.7 32.9 %all-to-all-done = bf16[64,8,1280]{2,1,0:T(8,128)(2,1)S(1)} async-done(((bf16[64,8,1280]{2,1,0:T(8,128)(2,1)}), bf16[64,8,1280]{2,1,0:T(8,128)(2,1)S(1)}, u32[]{:S(2)}, u32[]{:S(2)}) %all-to-all-start) | async-done | bytes 1310752 | tf_op jit(solution)/shard_map/all_to_all | solution.py:254
  50.1 1.6 collective-permute-start
  51.7 1.7 collective-permute-start.1
  53.5 5.9 %collective-permute-done = bf16[16,8,1280]{2,1,0:T(8,128)(2,1)S(1)} collective-permute-done((bf16[16,8,1280]{2,1,0:T(8,128)(2,1)S(1)}, bf16[16,8,1280]{2,1,0:T(8,128)(2,1)S(1)}, u32[]{:S(2)}, u32[]{:S(2)}) %collective-permute-start) | collective-permute-done | bytes 327712 | tf_op jit(solution)/shard_map/ppermute | solution.py:32
  59.8 3.0 %collective-permute-start.3 = (bf16[8,8,1280]{2,1,0:T(8,128)(2,1)S(1)}, bf16[8,8,1280]{2,1,0:T(8,128)(2,1)S(1)}, u32[]{:S(2)}, u32[]{:S(2)}) collective-permute-start(bf16[8,8,1280]{2,1,0:T(8,128)(2,1)S(1)} %slice.56), channel_id=1, source_target_pairs={{0,6},{2,0},{4,2},{6,4},{1,7},{3,1},{5,3},{7,5},{8,14},{10,8},{12,... | collective-permute-start | bytes 491528 | tf_op jit(solution)/shard_map/ppermute | solution.py:32
  62.9 3.1 %collective-permute-done.2 = bf16[8,8,1280]{2,1,0:T(8,128)(2,1)S(1)} collective-permute-done((bf16[8,8,1280]{2,1,0:T(8,128)(2,1)S(1)}, bf16[8,8,1280]{2,1,0:T(8,128)(2,1)S(1)}, u32[]{:S(2)}, u32[]{:S(2)}) %collective-permute-start.2) | collective-permute-done | bytes 163872 | tf_op jit(solution)/shard_map/ppermute | solution.py:32
  66.4 2.9 %collective-permute-done.4.other_any = bf16[4,16,8,1280]{3,2,1,0:T(8,128)(2,1)S(1)} collective-permute-done((bf16[4,16,8,1280]{3,2,1,0:T(8,128)(2,1)S(1)}, bf16[4,16,8,1280]{3,2,1,0:T(8,128)(2,1)S(1)}, u32[]{:S(2)}, u32[]{:S(2)}) %collective-permute-start.4) | collective-permute-done | bytes 1310752 | tf_op jit(solution)/shard_map/ppermute | solution.py:32
  69.3 16.7 %main.1 = (bf16[512,512]{1,0:T(8,128)(2,1)}, bf16[512,512]{1,0:T(8,128)(2,1)}, bf16[4,16,8,1280]{3,2,1,0:T(8,128)(2,1)S(1)}, bf16[4,16,8,1280]{3,2,1,0:T(8,128)(2,1)S(1)}, bf16[16384,1280]{1,0:T(8,128)(2,1)}) custom-call(s32[4]{0:T(128)S(1)} %fusion.10.start_ref, bf16[4,16,8,1280]{3,2,1,0:T(8,128)(2,1)S(1)} %bitcast.33, ...), custom_call_target="tpu_custom_call" | custom-call | flops 6442450944 | bytes 16777216 | tf_op jit(solution)/shard_map/main/pallas_call | solution.py:276
  86.2 2.9 %collective-permute-done.16 = bf16[4,16,8,1280]{3,2,1,0:T(8,128)(2,1)S(1)} collective-permute-done((bf16[4,16,8,1280]{3,2,1,0:T(8,128)(2,1)S(1)}, bf16[4,16,8,1280]{3,2,1,0:T(8,128)(2,1)S(1)}, u32[]{:S(2)}, u32[]{:S(2)}) %collective-permute-start.16) | collective-permute-done | bytes 1310752 | tf_op jit(solution)/shard_map/ppermute | solution.py:32
  90.1 2.8 %collective-permute-start.18 = (bf16[16,8,1280]{2,1,0:T(8,128)(2,1)S(1)}, bf16[16,8,1280]{2,1,0:T(8,128)(2,1)S(1)}, u32[]{:S(2)}, u32[]{:S(2)}) collective-permute-start(bf16[16,8,1280]{2,1,0:T(8,128)(2,1)S(1)} %get-tuple-element.48), channel_id=1, source_target_pairs={{0,6},{2,0},{4,2},{6,4},{1,7},{3,1},{5,3},{7,5},{8,14},{10,8},{12,... | collective-permute-start | bytes 983048 | tf_op jit(solution)/shard_map/ppermute | solution.py:32
  94.2 6.5 %collective-permute-done.17.left_ref = bf16[16,8,1280]{2,1,0:T(8,128)(2,1)S(1)} collective-permute-done((bf16[16,8,1280]{2,1,0:T(8,128)(2,1)S(1)}, bf16[16,8,1280]{2,1,0:T(8,128)(2,1)S(1)}, u32[]{:S(2)}, u32[]{:S(2)}) %collective-permute-start.17) | collective-permute-done | bytes 327712 | tf_op jit(solution)/shard_map/ppermute | solution.py:32
  100.8 6.4 %collective-permute-done.18.right_ref = bf16[16,8,1280]{2,1,0:T(8,128)(2,1)S(1)} collective-permute-done((bf16[16,8,1280]{2,1,0:T(8,128)(2,1)S(1)}, bf16[16,8,1280]{2,1,0:T(8,128)(2,1)S(1)}, u32[]{:S(2)}, u32[]{:S(2)}) %collective-permute-start.18) | collective-permute-done | bytes 327712 | tf_op jit(solution)/shard_map/ppermute | solution.py:32
  107.2 1.8 collective-permute-done.19.far_ref
  109.0 2.0 %pack.1 = bf16[64,8,1280]{2,1,0:T(8,128)(2,1)} custom-call(s32[16]{0:T(128)S(1)} %bitcast.36, bf16[16,8,1280]{2,1,0:T(8,128)(2,1)S(1)} %get-tuple-element.50.own_ref, bf16[16,8,1280]{2,1,0:T(8,128)(2,1)S(1)} %collective-permute-done.17.left_ref, bf16[16,8,1280]{2,1,0:T(8,128)(2,1)S(1)} %collective-permute-done.18.right_ref, ...), custom_call_target="tpu_custom_call" | custom-call | tf_op jit(solution)/shard_map/pack/pallas_call | solution.py:349
  111.0 6.7 %all-to-all-start.1 = ((bf16[64,8,1280]{2,1,0:T(8,128)(2,1)}), bf16[64,8,1280]{2,1,0:T(8,128)(2,1)S(1)}, u32[]{:S(2)}, u32[]{:S(2)}) async-start(bf16[64,8,1280]{2,1,0:T(8,128)(2,1)} %pack.1), calls=%async_computation.1 | async-start | bytes 2621440 | tf_op jit(solution)/shard_map/all_to_all | solution.py:357
  117.7 4.2 %shard_map.119 = (bf16[4,40,1024]{2,1,0:T(8,128)(2,1)S(1)}, bf16[4,40,1024]{2,1,0:T(8,128)(2,1)S(1)}, bf16[4,40,1024]{2,1,0:T(8,128)(2,1)S(1)}, bf16[4,40,1024]{2,1,0:T(8,128)(2,1)S(1)}) custom-call(s32[1]{0:T(128)} %bitcast.4.y_ref, bf16[16384,1280]{1,0:T(8,128)(2,1)} %get-tuple-element.28.shelf_any), custom_call_target="tpu_custom_call" | custom-call | flops 1342177280 | bytes 6291456 | tf_op jit(solution)/shard_map/pallas_call | solution.py:314
  123.5 4.2 %shard_map.120 = (bf16[4,40,1024]{2,1,0:T(8,128)(2,1)S(1)}, bf16[4,40,1024]{2,1,0:T(8,128)(2,1)S(1)}, bf16[4,40,1024]{2,1,0:T(8,128)(2,1)S(1)}, bf16[4,40,1024]{2,1,0:T(8,128)(2,1)S(1)}) custom-call(s32[1]{0:T(128)} %bitcast.4.y_ref, bf16[16384,1280]{1,0:T(8,128)(2,1)} %get-tuple-element.28.shelf_any), custom_call_target="tpu_custom_call" | custom-call | flops 1342177280 | bytes 6291456 | tf_op jit(solution)/shard_map/pallas_call | solution.py:314
  128.3 6.6 %collective-permute-done.5 = bf16[4,40,1024]{2,1,0:T(8,128)(2,1)S(1)} collective-permute-done((bf16[4,40,1024]{2,1,0:T(8,128)(2,1)S(1)}, bf16[4,40,1024]{2,1,0:T(8,128)(2,1)S(1)}, u32[]{:S(2)}, u32[]{:S(2)}) %collective-permute-start.5) | collective-permute-done | bytes 327712 | tf_op jit(solution)/shard_map/ppermute | solution.py:32
  136.0 2.5 %collective-permute-start.6 = (bf16[8,40,1024]{2,1,0:T(8,128)(2,1)}, bf16[8,40,1024]{2,1,0:T(8,128)(2,1)S(1)}, u32[]{:S(2)}, u32[]{:S(2)}) collective-permute-start(bf16[8,40,1024]{2,1,0:T(8,128)(2,1)} %pad_maximum_fusion), channel_id=1, source_target_pairs={{0,8},{8,16},{16,24},{24,0},{1,9},{9,17},{17,25},{25,1},{2,10},{10... | collective-permute-start | bytes 1966088 | tf_op jit(solution)/shard_map/ppermute | solution.py:32
  138.4 2.4 %collective-permute-done.7 = bf16[4,40,1024]{2,1,0:T(8,128)(2,1)S(1)} collective-permute-done((bf16[4,40,1024]{2,1,0:T(8,128)(2,1)S(1)}, bf16[4,40,1024]{2,1,0:T(8,128)(2,1)S(1)}, u32[]{:S(2)}, u32[]{:S(2)}) %collective-permute-start.7) | collective-permute-done | bytes 327712 | tf_op jit(solution)/shard_map/ppermute | solution.py:32
  142.7 14.5 %collective-permute-done.6 = bf16[8,40,1024]{2,1,0:T(8,128)(2,1)S(1)} collective-permute-done((bf16[8,40,1024]{2,1,0:T(8,128)(2,1)}, bf16[8,40,1024]{2,1,0:T(8,128)(2,1)S(1)}, u32[]{:S(2)}, u32[]{:S(2)}) %collective-permute-start.6) | collective-permute-done | bytes 655392 | tf_op jit(solution)/shard_map/ppermute | solution.py:32
  157.1 2.1 %collective-permute-done.8 = bf16[8,40,1024]{2,1,0:T(8,128)(2,1)S(1)} collective-permute-done((bf16[8,40,1024]{2,1,0:T(8,128)(2,1)}, bf16[8,40,1024]{2,1,0:T(8,128)(2,1)S(1)}, u32[]{:S(2)}, u32[]{:S(2)}) %collective-permute-start.8) | collective-permute-done | bytes 655392 | tf_op jit(solution)/shard_map/ppermute | solution.py:32
  161.6 2.5 %collective-permute-start.10 = (bf16[40,1024]{1,0:T(8,128)(2,1)S(1)}, bf16[40,1024]{1,0:T(8,128)(2,1)S(1)}, u32[]{:S(2)}, u32[]{:S(2)}) collective-permute-start(bf16[40,1024]{1,0:T(8,128)(2,1)S(1)} %get-tuple-element.56), channel_id=1, source_target_pairs={{0,96},{32,128},{64,160},{96,192},{128,224},{160,0},{192,32},{224,... | collective-permute-start | bytes 245768 | tf_op jit(solution)/shard_map/ppermute | solution.py:32
  164.1 2.6 %collective-permute-start.11 = (bf16[40,1024]{1,0:T(8,128)(2,1)S(1)}, bf16[40,1024]{1,0:T(8,128)(2,1)S(1)}, u32[]{:S(2)}, u32[]{:S(2)}) collective-permute-start(bf16[40,1024]{1,0:T(8,128)(2,1)S(1)} %get-tuple-element.55), channel_id=1, source_target_pairs={{0,160},{32,192},{64,224},{96,0},{128,32},{160,64},{192,96},{224,1... | collective-permute-start | bytes 245768 | tf_op jit(solution)/shard_map/ppermute | solution.py:32
  167.7 3.1 %collective-permute-start.13 = (bf16[40,1024]{1,0:T(8,128)(2,1)S(1)}, bf16[40,1024]{1,0:T(8,128)(2,1)S(1)}, u32[]{:S(2)}, u32[]{:S(2)}) collective-permute-start(bf16[40,1024]{1,0:T(8,128)(2,1)S(1)} %get-tuple-element.53), channel_id=1, source_target_pairs={{0,192},{32,224},{64,0},{96,32},{128,64},{160,96},{192,128},{224,1... | collective-permute-start | bytes 245768 | tf_op jit(solution)/shard_map/ppermute | solution.py:32
  170.8 1.7 collective-permute-start.14
  172.5 1.5 collective-permute-start.15
  174.1 3.6 %collective-permute-start.9 = (bf16[40,1024]{1,0:T(8,128)(2,1)S(1)}, bf16[40,1024]{1,0:T(8,128)(2,1)S(1)}, u32[]{:S(2)}, u32[]{:S(2)}) collective-permute-start(bf16[40,1024]{1,0:T(8,128)(2,1)S(1)} %get-tuple-element.57), channel_id=1, source_target_pairs={{0,128},{32,160},{64,192},{96,224},{128,0},{160,32},{192,64},{224,... | collective-permute-start | bytes 245768 | tf_op jit(solution)/shard_map/ppermute | solution.py:32
  177.7 2.3 %collect.1 = f32[12,8,1280]{2,1,0:T(8,128)} custom-call(s32[64]{0:T(128)S(1)} %reshape_squeeze.3.sent_ref, bf16[64,8,1280]{2,1,0:T(8,128)(2,1)S(1)} %all-to-all-done.1.got_ref), custom_call_target="tpu_custom_call" | custom-call | tf_op jit(solution)/shard_map/collect/pallas_call | solution.py:366
  180.0 3.3 %collective-permute-done.9 = bf16[40,1024]{1,0:T(8,128)(2,1)S(1)} collective-permute-done((bf16[40,1024]{1,0:T(8,128)(2,1)S(1)}, bf16[40,1024]{1,0:T(8,128)(2,1)S(1)}, u32[]{:S(2)}, u32[]{:S(2)}) %collective-permute-start.9) | collective-permute-done | bytes 81952 | tf_op jit(solution)/shard_map/ppermute | solution.py:32
  (56 shorter events, 15.5 us)
Async XLA Ops:
  1.5 1.5 copy-start
  4.9 11.7 %copy-start.2 = (s32[1,16]{1,0:T(1,128)S(1)}, s32[1,16]{1,0:T(1,128)}, u32[]{:S(2)}) copy-start(s32[1,16]{1,0:T(1,128)} %param.12) | copy-start | bytes 196
  4.9 44.6 %all-to-all-start = ((bf16[64,8,1280]{2,1,0:T(8,128)(2,1)}), bf16[64,8,1280]{2,1,0:T(8,128)(2,1)S(1)}, u32[]{:S(2)}, u32[]{:S(2)}) async-start(bf16[64,8,1280]{2,1,0:T(8,128)(2,1)} %spread.1), calls=%async_computation | async-start | bytes 2621440 | tf_op jit(solution)/shard_map/all_to_all | solution.py:254
  49.6 19.7 %copy-start.6 = (bf16[512,512]{1,0:T(8,128)(2,1)S(1)}, bf16[512,512]{1,0:T(8,128)(2,1)}, u32[]{:S(2)}) copy-start(bf16[512,512]{1,0:T(8,128)(2,1)} %g_any.1) | copy-start | bytes 1572868
  50.1 9.3 %collective-permute-start = (bf16[16,8,1280]{2,1,0:T(8,128)(2,1)S(1)}, bf16[16,8,1280]{2,1,0:T(8,128)(2,1)S(1)}, u32[]{:S(2)}, u32[]{:S(2)}) collective-permute-start(bf16[16,8,1280]{2,1,0:T(8,128)(2,1)S(1)} %gather_fusion), channel_id=1, source_target_pairs={{0,2},{2,4},{4,6},{6,0},{1,3},{3,5},{5,7},{7,1},{8,10},{10,12},{12... | collective-permute-start | bytes 983048 | tf_op jit(solution)/shard_map/ppermute | solution.py:32
  51.7 8.1 %collective-permute-start.1 = (bf16[16,8,1280]{2,1,0:T(8,128)(2,1)S(1)}, bf16[16,8,1280]{2,1,0:T(8,128)(2,1)S(1)}, u32[]{:S(2)}, u32[]{:S(2)}) collective-permute-start(bf16[16,8,1280]{2,1,0:T(8,128)(2,1)S(1)} %gather_fusion), channel_id=1, source_target_pairs={{0,6},{2,0},{4,2},{6,4},{1,7},{3,1},{5,3},{7,5},{8,14},{10,8},{12,... | collective-permute-start | bytes 983048 | tf_op jit(solution)/shard_map/ppermute | solution.py:32
  53.5 15.8 %copy-start.5 = (bf16[512,512]{1,0:T(8,128)(2,1)S(1)}, bf16[512,512]{1,0:T(8,128)(2,1)}, u32[]{:S(2)}) copy-start(bf16[512,512]{1,0:T(8,128)(2,1)} %q_any.1) | copy-start | bytes 1572868
  53.5 12.7 %copy-start.1 = (s32[512]{0:T(512)S(1)}, s32[512]{0:T(512)}, u32[]{:S(2)}) copy-start(s32[512]{0:T(512)} %param.14) | copy-start | bytes 6148
  53.5 15.8 %copy-start.3 = (bf16[1280,512]{1,0:T(8,128)(2,1)S(1)}, bf16[1280,512]{1,0:T(8,128)(2,1)}, u32[]{:S(2)}) copy-start(bf16[1280,512]{1,0:T(8,128)(2,1)} %wk_any.1) | copy-start | bytes 3932164
  53.5 15.7 %copy-start.4 = (bf16[1280,512]{1,0:T(8,128)(2,1)S(1)}, bf16[1280,512]{1,0:T(8,128)(2,1)}, u32[]{:S(2)}) copy-start(bf16[1280,512]{1,0:T(8,128)(2,1)} %wv_any.1) | copy-start | bytes 3932164
  59.5 6.6 %collective-permute-start.2 = (bf16[8,8,1280]{2,1,0:T(8,128)(2,1)S(1)}, bf16[8,8,1280]{2,1,0:T(8,128)(2,1)S(1)}, u32[]{:S(2)}, u32[]{:S(2)}) collective-permute-start(bf16[8,8,1280]{2,1,0:T(8,128)(2,1)S(1)} %slice.55), channel_id=1, source_target_pairs={{0,2},{2,4},{4,6},{6,0},{1,3},{3,5},{5,7},{7,1},{8,10},{10,12},{12... | collective-permute-start | bytes 491528 | tf_op jit(solution)/shard_map/ppermute | solution.py:32
  59.8 6.2 %collective-permute-start.3 = (bf16[8,8,1280]{2,1,0:T(8,128)(2,1)S(1)}, bf16[8,8,1280]{2,1,0:T(8,128)(2,1)S(1)}, u32[]{:S(2)}, u32[]{:S(2)}) collective-permute-start(bf16[8,8,1280]{2,1,0:T(8,128)(2,1)S(1)} %slice.56), channel_id=1, source_target_pairs={{0,6},{2,0},{4,2},{6,4},{1,7},{3,1},{5,3},{7,5},{8,14},{10,8},{12,... | collective-permute-start | bytes 491528 | tf_op jit(solution)/shard_map/ppermute | solution.py:32
  66.1 3.1 %collective-permute-start.4 = (bf16[4,16,8,1280]{3,2,1,0:T(8,128)(2,1)S(1)}, bf16[4,16,8,1280]{3,2,1,0:T(8,128)(2,1)S(1)}, u32[]{:S(2)}, u32[]{:S(2)}) collective-permute-start(bf16[4,16,8,1280]{3,2,1,0:T(8,128)(2,1)S(1)} %bitcast.32), channel_id=1, source_target_pairs={{0,1},{1,0},{2,3},{3,2},{4,5},{5,4},{6,7},{7,6},{8,9},{9,8},{10,11... | collective-permute-start | bytes 3932168 | tf_op jit(solution)/shard_map/ppermute | solution.py:32
  86.0 3.1 %collective-permute-start.16 = (bf16[4,16,8,1280]{3,2,1,0:T(8,128)(2,1)S(1)}, bf16[4,16,8,1280]{3,2,1,0:T(8,128)(2,1)S(1)}, u32[]{:S(2)}, u32[]{:S(2)}) collective-permute-start(bf16[4,16,8,1280]{3,2,1,0:T(8,128)(2,1)S(1)} %get-tuple-element.38), channel_id=1, source_target_pairs={{0,1},{1,0},{2,3},{3,2},{4,5},{5,4},{6,7},{7,6},{8,9},{9,8},{10,11... | collective-permute-start | bytes 3932168 | tf_op jit(solution)/shard_map/ppermute | solution.py:32
  89.4 11.4 %collective-permute-start.17 = (bf16[16,8,1280]{2,1,0:T(8,128)(2,1)S(1)}, bf16[16,8,1280]{2,1,0:T(8,128)(2,1)S(1)}, u32[]{:S(2)}, u32[]{:S(2)}) collective-permute-start(bf16[16,8,1280]{2,1,0:T(8,128)(2,1)S(1)} %get-tuple-element.49), channel_id=1, source_target_pairs={{0,2},{2,4},{4,6},{6,0},{1,3},{3,5},{5,7},{7,1},{8,10},{10,12},{12... | collective-permute-start | bytes 983048 | tf_op jit(solution)/shard_map/ppermute | solution.py:32
  90.1 17.1 %collective-permute-start.18 = (bf16[16,8,1280]{2,1,0:T(8,128)(2,1)S(1)}, bf16[16,8,1280]{2,1,0:T(8,128)(2,1)S(1)}, u32[]{:S(2)}, u32[]{:S(2)}) collective-permute-start(bf16[16,8,1280]{2,1,0:T(8,128)(2,1)S(1)} %get-tuple-element.48), channel_id=1, source_target_pairs={{0,6},{2,0},{4,2},{6,4},{1,7},{3,1},{5,3},{7,5},{8,14},{10,8},{12,... | collective-permute-start | bytes 983048 | tf_op jit(solution)/shard_map/ppermute | solution.py:32
  92.9 16.1 %collective-permute-start.19 = (bf16[16,8,1280]{2,1,0:T(8,128)(2,1)S(1)}, bf16[16,8,1280]{2,1,0:T(8,128)(2,1)S(1)}, u32[]{:S(2)}, u32[]{:S(2)}) collective-permute-start(bf16[16,8,1280]{2,1,0:T(8,128)(2,1)S(1)} %get-tuple-element.47), channel_id=1, source_target_pairs={{0,4},{2,6},{4,0},{6,2},{1,5},{3,7},{5,1},{7,3},{8,12},{10,14},{12... | collective-permute-start | bytes 983048 | tf_op jit(solution)/shard_map/ppermute | solution.py:32
  111.0 66.7 %all-to-all-start.1 = ((bf16[64,8,1280]{2,1,0:T(8,128)(2,1)}), bf16[64,8,1280]{2,1,0:T(8,128)(2,1)S(1)}, u32[]{:S(2)}, u32[]{:S(2)}) async-start(bf16[64,8,1280]{2,1,0:T(8,128)(2,1)} %pack.1), calls=%async_computation.1 | async-start | bytes 2621440 | tf_op jit(solution)/shard_map/all_to_all | solution.py:357
  121.9 13.0 %collective-permute-start.5 = (bf16[4,40,1024]{2,1,0:T(8,128)(2,1)S(1)}, bf16[4,40,1024]{2,1,0:T(8,128)(2,1)S(1)}, u32[]{:S(2)}, u32[]{:S(2)}) collective-permute-start(bf16[4,40,1024]{2,1,0:T(8,128)(2,1)S(1)} %get-tuple-element.32), channel_id=1, source_target_pairs={{0,8},{8,16},{16,24},{24,0},{1,9},{9,17},{17,25},{25,1},{2,10},{10... | collective-permute-start | bytes 983048 | tf_op jit(solution)/shard_map/ppermute | solution.py:32
  127.7 13.2 %collective-permute-start.7 = (bf16[4,40,1024]{2,1,0:T(8,128)(2,1)S(1)}, bf16[4,40,1024]{2,1,0:T(8,128)(2,1)S(1)}, u32[]{:S(2)}, u32[]{:S(2)}) collective-permute-start(bf16[4,40,1024]{2,1,0:T(8,128)(2,1)S(1)} %get-tuple-element.36), channel_id=1, source_target_pairs={{0,24},{8,0},{16,8},{24,16},{1,25},{9,1},{17,9},{25,17},{2,26},{10... | collective-permute-start | bytes 983048 | tf_op jit(solution)/shard_map/ppermute | solution.py:32
  136.0 21.2 %collective-permute-start.6 = (bf16[8,40,1024]{2,1,0:T(8,128)(2,1)}, bf16[8,40,1024]{2,1,0:T(8,128)(2,1)S(1)}, u32[]{:S(2)}, u32[]{:S(2)}) collective-permute-start(bf16[8,40,1024]{2,1,0:T(8,128)(2,1)} %pad_maximum_fusion), channel_id=1, source_target_pairs={{0,8},{8,16},{16,24},{24,0},{1,9},{9,17},{17,25},{25,1},{2,10},{10... | collective-permute-start | bytes 1966088 | tf_op jit(solution)/shard_map/ppermute | solution.py:32
  141.8 17.4 %collective-permute-start.8 = (bf16[8,40,1024]{2,1,0:T(8,128)(2,1)}, bf16[8,40,1024]{2,1,0:T(8,128)(2,1)S(1)}, u32[]{:S(2)}, u32[]{:S(2)}) collective-permute-start(bf16[8,40,1024]{2,1,0:T(8,128)(2,1)} %pad_maximum_fusion.1), channel_id=1, source_target_pairs={{0,24},{8,0},{16,8},{24,16},{1,25},{9,1},{17,9},{25,17},{2,26},{10... | collective-permute-start | bytes 1966088 | tf_op jit(solution)/shard_map/ppermute | solution.py:32
  159.3 0.8 copy-start.7
  161.6 10.9 %collective-permute-start.10 = (bf16[40,1024]{1,0:T(8,128)(2,1)S(1)}, bf16[40,1024]{1,0:T(8,128)(2,1)S(1)}, u32[]{:S(2)}, u32[]{:S(2)}) collective-permute-start(bf16[40,1024]{1,0:T(8,128)(2,1)S(1)} %get-tuple-element.56), channel_id=1, source_target_pairs={{0,96},{32,128},{64,160},{96,192},{128,224},{160,0},{192,32},{224,... | collective-permute-start | bytes 245768 | tf_op jit(solution)/shard_map/ppermute | solution.py:32
  164.1 9.9 %collective-permute-start.11 = (bf16[40,1024]{1,0:T(8,128)(2,1)S(1)}, bf16[40,1024]{1,0:T(8,128)(2,1)S(1)}, u32[]{:S(2)}, u32[]{:S(2)}) collective-permute-start(bf16[40,1024]{1,0:T(8,128)(2,1)S(1)} %get-tuple-element.55), channel_id=1, source_target_pairs={{0,160},{32,192},{64,224},{96,0},{128,32},{160,64},{192,96},{224,1... | collective-permute-start | bytes 245768 | tf_op jit(solution)/shard_map/ppermute | solution.py:32
  166.7 13.3 %collective-permute-start.12 = (bf16[40,1024]{1,0:T(8,128)(2,1)S(1)}, bf16[40,1024]{1,0:T(8,128)(2,1)S(1)}, u32[]{:S(2)}, u32[]{:S(2)}) collective-permute-start(bf16[40,1024]{1,0:T(8,128)(2,1)S(1)} %get-tuple-element.54), channel_id=1, source_target_pairs={{0,64},{32,96},{64,128},{96,160},{128,192},{160,224},{192,0},{224,... | collective-permute-start | bytes 245768 | tf_op jit(solution)/shard_map/ppermute | solution.py:32
  167.7 12.3 %collective-permute-start.13 = (bf16[40,1024]{1,0:T(8,128)(2,1)S(1)}, bf16[40,1024]{1,0:T(8,128)(2,1)S(1)}, u32[]{:S(2)}, u32[]{:S(2)}) collective-permute-start(bf16[40,1024]{1,0:T(8,128)(2,1)S(1)} %get-tuple-element.53), channel_id=1, source_target_pairs={{0,192},{32,224},{64,0},{96,32},{128,64},{160,96},{192,128},{224,1... | collective-permute-start | bytes 245768 | tf_op jit(solution)/shard_map/ppermute | solution.py:32
  170.8 9.1 %collective-permute-start.14 = (bf16[40,1024]{1,0:T(8,128)(2,1)S(1)}, bf16[40,1024]{1,0:T(8,128)(2,1)S(1)}, u32[]{:S(2)}, u32[]{:S(2)}) collective-permute-start(bf16[40,1024]{1,0:T(8,128)(2,1)S(1)} %get-tuple-element.52), channel_id=1, source_target_pairs={{0,32},{32,64},{64,96},{96,128},{128,160},{160,192},{192,224},{224... | collective-permute-start | bytes 245768 | tf_op jit(solution)/shard_map/ppermute | solution.py:32
  172.5 7.4 %collective-permute-start.15 = (bf16[40,1024]{1,0:T(8,128)(2,1)S(1)}, bf16[40,1024]{1,0:T(8,128)(2,1)S(1)}, u32[]{:S(2)}, u32[]{:S(2)}) collective-permute-start(bf16[40,1024]{1,0:T(8,128)(2,1)S(1)} %get-tuple-element.51), channel_id=1, source_target_pairs={{0,224},{32,0},{64,32},{96,64},{128,96},{160,128},{192,160},{224,1... | collective-permute-start | bytes 245768 | tf_op jit(solution)/shard_map/ppermute | solution.py:32
  174.1 9.2 %collective-permute-start.9 = (bf16[40,1024]{1,0:T(8,128)(2,1)S(1)}, bf16[40,1024]{1,0:T(8,128)(2,1)S(1)}, u32[]{:S(2)}, u32[]{:S(2)}) collective-permute-start(bf16[40,1024]{1,0:T(8,128)(2,1)S(1)} %get-tuple-element.57), channel_id=1, source_target_pairs={{0,128},{32,160},{64,192},{96,224},{128,0},{160,32},{192,64},{224,... | collective-permute-start | bytes 245768 | tf_op jit(solution)/shard_map/ppermute | solution.py:32

commit v6 on v5

--- a/solution.py
+++ b/solution.py
@@ -338,13 +338,20 @@
     from_right = shift(summed[1], "x", -1, nx)
 
     gw_up = shift(far_a, "y", 1, ny)
-    gw_down = shift(far_b, "y", -1, ny)
-    gw_next = jnp.concatenate([add2(next_a, gw_up), next_b], axis=0)
-    gw_prev = jnp.concatenate([prev_a, add2(prev_b, gw_down)], axis=0)
-    gw_l = shift(gw_next, "y", 1, ny)
-    gw_r = shift(gw_prev, "y", -1, ny)
-    gw_own = jnp.concatenate([own_a, own_b], axis=0)
-    gw_y = (gw_own.astype(F32) + gw_l.astype(F32) + gw_r.astype(F32)).astype(BF)
+    far_high = shift(far_b, "y", 2, ny)
+    prev_low = shift(prev_a, "y", -1, ny)
+    next_high = shift(next_b, "y", 1, ny)
+    next_low = shift(add2(next_a, gw_up), "y", 1, ny)
+    prev_high = shift(prev_b, "y", -1, ny)
+    gw_y = jnp.concatenate(
+        [
+            (own_a.astype(F32) + next_low.astype(F32) + prev_low.astype(F32)).astype(BF),
+            (
+                own_b.astype(F32) + next_high.astype(F32) + prev_high.astype(F32) + far_high.astype(F32)
+            ).astype(BF),
+        ],
+        axis=0,
+    )
 
     back = pl.pallas_call(
         pack_kernel,

time: 185 us -> 188 us (1.016); the launches traced: 184 us -> 185 us
  starting transfers between devices: 51.8 us -> 56.8 us
  waiting for transfers between devices: 91.4 us -> 87.8 us
    ppermute x20 -> x22, starting transfers between devices: 33.3 us -> 38.4 us  [shift(): return lax.ppermute(v, axis, [(i, (i + step) % size) for i in range(size)])]
    ppermute x20 -> x22, waiting for transfers between devices: 58.6 us -> 55 us  [shift(): return lax.ppermute(v, axis, [(i, (i + step) % size) for i in range(size)])]
  transfers between devices with their start and end apart: 22 -> 24, of which waited for: 13 -> 15; matrix products, arithmetic and copies ran while one was open for 2% -> 2% of each run, Pallas kernels for 6% -> 6%
where the time goes in v6:
time: 188 us; the launch traced here: 185 us
  waiting for transfers between devices  87.8 us (47%)
  starting transfers between devices  56.8 us (30%)
  Pallas kernels  31.2 us (17%)
  other arithmetic  4.32 us (2%)
  local copies, waits for them, and re-layouts  3.79 us (2%)
    ppermute x22, waiting for transfers between devices, shift(): return lax.ppermute(v, axis, [(i, (i + step) % size) for i in range(size)])  55 us
    ppermute x22, starting transfers between devices, shift(): return lax.ppermute(v, axis, [(i, (i + step) % size) for i in range(size)])  38.4 us
    all_to_all x1, waiting for transfers between devices, local(): got = lax.all_to_all(send, seq, split_axis=0, concat_axis=0, tiled=True)  32.9 us
    pallas_call x1, Pallas kernels, local(): pl.pallas_call(main_kernel, name='main', out_shape=(tokens_out, tokens_ou...  16.6 us
    all_to_all x1, starting transfers between devices, local(): got = lax.all_to_all(send, seq, split_axis=0, concat_axis=0, tiled=True)  11.7 us
    pallas_call x2, Pallas kernels, heavy(): pl.pallas_call(functools.partial(weight_kernel, n * (width // 2)), out_sh...  8.43 us
    all_to_all x1, starting transfers between devices, local(): lax.all_to_all(back, seq, split_axis=0, concat_axis=0, tiled=True)  6.71 us
  transfers between devices with their start and end apart: 24, of which 15 were waited for; matrix products, arithmetic and copies ran while one was open for 2% of the time, Pallas kernels for 6%

profile of v6, /device:TPU:8, one launch (start us, length us, event | category | flops | bytes accessed | tf_op | source)
XLA Modules:
  0.0 184.9 jit_solution(8264412235969380748)
XLA Ops:
  1.5 1.5 copy-done
  3.1 1.9 %spread.1 = bf16[64,8,1280]{2,1,0:T(8,128)(2,1)} custom-call(s32[64]{0:T(128)S(1)} %reshape_squeeze.3.sent_ref, s32[1]{0:T(128)} %bitcast.1.me_ref, bf16[12,64,1280]{2,1,0:T(8,128)(2,1)S(1)} %copy-done), custom_call_target="tpu_custom_call" | custom-call | tf_op jit(solution)/shard_map/spread/pallas_call | solution.py:245
  4.9 11.7 %all-to-all-start = ((bf16[64,8,1280]{2,1,0:T(8,128)(2,1)}), bf16[64,8,1280]{2,1,0:T(8,128)(2,1)S(1)}, u32[]{:S(2)}, u32[]{:S(2)}) async-start(bf16[64,8,1280]{2,1,0:T(8,128)(2,1)} %spread.1), calls=%async_computation | async-start | bytes 2621440 | tf_op jit(solution)/shard_map/all_to_all | solution.py:254
  16.7 32.9 %all-to-all-done = bf16[64,8,1280]{2,1,0:T(8,128)(2,1)S(1)} async-done(((bf16[64,8,1280]{2,1,0:T(8,128)(2,1)}), bf16[64,8,1280]{2,1,0:T(8,128)(2,1)S(1)}, u32[]{:S(2)}, u32[]{:S(2)}) %all-to-all-start) | async-done | bytes 1310752 | tf_op jit(solution)/shard_map/all_to_all | solution.py:254
  50.2 1.6 collective-permute-start
  51.7 1.7 collective-permute-start.1
  53.5 5.9 %collective-permute-done = bf16[16,8,1280]{2,1,0:T(8,128)(2,1)S(1)} collective-permute-done((bf16[16,8,1280]{2,1,0:T(8,128)(2,1)S(1)}, bf16[16,8,1280]{2,1,0:T(8,128)(2,1)S(1)}, u32[]{:S(2)}, u32[]{:S(2)}) %collective-permute-start) | collective-permute-done | bytes 327712 | tf_op jit(solution)/shard_map/ppermute | solution.py:32
  59.9 3.0 %collective-permute-start.3 = (bf16[8,8,1280]{2,1,0:T(8,128)(2,1)S(1)}, bf16[8,8,1280]{2,1,0:T(8,128)(2,1)S(1)}, u32[]{:S(2)}, u32[]{:S(2)}) collective-permute-start(bf16[8,8,1280]{2,1,0:T(8,128)(2,1)S(1)} %slice.56), channel_id=1, source_target_pairs={{0,6},{2,0},{4,2},{6,4},{1,7},{3,1},{5,3},{7,5},{8,14},{10,8},{12,... | collective-permute-start | bytes 491528 | tf_op jit(solution)/shard_map/ppermute | solution.py:32
  62.9 3.1 %collective-permute-done.2 = bf16[8,8,1280]{2,1,0:T(8,128)(2,1)S(1)} collective-permute-done((bf16[8,8,1280]{2,1,0:T(8,128)(2,1)S(1)}, bf16[8,8,1280]{2,1,0:T(8,128)(2,1)S(1)}, u32[]{:S(2)}, u32[]{:S(2)}) %collective-permute-start.2) | collective-permute-done | bytes 163872 | tf_op jit(solution)/shard_map/ppermute | solution.py:32
  66.4 2.9 %collective-permute-done.4.other_any = bf16[4,16,8,1280]{3,2,1,0:T(8,128)(2,1)S(1)} collective-permute-done((bf16[4,16,8,1280]{3,2,1,0:T(8,128)(2,1)S(1)}, bf16[4,16,8,1280]{3,2,1,0:T(8,128)(2,1)S(1)}, u32[]{:S(2)}, u32[]{:S(2)}) %collective-permute-start.4) | collective-permute-done | bytes 1310752 | tf_op jit(solution)/shard_map/ppermute | solution.py:32
  69.3 16.6 %main.1 = (bf16[512,512]{1,0:T(8,128)(2,1)}, bf16[512,512]{1,0:T(8,128)(2,1)}, bf16[4,16,8,1280]{3,2,1,0:T(8,128)(2,1)S(1)}, bf16[4,16,8,1280]{3,2,1,0:T(8,128)(2,1)S(1)}, bf16[16384,1280]{1,0:T(8,128)(2,1)}) custom-call(s32[4]{0:T(128)S(1)} %fusion.25.start_ref, bf16[4,16,8,1280]{3,2,1,0:T(8,128)(2,1)S(1)} %bitcast.33, ...), custom_call_target="tpu_custom_call" | custom-call | flops 6442450944 | bytes 16777216 | tf_op jit(solution)/shard_map/main/pallas_call | solution.py:276
  86.1 2.9 %collective-permute-done.18 = bf16[4,16,8,1280]{3,2,1,0:T(8,128)(2,1)S(1)} collective-permute-done((bf16[4,16,8,1280]{3,2,1,0:T(8,128)(2,1)S(1)}, bf16[4,16,8,1280]{3,2,1,0:T(8,128)(2,1)S(1)}, u32[]{:S(2)}, u32[]{:S(2)}) %collective-permute-start.18) | collective-permute-done | bytes 1310752 | tf_op jit(solution)/shard_map/ppermute | solution.py:32
  90.0 2.8 %collective-permute-start.20 = (bf16[16,8,1280]{2,1,0:T(8,128)(2,1)S(1)}, bf16[16,8,1280]{2,1,0:T(8,128)(2,1)S(1)}, u32[]{:S(2)}, u32[]{:S(2)}) collective-permute-start(bf16[16,8,1280]{2,1,0:T(8,128)(2,1)S(1)} %get-tuple-element.48), channel_id=1, source_target_pairs={{0,6},{2,0},{4,2},{6,4},{1,7},{3,1},{5,3},{7,5},{8,14},{10,8},{12,... | collective-permute-start | bytes 983048 | tf_op jit(solution)/shard_map/ppermute | solution.py:32
  94.2 6.5 %collective-permute-done.19.left_ref = bf16[16,8,1280]{2,1,0:T(8,128)(2,1)S(1)} collective-permute-done((bf16[16,8,1280]{2,1,0:T(8,128)(2,1)S(1)}, bf16[16,8,1280]{2,1,0:T(8,128)(2,1)S(1)}, u32[]{:S(2)}, u32[]{:S(2)}) %collective-permute-start.19) | collective-permute-done | bytes 327712 | tf_op jit(solution)/shard_map/ppermute | solution.py:32
  100.7 6.4 %collective-permute-done.20.right_ref = bf16[16,8,1280]{2,1,0:T(8,128)(2,1)S(1)} collective-permute-done((bf16[16,8,1280]{2,1,0:T(8,128)(2,1)S(1)}, bf16[16,8,1280]{2,1,0:T(8,128)(2,1)S(1)}, u32[]{:S(2)}, u32[]{:S(2)}) %collective-permute-start.20) | collective-permute-done | bytes 327712 | tf_op jit(solution)/shard_map/ppermute | solution.py:32
  107.1 1.8 collective-permute-done.21.far_ref
  108.9 2.0 %pack.1 = bf16[64,8,1280]{2,1,0:T(8,128)(2,1)} custom-call(s32[16]{0:T(128)S(1)} %bitcast.36, bf16[16,8,1280]{2,1,0:T(8,128)(2,1)S(1)} %get-tuple-element.50.own_ref, bf16[16,8,1280]{2,1,0:T(8,128)(2,1)S(1)} %collective-permute-done.19.left_ref, bf16[16,8,1280]{2,1,0:T(8,128)(2,1)S(1)} %collective-permute-done.20.right_ref, ...), custom_call_target="tpu_custom_call" | custom-call | tf_op jit(solution)/shard_map/pack/pallas_call | solution.py:356
  110.9 6.7 %all-to-all-start.1 = ((bf16[64,8,1280]{2,1,0:T(8,128)(2,1)}), bf16[64,8,1280]{2,1,0:T(8,128)(2,1)S(1)}, u32[]{:S(2)}, u32[]{:S(2)}) async-start(bf16[64,8,1280]{2,1,0:T(8,128)(2,1)} %pack.1), calls=%async_computation.1 | async-start | bytes 2621440 | tf_op jit(solution)/shard_map/all_to_all | solution.py:364
  117.6 4.2 %shard_map.119 = (bf16[4,40,1024]{2,1,0:T(8,128)(2,1)S(1)}, bf16[4,40,1024]{2,1,0:T(8,128)(2,1)S(1)}, bf16[4,40,1024]{2,1,0:T(8,128)(2,1)S(1)}, bf16[4,40,1024]{2,1,0:T(8,128)(2,1)S(1)}) custom-call(s32[1]{0:T(128)} %bitcast.4.y_ref, bf16[16384,1280]{1,0:T(8,128)(2,1)} %get-tuple-element.28.shelf_any), custom_call_target="tpu_custom_call" | custom-call | flops 1342177280 | bytes 6291456 | tf_op jit(solution)/shard_map/pallas_call | solution.py:314
  121.9 1.5 collective-permute-start.5
  123.4 4.2 %shard_map.120 = (bf16[4,40,1024]{2,1,0:T(8,128)(2,1)S(1)}, bf16[4,40,1024]{2,1,0:T(8,128)(2,1)S(1)}, bf16[4,40,1024]{2,1,0:T(8,128)(2,1)S(1)}, bf16[4,40,1024]{2,1,0:T(8,128)(2,1)S(1)}) custom-call(s32[1]{0:T(128)} %bitcast.4.y_ref, bf16[16384,1280]{1,0:T(8,128)(2,1)} %get-tuple-element.28.shelf_any), custom_call_target="tpu_custom_call" | custom-call | flops 1342177280 | bytes 6291456 | tf_op jit(solution)/shard_map/pallas_call | solution.py:314
  131.0 3.2 %collective-permute-start.7 = (bf16[4,40,1024]{2,1,0:T(8,128)(2,1)S(1)}, bf16[4,40,1024]{2,1,0:T(8,128)(2,1)}, u32[]{:S(2)}, u32[]{:S(2)}) collective-permute-start(bf16[4,40,1024]{2,1,0:T(8,128)(2,1)S(1)} %get-tuple-element.32), channel_id=1, source_target_pairs={{0,24},{8,0},{16,8},{24,16},{1,25},{9,1},{17,9},{25,17},{2,26},{10... | collective-permute-start | bytes 983048 | tf_op jit(solution)/shard_map/ppermute | solution.py:32
  134.2 13.0 %collective-permute-done.5 = bf16[4,40,1024]{2,1,0:T(8,128)(2,1)S(1)} collective-permute-done((bf16[4,40,1024]{2,1,0:T(8,128)(2,1)S(1)}, bf16[4,40,1024]{2,1,0:T(8,128)(2,1)S(1)}, u32[]{:S(2)}, u32[]{:S(2)}) %collective-permute-start.5) | collective-permute-done | bytes 327712 | tf_op jit(solution)/shard_map/ppermute | solution.py:32
  148.0 3.0 %collective-permute-start.6 = (bf16[4,40,1024]{2,1,0:T(8,128)(2,1)}, bf16[4,40,1024]{2,1,0:T(8,128)(2,1)}, u32[]{:S(2)}, u32[]{:S(2)}) collective-permute-start(bf16[4,40,1024]{2,1,0:T(8,128)(2,1)} %add_convert_fusion.6), channel_id=1, source_target_pairs={{0,8},{8,16},{16,24},{24,0},{1,9},{9,17},{17,25},{25,1},{2,10},{10... | collective-permute-start | bytes 983048 | tf_op jit(solution)/shard_map/ppermute | solution.py:32
  151.0 5.4 %collective-permute-done.8 = bf16[4,40,1024]{2,1,0:T(8,128)(2,1)} collective-permute-done((bf16[4,40,1024]{2,1,0:T(8,128)(2,1)S(1)}, bf16[4,40,1024]{2,1,0:T(8,128)(2,1)}, u32[]{:S(2)}, u32[]{:S(2)}) %collective-permute-start.8) | collective-permute-done | bytes 327712 | tf_op jit(solution)/shard_map/ppermute | solution.py:32
  157.8 1.7 collective-permute-done.7
  159.5 2.3 %collective-permute-done.6 = bf16[4,40,1024]{2,1,0:T(8,128)(2,1)} collective-permute-done((bf16[4,40,1024]{2,1,0:T(8,128)(2,1)}, bf16[4,40,1024]{2,1,0:T(8,128)(2,1)}, u32[]{:S(2)}, u32[]{:S(2)}) %collective-permute-start.6) | collective-permute-done | bytes 327712 | tf_op jit(solution)/shard_map/ppermute | solution.py:32
  164.5 4.4 %collective-permute-start.11 = (bf16[40,1024]{1,0:T(8,128)(2,1)S(1)}, bf16[40,1024]{1,0:T(8,128)(2,1)S(1)}, u32[]{:S(2)}, u32[]{:S(2)}) collective-permute-start(bf16[40,1024]{1,0:T(8,128)(2,1)S(1)} %get-tuple-element.52), channel_id=1, source_target_pairs={{0,128},{32,160},{64,192},{96,224},{128,0},{160,32},{192,64},{224,... | collective-permute-start | bytes 245768 | tf_op jit(solution)/shard_map/ppermute | solution.py:32
  170.0 4.0 %collective-permute-start.13 = (bf16[40,1024]{1,0:T(8,128)(2,1)S(1)}, bf16[40,1024]{1,0:T(8,128)(2,1)S(1)}, u32[]{:S(2)}, u32[]{:S(2)}) collective-permute-start(bf16[40,1024]{1,0:T(8,128)(2,1)S(1)} %get-tuple-element.54), channel_id=1, source_target_pairs={{0,160},{32,192},{64,224},{96,0},{128,32},{160,64},{192,96},{224,1... | collective-permute-start | bytes 245768 | tf_op jit(solution)/shard_map/ppermute | solution.py:32
  174.5 3.6 %collective-permute-start.15 = (bf16[40,1024]{1,0:T(8,128)(2,1)S(1)}, bf16[40,1024]{1,0:T(8,128)(2,1)S(1)}, u32[]{:S(2)}, u32[]{:S(2)}) collective-permute-start(bf16[40,1024]{1,0:T(8,128)(2,1)S(1)} %get-tuple-element.56), channel_id=1, source_target_pairs={{0,192},{32,224},{64,0},{96,32},{128,64},{160,96},{192,128},{224,1... | collective-permute-start | bytes 245768 | tf_op jit(solution)/shard_map/ppermute | solution.py:32
  178.8 2.3 %collect.1 = f32[12,8,1280]{2,1,0:T(8,128)} custom-call(s32[64]{0:T(128)S(1)} %reshape_squeeze.3.sent_ref, bf16[64,8,1280]{2,1,0:T(8,128)(2,1)S(1)} %all-to-all-done.1.got_ref), custom_call_target="tpu_custom_call" | custom-call | tf_op jit(solution)/shard_map/collect/pallas_call | solution.py:373
  181.7 2.0 %collective-permute-done.15 = bf16[40,1024]{1,0:T(8,128)(2,1)S(1)} collective-permute-done((bf16[40,1024]{1,0:T(8,128)(2,1)S(1)}, bf16[40,1024]{1,0:T(8,128)(2,1)S(1)}, u32[]{:S(2)}, u32[]{:S(2)}) %collective-permute-start.15) | collective-permute-done | bytes 81952 | tf_op jit(solution)/shard_map/ppermute | solution.py:32
  (57 shorter events, 17.1 us)
Async XLA Ops:
  1.5 1.5 copy-start
  4.9 11.7 %copy-start.2 = (s32[1,16]{1,0:T(1,128)S(1)}, s32[1,16]{1,0:T(1,128)}, u32[]{:S(2)}) copy-start(s32[1,16]{1,0:T(1,128)} %param.12) | copy-start | bytes 196
  4.9 44.6 %all-to-all-start = ((bf16[64,8,1280]{2,1,0:T(8,128)(2,1)}), bf16[64,8,1280]{2,1,0:T(8,128)(2,1)S(1)}, u32[]{:S(2)}, u32[]{:S(2)}) async-start(bf16[64,8,1280]{2,1,0:T(8,128)(2,1)} %spread.1), calls=%async_computation | async-start | bytes 2621440 | tf_op jit(solution)/shard_map/all_to_all | solution.py:254
  49.6 19.7 %copy-start.6 = (bf16[512,512]{1,0:T(8,128)(2,1)S(1)}, bf16[512,512]{1,0:T(8,128)(2,1)}, u32[]{:S(2)}) copy-start(bf16[512,512]{1,0:T(8,128)(2,1)} %g_any.1) | copy-start | bytes 1572868
  50.2 9.3 %collective-permute-start = (bf16[16,8,1280]{2,1,0:T(8,128)(2,1)S(1)}, bf16[16,8,1280]{2,1,0:T(8,128)(2,1)S(1)}, u32[]{:S(2)}, u32[]{:S(2)}) collective-permute-start(bf16[16,8,1280]{2,1,0:T(8,128)(2,1)S(1)} %gather_fusion), channel_id=1, source_target_pairs={{0,2},{2,4},{4,6},{6,0},{1,3},{3,5},{5,7},{7,1},{8,10},{10,12},{12... | collective-permute-start | bytes 983048 | tf_op jit(solution)/shard_map/ppermute | solution.py:32
  51.7 8.1 %collective-permute-start.1 = (bf16[16,8,1280]{2,1,0:T(8,128)(2,1)S(1)}, bf16[16,8,1280]{2,1,0:T(8,128)(2,1)S(1)}, u32[]{:S(2)}, u32[]{:S(2)}) collective-permute-start(bf16[16,8,1280]{2,1,0:T(8,128)(2,1)S(1)} %gather_fusion), channel_id=1, source_target_pairs={{0,6},{2,0},{4,2},{6,4},{1,7},{3,1},{5,3},{7,5},{8,14},{10,8},{12,... | collective-permute-start | bytes 983048 | tf_op jit(solution)/shard_map/ppermute | solution.py:32
  53.5 15.8 %copy-start.5 = (bf16[512,512]{1,0:T(8,128)(2,1)S(1)}, bf16[512,512]{1,0:T(8,128)(2,1)}, u32[]{:S(2)}) copy-start(bf16[512,512]{1,0:T(8,128)(2,1)} %q_any.1) | copy-start | bytes 1572868
  53.5 12.7 %copy-start.1 = (s32[512]{0:T(512)S(1)}, s32[512]{0:T(512)}, u32[]{:S(2)}) copy-start(s32[512]{0:T(512)} %param.14) | copy-start | bytes 6148
  53.5 15.8 %copy-start.3 = (bf16[1280,512]{1,0:T(8,128)(2,1)S(1)}, bf16[1280,512]{1,0:T(8,128)(2,1)}, u32[]{:S(2)}) copy-start(bf16[1280,512]{1,0:T(8,128)(2,1)} %wk_any.1) | copy-start | bytes 3932164
  53.5 15.7 %copy-start.4 = (bf16[1280,512]{1,0:T(8,128)(2,1)S(1)}, bf16[1280,512]{1,0:T(8,128)(2,1)}, u32[]{:S(2)}) copy-start(bf16[1280,512]{1,0:T(8,128)(2,1)} %wv_any.1) | copy-start | bytes 3932164
  59.5 6.6 %collective-permute-start.2 = (bf16[8,8,1280]{2,1,0:T(8,128)(2,1)S(1)}, bf16[8,8,1280]{2,1,0:T(8,128)(2,1)S(1)}, u32[]{:S(2)}, u32[]{:S(2)}) collective-permute-start(bf16[8,8,1280]{2,1,0:T(8,128)(2,1)S(1)} %slice.55), channel_id=1, source_target_pairs={{0,2},{2,4},{4,6},{6,0},{1,3},{3,5},{5,7},{7,1},{8,10},{10,12},{12... | collective-permute-start | bytes 491528 | tf_op jit(solution)/shard_map/ppermute | solution.py:32
  59.9 6.2 %collective-permute-start.3 = (bf16[8,8,1280]{2,1,0:T(8,128)(2,1)S(1)}, bf16[8,8,1280]{2,1,0:T(8,128)(2,1)S(1)}, u32[]{:S(2)}, u32[]{:S(2)}) collective-permute-start(bf16[8,8,1280]{2,1,0:T(8,128)(2,1)S(1)} %slice.56), channel_id=1, source_target_pairs={{0,6},{2,0},{4,2},{6,4},{1,7},{3,1},{5,3},{7,5},{8,14},{10,8},{12,... | collective-permute-start | bytes 491528 | tf_op jit(solution)/shard_map/ppermute | solution.py:32
  66.1 3.1 %collective-permute-start.4 = (bf16[4,16,8,1280]{3,2,1,0:T(8,128)(2,1)S(1)}, bf16[4,16,8,1280]{3,2,1,0:T(8,128)(2,1)S(1)}, u32[]{:S(2)}, u32[]{:S(2)}) collective-permute-start(bf16[4,16,8,1280]{3,2,1,0:T(8,128)(2,1)S(1)} %bitcast.32), channel_id=1, source_target_pairs={{0,1},{1,0},{2,3},{3,2},{4,5},{5,4},{6,7},{7,6},{8,9},{9,8},{10,11... | collective-permute-start | bytes 3932168 | tf_op jit(solution)/shard_map/ppermute | solution.py:32
  85.9 3.1 %collective-permute-start.18 = (bf16[4,16,8,1280]{3,2,1,0:T(8,128)(2,1)S(1)}, bf16[4,16,8,1280]{3,2,1,0:T(8,128)(2,1)S(1)}, u32[]{:S(2)}, u32[]{:S(2)}) collective-permute-start(bf16[4,16,8,1280]{3,2,1,0:T(8,128)(2,1)S(1)} %get-tuple-element.38), channel_id=1, source_target_pairs={{0,1},{1,0},{2,3},{3,2},{4,5},{5,4},{6,7},{7,6},{8,9},{9,8},{10,11... | collective-permute-start | bytes 3932168 | tf_op jit(solution)/shard_map/ppermute | solution.py:32
  89.3 11.4 %collective-permute-start.19 = (bf16[16,8,1280]{2,1,0:T(8,128)(2,1)S(1)}, bf16[16,8,1280]{2,1,0:T(8,128)(2,1)S(1)}, u32[]{:S(2)}, u32[]{:S(2)}) collective-permute-start(bf16[16,8,1280]{2,1,0:T(8,128)(2,1)S(1)} %get-tuple-element.49), channel_id=1, source_target_pairs={{0,2},{2,4},{4,6},{6,0},{1,3},{3,5},{5,7},{7,1},{8,10},{10,12},{12... | collective-permute-start | bytes 983048 | tf_op jit(solution)/shard_map/ppermute | solution.py:32
  90.0 17.1 %collective-permute-start.20 = (bf16[16,8,1280]{2,1,0:T(8,128)(2,1)S(1)}, bf16[16,8,1280]{2,1,0:T(8,128)(2,1)S(1)}, u32[]{:S(2)}, u32[]{:S(2)}) collective-permute-start(bf16[16,8,1280]{2,1,0:T(8,128)(2,1)S(1)} %get-tuple-element.48), channel_id=1, source_target_pairs={{0,6},{2,0},{4,2},{6,4},{1,7},{3,1},{5,3},{7,5},{8,14},{10,8},{12,... | collective-permute-start | bytes 983048 | tf_op jit(solution)/shard_map/ppermute | solution.py:32
  92.8 16.1 %collective-permute-start.21 = (bf16[16,8,1280]{2,1,0:T(8,128)(2,1)S(1)}, bf16[16,8,1280]{2,1,0:T(8,128)(2,1)S(1)}, u32[]{:S(2)}, u32[]{:S(2)}) collective-permute-start(bf16[16,8,1280]{2,1,0:T(8,128)(2,1)S(1)} %get-tuple-element.47), channel_id=1, source_target_pairs={{0,4},{2,6},{4,0},{6,2},{1,5},{3,7},{5,1},{7,3},{8,12},{10,14},{12... | collective-permute-start | bytes 983048 | tf_op jit(solution)/shard_map/ppermute | solution.py:32
  110.9 67.9 %all-to-all-start.1 = ((bf16[64,8,1280]{2,1,0:T(8,128)(2,1)}), bf16[64,8,1280]{2,1,0:T(8,128)(2,1)S(1)}, u32[]{:S(2)}, u32[]{:S(2)}) async-start(bf16[64,8,1280]{2,1,0:T(8,128)(2,1)} %pack.1), calls=%async_computation.1 | async-start | bytes 2621440 | tf_op jit(solution)/shard_map/all_to_all | solution.py:364
  121.9 25.3 %collective-permute-start.5 = (bf16[4,40,1024]{2,1,0:T(8,128)(2,1)S(1)}, bf16[4,40,1024]{2,1,0:T(8,128)(2,1)S(1)}, u32[]{:S(2)}, u32[]{:S(2)}) collective-permute-start(bf16[4,40,1024]{2,1,0:T(8,128)(2,1)S(1)} %get-tuple-element.31), channel_id=1, source_target_pairs={{0,8},{8,16},{16,24},{24,0},{1,9},{9,17},{17,25},{25,1},{2,10},{10... | collective-permute-start | bytes 983048 | tf_op jit(solution)/shard_map/ppermute | solution.py:32
  127.6 23.3 %collective-permute-start.10 = (bf16[4,40,1024]{2,1,0:T(8,128)(2,1)S(1)}, bf16[4,40,1024]{2,1,0:T(8,128)(2,1)}, u32[]{:S(2)}, u32[]{:S(2)}) collective-permute-start(bf16[4,40,1024]{2,1,0:T(8,128)(2,1)S(1)} %get-tuple-element.36), channel_id=1, source_target_pairs={{0,16},{8,24},{16,0},{24,8},{1,17},{9,25},{17,1},{25,9},{2,18},{10... | collective-permute-start | bytes 983048 | tf_op jit(solution)/shard_map/ppermute | solution.py:32
  128.7 27.7 %collective-permute-start.8 = (bf16[4,40,1024]{2,1,0:T(8,128)(2,1)S(1)}, bf16[4,40,1024]{2,1,0:T(8,128)(2,1)}, u32[]{:S(2)}, u32[]{:S(2)}) collective-permute-start(bf16[4,40,1024]{2,1,0:T(8,128)(2,1)S(1)} %get-tuple-element.34), channel_id=1, source_target_pairs={{0,8},{8,16},{16,24},{24,0},{1,9},{9,17},{17,25},{25,1},{2,10},{10... | collective-permute-start | bytes 983048 | tf_op jit(solution)/shard_map/ppermute | solution.py:32
  129.7 26.7 %collective-permute-start.9 = (bf16[4,40,1024]{2,1,0:T(8,128)(2,1)S(1)}, bf16[4,40,1024]{2,1,0:T(8,128)(2,1)}, u32[]{:S(2)}, u32[]{:S(2)}) collective-permute-start(bf16[4,40,1024]{2,1,0:T(8,128)(2,1)S(1)} %get-tuple-element.35), channel_id=1, source_target_pairs={{0,24},{8,0},{16,8},{24,16},{1,25},{9,1},{17,9},{25,17},{2,26},{10... | collective-permute-start | bytes 983048 | tf_op jit(solution)/shard_map/ppermute | solution.py:32
  131.0 28.5 %collective-permute-start.7 = (bf16[4,40,1024]{2,1,0:T(8,128)(2,1)S(1)}, bf16[4,40,1024]{2,1,0:T(8,128)(2,1)}, u32[]{:S(2)}, u32[]{:S(2)}) collective-permute-start(bf16[4,40,1024]{2,1,0:T(8,128)(2,1)S(1)} %get-tuple-element.32), channel_id=1, source_target_pairs={{0,24},{8,0},{16,8},{24,16},{1,25},{9,1},{17,9},{25,17},{2,26},{10... | collective-permute-start | bytes 983048 | tf_op jit(solution)/shard_map/ppermute | solution.py:32
  148.0 13.8 %collective-permute-start.6 = (bf16[4,40,1024]{2,1,0:T(8,128)(2,1)}, bf16[4,40,1024]{2,1,0:T(8,128)(2,1)}, u32[]{:S(2)}, u32[]{:S(2)}) collective-permute-start(bf16[4,40,1024]{2,1,0:T(8,128)(2,1)} %add_convert_fusion.6), channel_id=1, source_target_pairs={{0,8},{8,16},{16,24},{24,0},{1,9},{9,17},{17,25},{25,1},{2,10},{10... | collective-permute-start | bytes 983048 | tf_op jit(solution)/shard_map/ppermute | solution.py:32
  163.1 11.4 %collective-permute-start.16 = (bf16[40,1024]{1,0:T(8,128)(2,1)S(1)}, bf16[40,1024]{1,0:T(8,128)(2,1)S(1)}, u32[]{:S(2)}, u32[]{:S(2)}) collective-permute-start(bf16[40,1024]{1,0:T(8,128)(2,1)S(1)} %fusion.19), channel_id=1, source_target_pairs={{0,32},{32,64},{64,96},{96,128},{128,160},{160,192},{192,224},{224... | collective-permute-start | bytes 245768 | tf_op jit(solution)/shard_map/ppermute | solution.py:32
  164.5 13.6 %collective-permute-start.11 = (bf16[40,1024]{1,0:T(8,128)(2,1)S(1)}, bf16[40,1024]{1,0:T(8,128)(2,1)S(1)}, u32[]{:S(2)}, u32[]{:S(2)}) collective-permute-start(bf16[40,1024]{1,0:T(8,128)(2,1)S(1)} %get-tuple-element.52), channel_id=1, source_target_pairs={{0,128},{32,160},{64,192},{96,224},{128,0},{160,32},{192,64},{224,... | collective-permute-start | bytes 245768 | tf_op jit(solution)/shard_map/ppermute | solution.py:32
  169.0 12.7 %collective-permute-start.12 = (bf16[40,1024]{1,0:T(8,128)(2,1)S(1)}, bf16[40,1024]{1,0:T(8,128)(2,1)S(1)}, u32[]{:S(2)}, u32[]{:S(2)}) collective-permute-start(bf16[40,1024]{1,0:T(8,128)(2,1)S(1)} %get-tuple-element.53), channel_id=1, source_target_pairs={{0,96},{32,128},{64,160},{96,192},{128,224},{160,0},{192,32},{224,... | collective-permute-start | bytes 245768 | tf_op jit(solution)/shard_map/ppermute | solution.py:32
  170.0 11.7 %collective-permute-start.13 = (bf16[40,1024]{1,0:T(8,128)(2,1)S(1)}, bf16[40,1024]{1,0:T(8,128)(2,1)S(1)}, u32[]{:S(2)}, u32[]{:S(2)}) collective-permute-start(bf16[40,1024]{1,0:T(8,128)(2,1)S(1)} %get-tuple-element.54), channel_id=1, source_target_pairs={{0,160},{32,192},{64,224},{96,0},{128,32},{160,64},{192,96},{224,1... | collective-permute-start | bytes 245768 | tf_op jit(solution)/shard_map/ppermute | solution.py:32
  174.0 7.7 %collective-permute-start.14 = (bf16[40,1024]{1,0:T(8,128)(2,1)S(1)}, bf16[40,1024]{1,0:T(8,128)(2,1)S(1)}, u32[]{:S(2)}, u32[]{:S(2)}) collective-permute-start(bf16[40,1024]{1,0:T(8,128)(2,1)S(1)} %get-tuple-element.55), channel_id=1, source_target_pairs={{0,64},{32,96},{64,128},{96,160},{128,192},{160,224},{192,0},{224,... | collective-permute-start | bytes 245768 | tf_op jit(solution)/shard_map/ppermute | solution.py:32
  174.5 9.2 %collective-permute-start.15 = (bf16[40,1024]{1,0:T(8,128)(2,1)S(1)}, bf16[40,1024]{1,0:T(8,128)(2,1)S(1)}, u32[]{:S(2)}, u32[]{:S(2)}) collective-permute-start(bf16[40,1024]{1,0:T(8,128)(2,1)S(1)} %get-tuple-element.56), channel_id=1, source_target_pairs={{0,192},{32,224},{64,0},{96,32},{128,64},{160,96},{192,128},{224,1... | collective-permute-start | bytes 245768 | tf_op jit(solution)/shard_map/ppermute | solution.py:32
  178.1 5.9 %collective-permute-start.17 = (bf16[40,1024]{1,0:T(8,128)(2,1)S(1)}, bf16[40,1024]{1,0:T(8,128)(2,1)S(1)}, u32[]{:S(2)}, u32[]{:S(2)}) collective-permute-start(bf16[40,1024]{1,0:T(8,128)(2,1)S(1)} %get-tuple-element.51), channel_id=1, source_target_pairs={{0,224},{32,0},{64,32},{96,64},{128,96},{160,128},{192,160},{224,1... | collective-permute-start | bytes 245768 | tf_op jit(solution)/shard_map/ppermute | solution.py:32

commit v7 on v6

--- a/solution.py
+++ b/solution.py
@@ -176,10 +176,12 @@
 
 
 def weight_kernel(
-    base, y_ref, shelf_any, own_ref, next_ref, far_ref, prev_ref,
-    lat_ref, bg_ref, t_ref, sum_ref, lat_sem, bg_sem,
+    base, y_ref, shelf_any, *refs,
 ):
+    early_refs = refs[:-10]
+    own_ref, next_ref, far_ref, prev_ref, lat_ref, bg_ref, t_ref, sum_ref, lat_sem, bg_sem = refs[-10:]
     nz, part, cols = own_ref.shape
+    skip = prev_ref.shape[0] - nz
     keys, half = lat_ref.shape
     ny = half // (nz * part)
     my_y = y_ref[0]
@@ -201,7 +203,10 @@
         there = lax.rem(my_y + rel, ny)
         for z in range(nz):
             rows = pl.ds(pl.multiple_of((z * ny + there) * part, SUB), part)
-            out_ref[z] = sum_ref[rows, :].astype(BF)
+            spot = z + skip if out_ref is prev_ref else z
+            out_ref[spot] = sum_ref[rows, :].astype(BF)
+    for early_ref in early_refs:
+        prev_ref[:skip] = early_ref[...]
 
 
 def pack_kernel(place_ref, own_ref, left_ref, right_ref, far_ref, out_ref):
@@ -217,16 +222,17 @@
             out_ref[place] = total[v]
 
 
-def collect_kernel(sent_ref, got_ref, out_ref):
-    out_ref[...] = jnp.zeros_like(out_ref)
-
-    @pl.loop(0, got_ref.shape[0])
+def collect_kernel(sent_ref, got_ref, out_ref, sum_ref):
+    images = out_ref.shape[0]
+    sum_ref[...] = jnp.zeros_like(sum_ref)
+
+    @pl.loop(0, got_ref.shape[0], unroll=4)
     def _(e):
         image = sent_ref[e]
-
-        @pl.when(image >= 0)
-        def _():
-            out_ref[image] += got_ref[e].astype(F32)
+        at = jnp.where(image >= 0, image, images)
+        sum_ref[at] += got_ref[e].astype(F32)
+
+    out_ref[...] = sum_ref[:images]
 
 
 def local(queries, latents, key_weight, value_weight, visible, outbound, token_slot, grad_out):
@@ -272,6 +278,7 @@
     tokens_out = jax.ShapeDtypeStruct((tokens, cols), BF)
     rows_out = jax.ShapeDtypeStruct((nx, vis, SUB, width), BF)
     split = jax.ShapeDtypeStruct((zh, part, 2 * cols), BF)
+    full = jax.ShapeDtypeStruct((nz, part, 2 * cols), BF)
     chunks = vis // WIN
     att, dq, keep, give, shelf = pl.pallas_call(
         main_kernel,
@@ -310,11 +317,11 @@
 
     swapped = shift(give, "core", 1, 2)
 
-    def heavy(n):
+    def heavy(n, *early):
         return pl.pallas_call(
             functools.partial(weight_kernel, n * (width // 2)),
-            out_shape=(split,) * 4,
-            in_specs=[smem(), far()],
+            out_shape=(split, split, split, full if early else split),
+            in_specs=[smem(), far()] + [vmem()] * len(early),
             out_specs=(vmem(),) * 4,
             scratch_shapes=[
                 pltpu.VMEM((keys, width // 2), BF),
@@ -328,26 +335,28 @@
             cost_estimate=pl.CostEstimate(
                 flops=2 * keys * width * cols, bytes_accessed=6 * 1024 * 1024, transcendentals=0
             ),
-        )(y_here, shelf)
+        )(y_here, shelf, *early)
 
     own_a, next_a, far_a, prev_a = heavy(0)
-    own_b, next_b, far_b, prev_b = heavy(1)
+    own_b, next_b, far_b, prev_all = heavy(1, prev_a)
     summed = [add2(keep[r], swapped[r]) for r in range(nx)]
     from_far = shift(summed[3], "x", 2, nx)
     from_left = shift(summed[2], "x", 1, nx)
     from_right = shift(summed[1], "x", -1, nx)
 
-    gw_up = shift(far_a, "y", 1, ny)
+    relayed = shift(far_a, "y", 1, ny)
     far_high = shift(far_b, "y", 2, ny)
-    prev_low = shift(prev_a, "y", -1, ny)
+    prev_got = shift(prev_all, "y", -1, ny)
     next_high = shift(next_b, "y", 1, ny)
-    next_low = shift(add2(next_a, gw_up), "y", 1, ny)
-    prev_high = shift(prev_b, "y", -1, ny)
+    next_low = shift(add2(next_a, relayed), "y", 1, ny)
     gw_y = jnp.concatenate(
         [
-            (own_a.astype(F32) + next_low.astype(F32) + prev_low.astype(F32)).astype(BF),
+            (own_a.astype(F32) + next_low.astype(F32) + prev_got[:zh].astype(F32)).astype(BF),
             (
-                own_b.astype(F32) + next_high.astype(F32) + prev_high.astype(F32) + far_high.astype(F32)
+                own_b.astype(F32)
+                + next_high.astype(F32)
+                + prev_got[zh:].astype(F32)
+                + far_high.astype(F32)
             ).astype(BF),
         ],
         axis=0,
@@ -376,6 +385,7 @@
         out_shape=jax.ShapeDtypeStruct((images, SUB, width), F32),
         in_specs=[smem(), vmem()],
         out_specs=vmem(),
+        scratch_shapes=[pltpu.VMEM((images + 1, SUB, width), F32)],
         compiler_params=grant(8),
     )(sent, returned)
     arrived, grad_latents = lax.optimization_barrier((arrived, grad_latents))

time: 188 us -> 188 us (level)
  waiting for transfers between devices: 87.8 us -> 93.8 us
  starting transfers between devices: 56.8 us -> 52.6 us
    ppermute x22 -> x21, waiting for transfers between devices: 55 us -> 61 us  [shift(): return lax.ppermute(v, axis, [(i, (i + step) % size) for i in range(size)])]
    ppermute x22 -> x21, starting transfers between devices: 38.4 us -> 34.2 us  [shift(): return lax.ppermute(v, axis, [(i, (i + step) % size) for i in range(size)])]
  transfers between devices with their start and end apart: 24 -> 23, of which waited for: 15 -> 15; matrix products, arithmetic and copies ran while one was open for 2% -> 2% of each run, Pallas kernels for 6% -> 6%
where the time goes in v7:
time: 188 us; the launch traced here: 185 us
  waiting for transfers between devices  93.8 us (50%)
  starting transfers between devices  52.6 us (28%)
  Pallas kernels  30.8 us (16%)
  local copies, waits for them, and re-layouts  3.79 us (2%)
  other arithmetic  3.47 us (2%)
    ppermute x21, waiting for transfers between devices, shift(): return lax.ppermute(v, axis, [(i, (i + step) % size) for i in range(size)])  61 us
    ppermute x21, starting transfers between devices, shift(): return lax.ppermute(v, axis, [(i, (i + step) % size) for i in range(size)])  34.2 us
    all_to_all x1, waiting for transfers between devices, local(): got = lax.all_to_all(send, seq, split_axis=0, concat_axis=0, tiled=True)  32.9 us
    pallas_call x1, Pallas kernels, local(): pl.pallas_call(main_kernel, name='main', out_shape=(tokens_out, tokens_ou...  16.6 us
    all_to_all x1, starting transfers between devices, local(): got = lax.all_to_all(send, seq, split_axis=0, concat_axis=0, tiled=True)  11.7 us
    pallas_call x2, Pallas kernels, heavy(): pl.pallas_call(functools.partial(weight_kernel, n * (width // 2)), out_sh...  8.45 us
    all_to_all x1, starting transfers between devices, local(): lax.all_to_all(back, seq, split_axis=0, concat_axis=0, tiled=True)  6.71 us
  transfers between devices with their start and end apart: 23, of which 15 were waited for; matrix products, arithmetic and copies ran while one was open for 2% of the time, Pallas kernels for 6%

profile of v7, /device:TPU:8, one launch (start us, length us, event | category | flops | bytes accessed | tf_op | source)
XLA Modules:
  0.0 185.4 jit_solution(9402142401541395114)
XLA Ops:
  1.5 1.5 copy-done
  3.1 1.9 %spread.1 = bf16[64,8,1280]{2,1,0:T(8,128)(2,1)} custom-call(s32[64]{0:T(128)S(1)} %reshape_squeeze.3.sent_ref, s32[1]{0:T(128)} %bitcast.1.me_ref, bf16[12,64,1280]{2,1,0:T(8,128)(2,1)S(1)} %copy-done), custom_call_target="tpu_custom_call" | custom-call | tf_op jit(solution)/shard_map/spread/pallas_call | solution.py:251
  4.9 11.7 %all-to-all-start = ((bf16[64,8,1280]{2,1,0:T(8,128)(2,1)}), bf16[64,8,1280]{2,1,0:T(8,128)(2,1)S(1)}, u32[]{:S(2)}, u32[]{:S(2)}) async-start(bf16[64,8,1280]{2,1,0:T(8,128)(2,1)} %spread.1), calls=%async_computation | async-start | bytes 2621440 | tf_op jit(solution)/shard_map/all_to_all | solution.py:260
  16.7 32.9 %all-to-all-done = bf16[64,8,1280]{2,1,0:T(8,128)(2,1)S(1)} async-done(((bf16[64,8,1280]{2,1,0:T(8,128)(2,1)}), bf16[64,8,1280]{2,1,0:T(8,128)(2,1)S(1)}, u32[]{:S(2)}, u32[]{:S(2)}) %all-to-all-start) | async-done | bytes 1310752 | tf_op jit(solution)/shard_map/all_to_all | solution.py:260
  50.2 1.6 collective-permute-start
  51.7 1.7 collective-permute-start.1
  53.5 5.9 %collective-permute-done = bf16[16,8,1280]{2,1,0:T(8,128)(2,1)S(1)} collective-permute-done((bf16[16,8,1280]{2,1,0:T(8,128)(2,1)S(1)}, bf16[16,8,1280]{2,1,0:T(8,128)(2,1)S(1)}, u32[]{:S(2)}, u32[]{:S(2)}) %collective-permute-start) | collective-permute-done | bytes 327712 | tf_op jit(solution)/shard_map/ppermute | solution.py:32
  59.9 3.0 %collective-permute-start.3 = (bf16[8,8,1280]{2,1,0:T(8,128)(2,1)S(1)}, bf16[8,8,1280]{2,1,0:T(8,128)(2,1)S(1)}, u32[]{:S(2)}, u32[]{:S(2)}) collective-permute-start(bf16[8,8,1280]{2,1,0:T(8,128)(2,1)S(1)} %slice.64), channel_id=1, source_target_pairs={{0,6},{2,0},{4,2},{6,4},{1,7},{3,1},{5,3},{7,5},{8,14},{10,8},{12,... | collective-permute-start | bytes 491528 | tf_op jit(solution)/shard_map/ppermute | solution.py:32
  62.9 3.1 %collective-permute-done.2 = bf16[8,8,1280]{2,1,0:T(8,128)(2,1)S(1)} collective-permute-done((bf16[8,8,1280]{2,1,0:T(8,128)(2,1)S(1)}, bf16[8,8,1280]{2,1,0:T(8,128)(2,1)S(1)}, u32[]{:S(2)}, u32[]{:S(2)}) %collective-permute-start.2) | collective-permute-done | bytes 163872 | tf_op jit(solution)/shard_map/ppermute | solution.py:32
  66.4 2.9 %collective-permute-done.4.other_any = bf16[4,16,8,1280]{3,2,1,0:T(8,128)(2,1)S(1)} collective-permute-done((bf16[4,16,8,1280]{3,2,1,0:T(8,128)(2,1)S(1)}, bf16[4,16,8,1280]{3,2,1,0:T(8,128)(2,1)S(1)}, u32[]{:S(2)}, u32[]{:S(2)}) %collective-permute-start.4) | collective-permute-done | bytes 1310752 | tf_op jit(solution)/shard_map/ppermute | solution.py:32
  69.3 16.6 %main.1 = (bf16[512,512]{1,0:T(8,128)(2,1)}, bf16[512,512]{1,0:T(8,128)(2,1)}, bf16[4,16,8,1280]{3,2,1,0:T(8,128)(2,1)S(1)}, bf16[4,16,8,1280]{3,2,1,0:T(8,128)(2,1)S(1)}, bf16[16384,1280]{1,0:T(8,128)(2,1)}) custom-call(s32[4]{0:T(128)S(1)} %fusion.25.start_ref, bf16[4,16,8,1280]{3,2,1,0:T(8,128)(2,1)S(1)} %bitcast.33, ...), custom_call_target="tpu_custom_call" | custom-call | flops 6442450944 | bytes 16777216 | tf_op jit(solution)/shard_map/main/pallas_call | solution.py:283
  86.1 2.9 %collective-permute-done.17 = bf16[4,16,8,1280]{3,2,1,0:T(8,128)(2,1)S(1)} collective-permute-done((bf16[4,16,8,1280]{3,2,1,0:T(8,128)(2,1)S(1)}, bf16[4,16,8,1280]{3,2,1,0:T(8,128)(2,1)S(1)}, u32[]{:S(2)}, u32[]{:S(2)}) %collective-permute-start.17) | collective-permute-done | bytes 1310752 | tf_op jit(solution)/shard_map/ppermute | solution.py:32
  90.0 2.8 %collective-permute-start.19 = (bf16[16,8,1280]{2,1,0:T(8,128)(2,1)S(1)}, bf16[16,8,1280]{2,1,0:T(8,128)(2,1)S(1)}, u32[]{:S(2)}, u32[]{:S(2)}) collective-permute-start(bf16[16,8,1280]{2,1,0:T(8,128)(2,1)S(1)} %get-tuple-element.48), channel_id=1, source_target_pairs={{0,6},{2,0},{4,2},{6,4},{1,7},{3,1},{5,3},{7,5},{8,14},{10,8},{12,... | collective-permute-start | bytes 983048 | tf_op jit(solution)/shard_map/ppermute | solution.py:32
  94.2 6.5 %collective-permute-done.18.left_ref = bf16[16,8,1280]{2,1,0:T(8,128)(2,1)S(1)} collective-permute-done((bf16[16,8,1280]{2,1,0:T(8,128)(2,1)S(1)}, bf16[16,8,1280]{2,1,0:T(8,128)(2,1)S(1)}, u32[]{:S(2)}, u32[]{:S(2)}) %collective-permute-start.18) | collective-permute-done | bytes 327712 | tf_op jit(solution)/shard_map/ppermute | solution.py:32
  100.7 6.4 %collective-permute-done.19.right_ref = bf16[16,8,1280]{2,1,0:T(8,128)(2,1)S(1)} collective-permute-done((bf16[16,8,1280]{2,1,0:T(8,128)(2,1)S(1)}, bf16[16,8,1280]{2,1,0:T(8,128)(2,1)S(1)}, u32[]{:S(2)}, u32[]{:S(2)}) %collective-permute-start.19) | collective-permute-done | bytes 327712 | tf_op jit(solution)/shard_map/ppermute | solution.py:32
  107.1 1.8 collective-permute-done.20.far_ref
  108.9 2.0 %pack.1 = bf16[64,8,1280]{2,1,0:T(8,128)(2,1)} custom-call(s32[16]{0:T(128)S(1)} %bitcast.36, bf16[16,8,1280]{2,1,0:T(8,128)(2,1)S(1)} %get-tuple-element.50.own_ref, bf16[16,8,1280]{2,1,0:T(8,128)(2,1)S(1)} %collective-permute-done.18.left_ref, bf16[16,8,1280]{2,1,0:T(8,128)(2,1)S(1)} %collective-permute-done.19.right_ref, ...), custom_call_target="tpu_custom_call" | custom-call | tf_op jit(solution)/shard_map/pack/pallas_call | solution.py:365
  110.9 6.7 %all-to-all-start.1 = ((bf16[64,8,1280]{2,1,0:T(8,128)(2,1)}), bf16[64,8,1280]{2,1,0:T(8,128)(2,1)S(1)}, u32[]{:S(2)}, u32[]{:S(2)}) async-start(bf16[64,8,1280]{2,1,0:T(8,128)(2,1)} %pack.1), calls=%async_computation.1 | async-start | bytes 2621440 | tf_op jit(solution)/shard_map/all_to_all | solution.py:373
  117.6 4.2 %shard_map.119 = (bf16[4,40,1024]{2,1,0:T(8,128)(2,1)S(1)}, bf16[4,40,1024]{2,1,0:T(8,128)(2,1)S(1)}, bf16[4,40,1024]{2,1,0:T(8,128)(2,1)S(1)}, bf16[4,40,1024]{2,1,0:T(8,128)(2,1)S(1)}) custom-call(s32[1]{0:T(128)} %bitcast.4.y_ref, bf16[16384,1280]{1,0:T(8,128)(2,1)} %get-tuple-element.28.shelf_any), custom_call_target="tpu_custom_call" | custom-call | flops 1342177280 | bytes 6291456 | tf_op jit(solution)/shard_map/pallas_call | solution.py:321
  121.9 1.5 collective-permute-start.5
  123.4 4.2 %shard_map.120 = (bf16[4,40,1024]{2,1,0:T(8,128)(2,1)S(1)}, bf16[4,40,1024]{2,1,0:T(8,128)(2,1)S(1)}, bf16[4,40,1024]{2,1,0:T(8,128)(2,1)S(1)}, bf16[8,40,1024]{2,1,0:T(8,128)(2,1)S(1)}) custom-call(s32[1]{0:T(128)} %bitcast.4.y_ref, bf16[16384,1280]{1,0:T(8,128)(2,1)} %get-tuple-element.28.shelf_any, bf16[4,40,1024]{2,1,0:T(8,128)(2,1)S(1)} %get-tuple-element.32.refs_0_), custom_call_target="tpu_custom_call" | custom-call | flops 1342177280 | bytes 6291456 | tf_op jit(solution)/shard_map/pallas_call | solution.py:321
  129.8 2.2 %collective-permute-start.9 = (bf16[4,40,1024]{2,1,0:T(8,128)(2,1)S(1)}, bf16[4,40,1024]{2,1,0:T(8,128)(2,1)}, u32[]{:S(2)}, u32[]{:S(2)}) collective-permute-start(bf16[4,40,1024]{2,1,0:T(8,128)(2,1)S(1)} %get-tuple-element.36), channel_id=1, source_target_pairs={{0,16},{8,24},{16,0},{24,8},{1,17},{9,25},{17,1},{25,9},{2,18},{10... | collective-permute-start | bytes 983048 | tf_op jit(solution)/shard_map/ppermute | solution.py:32
  132.0 6.2 %collective-permute-done.5 = bf16[4,40,1024]{2,1,0:T(8,128)(2,1)S(1)} collective-permute-done((bf16[4,40,1024]{2,1,0:T(8,128)(2,1)S(1)}, bf16[4,40,1024]{2,1,0:T(8,128)(2,1)S(1)}, u32[]{:S(2)}, u32[]{:S(2)}) %collective-permute-start.5) | collective-permute-done | bytes 327712 | tf_op jit(solution)/shard_map/ppermute | solution.py:32
  140.1 14.1 %collective-permute-done.8 = bf16[4,40,1024]{2,1,0:T(8,128)(2,1)} collective-permute-done((bf16[4,40,1024]{2,1,0:T(8,128)(2,1)S(1)}, bf16[4,40,1024]{2,1,0:T(8,128)(2,1)}, u32[]{:S(2)}, u32[]{:S(2)}) %collective-permute-start.8) | collective-permute-done | bytes 327712 | tf_op jit(solution)/shard_map/ppermute | solution.py:32
  154.2 4.5 %collective-permute-done.9 = bf16[4,40,1024]{2,1,0:T(8,128)(2,1)} collective-permute-done((bf16[4,40,1024]{2,1,0:T(8,128)(2,1)S(1)}, bf16[4,40,1024]{2,1,0:T(8,128)(2,1)}, u32[]{:S(2)}, u32[]{:S(2)}) %collective-permute-start.9) | collective-permute-done | bytes 327712 | tf_op jit(solution)/shard_map/ppermute | solution.py:32
  158.7 3.2 %collective-permute-done.6 = bf16[4,40,1024]{2,1,0:T(8,128)(2,1)} collective-permute-done((bf16[4,40,1024]{2,1,0:T(8,128)(2,1)}, bf16[4,40,1024]{2,1,0:T(8,128)(2,1)}, u32[]{:S(2)}, u32[]{:S(2)}) %collective-permute-start.6) | collective-permute-done | bytes 327712 | tf_op jit(solution)/shard_map/ppermute | solution.py:32
  161.8 1.8 add_convert_fusion.5
  165.0 4.4 %collective-permute-start.10 = (bf16[40,1024]{1,0:T(8,128)(2,1)S(1)}, bf16[40,1024]{1,0:T(8,128)(2,1)S(1)}, u32[]{:S(2)}, u32[]{:S(2)}) collective-permute-start(bf16[40,1024]{1,0:T(8,128)(2,1)S(1)} %get-tuple-element.52), channel_id=1, source_target_pairs={{0,128},{32,160},{64,192},{96,224},{128,0},{160,32},{192,64},{224,... | collective-permute-start | bytes 245768 | tf_op jit(solution)/shard_map/ppermute | solution.py:32
  170.5 3.9 %collective-permute-start.12 = (bf16[40,1024]{1,0:T(8,128)(2,1)S(1)}, bf16[40,1024]{1,0:T(8,128)(2,1)S(1)}, u32[]{:S(2)}, u32[]{:S(2)}) collective-permute-start(bf16[40,1024]{1,0:T(8,128)(2,1)S(1)} %get-tuple-element.54), channel_id=1, source_target_pairs={{0,160},{32,192},{64,224},{96,0},{128,32},{160,64},{192,96},{224,1... | collective-permute-start | bytes 245768 | tf_op jit(solution)/shard_map/ppermute | solution.py:32
  175.0 3.6 %collective-permute-start.14 = (bf16[40,1024]{1,0:T(8,128)(2,1)S(1)}, bf16[40,1024]{1,0:T(8,128)(2,1)S(1)}, u32[]{:S(2)}, u32[]{:S(2)}) collective-permute-start(bf16[40,1024]{1,0:T(8,128)(2,1)S(1)} %get-tuple-element.56), channel_id=1, source_target_pairs={{0,192},{32,224},{64,0},{96,32},{128,64},{160,96},{192,128},{224,1... | collective-permute-start | bytes 245768 | tf_op jit(solution)/shard_map/ppermute | solution.py:32
  179.2 1.9 %collect.1 = f32[12,8,1280]{2,1,0:T(8,128)} custom-call(s32[64]{0:T(128)S(1)} %reshape_squeeze.3.sent_ref, bf16[64,8,1280]{2,1,0:T(8,128)(2,1)S(1)} %all-to-all-done.1.got_ref), custom_call_target="tpu_custom_call" | custom-call | tf_op jit(solution)/shard_map/collect/pallas_call | solution.py:382
  182.1 2.0 %collective-permute-done.14 = bf16[40,1024]{1,0:T(8,128)(2,1)S(1)} collective-permute-done((bf16[40,1024]{1,0:T(8,128)(2,1)S(1)}, bf16[40,1024]{1,0:T(8,128)(2,1)S(1)}, u32[]{:S(2)}, u32[]{:S(2)}) %collective-permute-start.14) | collective-permute-done | bytes 81952 | tf_op jit(solution)/shard_map/ppermute | solution.py:32
  (54 shorter events, 14.9 us)
Async XLA Ops:
  1.5 1.5 copy-start
  4.9 11.7 %copy-start.2 = (s32[1,16]{1,0:T(1,128)S(1)}, s32[1,16]{1,0:T(1,128)}, u32[]{:S(2)}) copy-start(s32[1,16]{1,0:T(1,128)} %param.12) | copy-start | bytes 196
  4.9 44.6 %all-to-all-start = ((bf16[64,8,1280]{2,1,0:T(8,128)(2,1)}), bf16[64,8,1280]{2,1,0:T(8,128)(2,1)S(1)}, u32[]{:S(2)}, u32[]{:S(2)}) async-start(bf16[64,8,1280]{2,1,0:T(8,128)(2,1)} %spread.1), calls=%async_computation | async-start | bytes 2621440 | tf_op jit(solution)/shard_map/all_to_all | solution.py:260
  49.6 19.7 %copy-start.6 = (bf16[512,512]{1,0:T(8,128)(2,1)S(1)}, bf16[512,512]{1,0:T(8,128)(2,1)}, u32[]{:S(2)}) copy-start(bf16[512,512]{1,0:T(8,128)(2,1)} %g_any.1) | copy-start | bytes 1572868
  50.2 9.3 %collective-permute-start = (bf16[16,8,1280]{2,1,0:T(8,128)(2,1)S(1)}, bf16[16,8,1280]{2,1,0:T(8,128)(2,1)S(1)}, u32[]{:S(2)}, u32[]{:S(2)}) collective-permute-start(bf16[16,8,1280]{2,1,0:T(8,128)(2,1)S(1)} %gather_fusion), channel_id=1, source_target_pairs={{0,2},{2,4},{4,6},{6,0},{1,3},{3,5},{5,7},{7,1},{8,10},{10,12},{12... | collective-permute-start | bytes 983048 | tf_op jit(solution)/shard_map/ppermute | solution.py:32
  51.7 8.1 %collective-permute-start.1 = (bf16[16,8,1280]{2,1,0:T(8,128)(2,1)S(1)}, bf16[16,8,1280]{2,1,0:T(8,128)(2,1)S(1)}, u32[]{:S(2)}, u32[]{:S(2)}) collective-permute-start(bf16[16,8,1280]{2,1,0:T(8,128)(2,1)S(1)} %gather_fusion), channel_id=1, source_target_pairs={{0,6},{2,0},{4,2},{6,4},{1,7},{3,1},{5,3},{7,5},{8,14},{10,8},{12,... | collective-permute-start | bytes 983048 | tf_op jit(solution)/shard_map/ppermute | solution.py:32
  53.5 15.8 %copy-start.5 = (bf16[512,512]{1,0:T(8,128)(2,1)S(1)}, bf16[512,512]{1,0:T(8,128)(2,1)}, u32[]{:S(2)}) copy-start(bf16[512,512]{1,0:T(8,128)(2,1)} %q_any.1) | copy-start | bytes 1572868
  53.5 12.7 %copy-start.1 = (s32[512]{0:T(512)S(1)}, s32[512]{0:T(512)}, u32[]{:S(2)}) copy-start(s32[512]{0:T(512)} %param.14) | copy-start | bytes 6148
  53.5 15.8 %copy-start.3 = (bf16[1280,512]{1,0:T(8,128)(2,1)S(1)}, bf16[1280,512]{1,0:T(8,128)(2,1)}, u32[]{:S(2)}) copy-start(bf16[1280,512]{1,0:T(8,128)(2,1)} %wk_any.1) | copy-start | bytes 3932164
  53.5 15.7 %copy-start.4 = (bf16[1280,512]{1,0:T(8,128)(2,1)S(1)}, bf16[1280,512]{1,0:T(8,128)(2,1)}, u32[]{:S(2)}) copy-start(bf16[1280,512]{1,0:T(8,128)(2,1)} %wv_any.1) | copy-start | bytes 3932164
  59.5 6.6 %collective-permute-start.2 = (bf16[8,8,1280]{2,1,0:T(8,128)(2,1)S(1)}, bf16[8,8,1280]{2,1,0:T(8,128)(2,1)S(1)}, u32[]{:S(2)}, u32[]{:S(2)}) collective-permute-start(bf16[8,8,1280]{2,1,0:T(8,128)(2,1)S(1)} %slice.63), channel_id=1, source_target_pairs={{0,2},{2,4},{4,6},{6,0},{1,3},{3,5},{5,7},{7,1},{8,10},{10,12},{12... | collective-permute-start | bytes 491528 | tf_op jit(solution)/shard_map/ppermute | solution.py:32
  59.9 6.2 %collective-permute-start.3 = (bf16[8,8,1280]{2,1,0:T(8,128)(2,1)S(1)}, bf16[8,8,1280]{2,1,0:T(8,128)(2,1)S(1)}, u32[]{:S(2)}, u32[]{:S(2)}) collective-permute-start(bf16[8,8,1280]{2,1,0:T(8,128)(2,1)S(1)} %slice.64), channel_id=1, source_target_pairs={{0,6},{2,0},{4,2},{6,4},{1,7},{3,1},{5,3},{7,5},{8,14},{10,8},{12,... | collective-permute-start | bytes 491528 | tf_op jit(solution)/shard_map/ppermute | solution.py:32
  66.1 3.1 %collective-permute-start.4 = (bf16[4,16,8,1280]{3,2,1,0:T(8,128)(2,1)S(1)}, bf16[4,16,8,1280]{3,2,1,0:T(8,128)(2,1)S(1)}, u32[]{:S(2)}, u32[]{:S(2)}) collective-permute-start(bf16[4,16,8,1280]{3,2,1,0:T(8,128)(2,1)S(1)} %bitcast.32), channel_id=1, source_target_pairs={{0,1},{1,0},{2,3},{3,2},{4,5},{5,4},{6,7},{7,6},{8,9},{9,8},{10,11... | collective-permute-start | bytes 3932168 | tf_op jit(solution)/shard_map/ppermute | solution.py:32
  85.9 3.1 %collective-permute-start.17 = (bf16[4,16,8,1280]{3,2,1,0:T(8,128)(2,1)S(1)}, bf16[4,16,8,1280]{3,2,1,0:T(8,128)(2,1)S(1)}, u32[]{:S(2)}, u32[]{:S(2)}) collective-permute-start(bf16[4,16,8,1280]{3,2,1,0:T(8,128)(2,1)S(1)} %get-tuple-element.38), channel_id=1, source_target_pairs={{0,1},{1,0},{2,3},{3,2},{4,5},{5,4},{6,7},{7,6},{8,9},{9,8},{10,11... | collective-permute-start | bytes 3932168 | tf_op jit(solution)/shard_map/ppermute | solution.py:32
  89.3 11.4 %collective-permute-start.18 = (bf16[16,8,1280]{2,1,0:T(8,128)(2,1)S(1)}, bf16[16,8,1280]{2,1,0:T(8,128)(2,1)S(1)}, u32[]{:S(2)}, u32[]{:S(2)}) collective-permute-start(bf16[16,8,1280]{2,1,0:T(8,128)(2,1)S(1)} %get-tuple-element.49), channel_id=1, source_target_pairs={{0,2},{2,4},{4,6},{6,0},{1,3},{3,5},{5,7},{7,1},{8,10},{10,12},{12... | collective-permute-start | bytes 983048 | tf_op jit(solution)/shard_map/ppermute | solution.py:32
  90.0 17.1 %collective-permute-start.19 = (bf16[16,8,1280]{2,1,0:T(8,128)(2,1)S(1)}, bf16[16,8,1280]{2,1,0:T(8,128)(2,1)S(1)}, u32[]{:S(2)}, u32[]{:S(2)}) collective-permute-start(bf16[16,8,1280]{2,1,0:T(8,128)(2,1)S(1)} %get-tuple-element.48), channel_id=1, source_target_pairs={{0,6},{2,0},{4,2},{6,4},{1,7},{3,1},{5,3},{7,5},{8,14},{10,8},{12,... | collective-permute-start | bytes 983048 | tf_op jit(solution)/shard_map/ppermute | solution.py:32
  92.8 16.1 %collective-permute-start.20 = (bf16[16,8,1280]{2,1,0:T(8,128)(2,1)S(1)}, bf16[16,8,1280]{2,1,0:T(8,128)(2,1)S(1)}, u32[]{:S(2)}, u32[]{:S(2)}) collective-permute-start(bf16[16,8,1280]{2,1,0:T(8,128)(2,1)S(1)} %get-tuple-element.47), channel_id=1, source_target_pairs={{0,4},{2,6},{4,0},{6,2},{1,5},{3,7},{5,1},{7,3},{8,12},{10,14},{12... | collective-permute-start | bytes 983048 | tf_op jit(solution)/shard_map/ppermute | solution.py:32
  110.9 68.3 %all-to-all-start.1 = ((bf16[64,8,1280]{2,1,0:T(8,128)(2,1)}), bf16[64,8,1280]{2,1,0:T(8,128)(2,1)S(1)}, u32[]{:S(2)}, u32[]{:S(2)}) async-start(bf16[64,8,1280]{2,1,0:T(8,128)(2,1)} %pack.1), calls=%async_computation.1 | async-start | bytes 2621440 | tf_op jit(solution)/shard_map/all_to_all | solution.py:373
  121.9 16.3 %collective-permute-start.5 = (bf16[4,40,1024]{2,1,0:T(8,128)(2,1)S(1)}, bf16[4,40,1024]{2,1,0:T(8,128)(2,1)S(1)}, u32[]{:S(2)}, u32[]{:S(2)}) collective-permute-start(bf16[4,40,1024]{2,1,0:T(8,128)(2,1)S(1)} %get-tuple-element.31), channel_id=1, source_target_pairs={{0,8},{8,16},{16,24},{24,0},{1,9},{9,17},{17,25},{25,1},{2,10},{10... | collective-permute-start | bytes 983048 | tf_op jit(solution)/shard_map/ppermute | solution.py:32
  127.6 31.0 %collective-permute-start.7 = (bf16[8,40,1024]{2,1,0:T(8,128)(2,1)S(1)}, bf16[8,40,1024]{2,1,0:T(8,128)(2,1)}, u32[]{:S(2)}, u32[]{:S(2)}) collective-permute-start(bf16[8,40,1024]{2,1,0:T(8,128)(2,1)S(1)} %get-tuple-element.33), channel_id=1, source_target_pairs={{0,24},{8,0},{16,8},{24,16},{1,25},{9,1},{17,9},{25,17},{2,26},{10... | collective-permute-start | bytes 1966088 | tf_op jit(solution)/shard_map/ppermute | solution.py:32
  128.3 25.9 %collective-permute-start.8 = (bf16[4,40,1024]{2,1,0:T(8,128)(2,1)S(1)}, bf16[4,40,1024]{2,1,0:T(8,128)(2,1)}, u32[]{:S(2)}, u32[]{:S(2)}) collective-permute-start(bf16[4,40,1024]{2,1,0:T(8,128)(2,1)S(1)} %get-tuple-element.35), channel_id=1, source_target_pairs={{0,8},{8,16},{16,24},{24,0},{1,9},{9,17},{17,25},{25,1},{2,10},{10... | collective-permute-start | bytes 983048 | tf_op jit(solution)/shard_map/ppermute | solution.py:32
  129.8 28.9 %collective-permute-start.9 = (bf16[4,40,1024]{2,1,0:T(8,128)(2,1)S(1)}, bf16[4,40,1024]{2,1,0:T(8,128)(2,1)}, u32[]{:S(2)}, u32[]{:S(2)}) collective-permute-start(bf16[4,40,1024]{2,1,0:T(8,128)(2,1)S(1)} %get-tuple-element.36), channel_id=1, source_target_pairs={{0,16},{8,24},{16,0},{24,8},{1,17},{9,25},{17,1},{25,9},{2,18},{10... | collective-permute-start | bytes 983048 | tf_op jit(solution)/shard_map/ppermute | solution.py:32
  139.0 22.9 %collective-permute-start.6 = (bf16[4,40,1024]{2,1,0:T(8,128)(2,1)}, bf16[4,40,1024]{2,1,0:T(8,128)(2,1)}, u32[]{:S(2)}, u32[]{:S(2)}) collective-permute-start(bf16[4,40,1024]{2,1,0:T(8,128)(2,1)} %add_convert_fusion.6), channel_id=1, source_target_pairs={{0,8},{8,16},{16,24},{24,0},{1,9},{9,17},{17,25},{25,1},{2,10},{10... | collective-permute-start | bytes 983048 | tf_op jit(solution)/shard_map/ppermute | solution.py:32
  163.7 11.4 %collective-permute-start.15 = (bf16[40,1024]{1,0:T(8,128)(2,1)S(1)}, bf16[40,1024]{1,0:T(8,128)(2,1)S(1)}, u32[]{:S(2)}, u32[]{:S(2)}) collective-permute-start(bf16[40,1024]{1,0:T(8,128)(2,1)S(1)} %fusion.19), channel_id=1, source_target_pairs={{0,32},{32,64},{64,96},{96,128},{128,160},{160,192},{192,224},{224... | collective-permute-start | bytes 245768 | tf_op jit(solution)/shard_map/ppermute | solution.py:32
  165.0 13.6 %collective-permute-start.10 = (bf16[40,1024]{1,0:T(8,128)(2,1)S(1)}, bf16[40,1024]{1,0:T(8,128)(2,1)S(1)}, u32[]{:S(2)}, u32[]{:S(2)}) collective-permute-start(bf16[40,1024]{1,0:T(8,128)(2,1)S(1)} %get-tuple-element.52), channel_id=1, source_target_pairs={{0,128},{32,160},{64,192},{96,224},{128,0},{160,32},{192,64},{224,... | collective-permute-start | bytes 245768 | tf_op jit(solution)/shard_map/ppermute | solution.py:32
  169.4 12.7 %collective-permute-start.11 = (bf16[40,1024]{1,0:T(8,128)(2,1)S(1)}, bf16[40,1024]{1,0:T(8,128)(2,1)S(1)}, u32[]{:S(2)}, u32[]{:S(2)}) collective-permute-start(bf16[40,1024]{1,0:T(8,128)(2,1)S(1)} %get-tuple-element.53), channel_id=1, source_target_pairs={{0,96},{32,128},{64,160},{96,192},{128,224},{160,0},{192,32},{224,... | collective-permute-start | bytes 245768 | tf_op jit(solution)/shard_map/ppermute | solution.py:32
  170.5 11.6 %collective-permute-start.12 = (bf16[40,1024]{1,0:T(8,128)(2,1)S(1)}, bf16[40,1024]{1,0:T(8,128)(2,1)S(1)}, u32[]{:S(2)}, u32[]{:S(2)}) collective-permute-start(bf16[40,1024]{1,0:T(8,128)(2,1)S(1)} %get-tuple-element.54), channel_id=1, source_target_pairs={{0,160},{32,192},{64,224},{96,0},{128,32},{160,64},{192,96},{224,1... | collective-permute-start | bytes 245768 | tf_op jit(solution)/shard_map/ppermute | solution.py:32
  174.4 7.7 %collective-permute-start.13 = (bf16[40,1024]{1,0:T(8,128)(2,1)S(1)}, bf16[40,1024]{1,0:T(8,128)(2,1)S(1)}, u32[]{:S(2)}, u32[]{:S(2)}) collective-permute-start(bf16[40,1024]{1,0:T(8,128)(2,1)S(1)} %get-tuple-element.55), channel_id=1, source_target_pairs={{0,64},{32,96},{64,128},{96,160},{128,192},{160,224},{192,0},{224,... | collective-permute-start | bytes 245768 | tf_op jit(solution)/shard_map/ppermute | solution.py:32
  175.0 9.1 %collective-permute-start.14 = (bf16[40,1024]{1,0:T(8,128)(2,1)S(1)}, bf16[40,1024]{1,0:T(8,128)(2,1)S(1)}, u32[]{:S(2)}, u32[]{:S(2)}) collective-permute-start(bf16[40,1024]{1,0:T(8,128)(2,1)S(1)} %get-tuple-element.56), channel_id=1, source_target_pairs={{0,192},{32,224},{64,0},{96,32},{128,64},{160,96},{192,128},{224,1... | collective-permute-start | bytes 245768 | tf_op jit(solution)/shard_map/ppermute | solution.py:32
  178.6 6.0 %collective-permute-start.16 = (bf16[40,1024]{1,0:T(8,128)(2,1)S(1)}, bf16[40,1024]{1,0:T(8,128)(2,1)S(1)}, u32[]{:S(2)}, u32[]{:S(2)}) collective-permute-start(bf16[40,1024]{1,0:T(8,128)(2,1)S(1)} %get-tuple-element.51), channel_id=1, source_target_pairs={{0,224},{32,0},{64,32},{96,64},{128,96},{160,128},{192,160},{224,1... | collective-permute-start | bytes 245768 | tf_op jit(solution)/shard_map/ppermute | solution.py:32
